TPU v7x, 32 devices: a whole 2x2x4 slice. The times are simulated.
32 devices in a mesh: fsdp: 2 (over x), heads: 4 (over y, core), tensor: 4 (over z).
Axes of the slice: x: 2, y: 2, z: 4, core: 2. Of those that a mesh axis runs over, the one named last changes fastest.
Arguments:
- tokens: bfloat16 [8, 1024, 2048], P('fsdp', 'heads'), may hold values from -6 to 6
- segments: int32 [8, 1024], P('fsdp'), may hold values from 0 to 3, never falling along the last dimension, each value on 1 to 768 neighbouring positions
- q_weight: bfloat16 [2048, 2048], P(('fsdp', 'heads'), 'tensor'), may hold values from -0.125 to 0.125
- k_weight: bfloat16 [2048, 512], P(('fsdp', 'heads'), 'tensor'), may hold values from -0.125 to 0.125
- v_weight: bfloat16 [2048, 512], P(('fsdp', 'heads'), 'tensor'), may hold values from -0.125 to 0.125
- o_weight: bfloat16 [2048, 2048], P(('fsdp', 'heads'), 'tensor'), may hold values from -0.75 to 0.75
- attn_gain: bfloat16 [2048], P(('fsdp', 'heads')), may hold values from 0.25 to 1.75
- gate_weight: bfloat16 [2048, 8192], P(('fsdp', 'heads'), 'tensor'), may hold values from -0.125 to 0.125
- up_weight: bfloat16 [2048, 8192], P(('fsdp', 'heads'), 'tensor'), may hold values from -0.125 to 0.125
- down_weight: bfloat16 [2048, 8192], P(('fsdp', 'heads'), 'tensor'), may hold values from -0.0625 to 0.0625
- ffn_gain: bfloat16 [2048], P(('fsdp', 'heads')), may hold values from 0.25 to 1.75
- cotangent: bfloat16 [8, 1024, 2048], P('fsdp', 'heads'), may hold values from -6 to 6
Outputs:
- output: bfloat16 [8, 1024, 2048], P('fsdp', 'heads')
- input_grad: float32 [8, 1024, 2048], P('fsdp', 'heads')
- q_weight_grad: float32 [2048, 2048], P(('fsdp', 'heads'), 'tensor')
- k_weight_grad: float32 [2048, 512], P(('fsdp', 'heads'), 'tensor')
- v_weight_grad: float32 [2048, 512], P(('fsdp', 'heads'), 'tensor')
- o_weight_grad: float32 [2048, 2048], P(('fsdp', 'heads'), 'tensor')
- attn_gain_grad: float32 [2048], P(('fsdp', 'heads'))
- gate_grad: float32 [2048, 8192], P(('fsdp', 'heads'), 'tensor')
- up_grad: float32 [2048, 8192], P(('fsdp', 'heads'), 'tensor')
- down_grad: float32 [2048, 8192], P(('fsdp', 'heads'), 'tensor')
- ffn_gain_grad: float32 [2048], P(('fsdp', 'heads'))
Inputs may be any that keep to these rules, and one draw needn't show every extreme that they name: `segments`: in each sequence the document numbers start at 0, never fall, and take every value up to the largest; a document holds 1 to 768 tokens.
All inputs are finite; a program needn't handle non-finite values.
Results may differ from a plain program's by a relative error of at most 0.02.
Values may be sent and summed in bfloat16 or wider, within the bound.
No kernel may reach another device: no remote copies, remote signals or barrier semaphores. Data moves between devices by JAX's collectives and lax.ppermute only.
A program may use at most 256 MiB of HBM per device.

v0:
```python
import math

import jax
import jax.numpy as jnp
import numpy as np
from jax import lax
from jax.sharding import PartitionSpec as P

HD = 64


EPSILON = 1e-05
ROPE_BASE = 500000.0
NEG_FILL = -1e30


def shortened(x):

    def short(part):
        return part.astype(jnp.bfloat16) if part.dtype == jnp.float32 else part

    return jax.tree.map(short, x)


def positions(segments):
    length_of = segments.shape[-1]
    column = jnp.arange(length_of, dtype=jnp.int32)
    before = jnp.concatenate([segments[..., :1] - 1, segments[..., :-1]], axis=-1)
    firsts = jnp.where(segments != before, column, jnp.zeros_like(column))
    starts = lax.cummax(firsts, axis=firsts.ndim - 1)
    return column - starts


def rotate(values_in, where_at, direction):
    half_dim = values_in.shape[-1] // 2
    frequency = ROPE_BASE ** (-2.0 * jnp.arange(half_dim, dtype=jnp.float32) / values_in.shape[-1])
    angles = where_at.astype(jnp.float32)[..., None, None] * frequency
    cosine = jnp.cos(angles)
    sine_part = direction * jnp.sin(angles)
    first_half = values_in[..., :half_dim]
    second_half = values_in[..., half_dim:]
    return jnp.concatenate(
        [
            first_half * cosine - second_half * sine_part,
            second_half * cosine + first_half * sine_part,
        ],
        axis=-1,
    )


def normed(values_in, gain_in):
    return (
        values_in
        * lax.rsqrt(jnp.mean(values_in * values_in, axis=-1, keepdims=True) + EPSILON)
        * gain_in
    )


def dot_plain(left_in, right_in):
    return jnp.dot(left_in, right_in, preferred_element_type=jnp.float32)


def dot_rows(left_in, right_in):
    return lax.dot_general(
        left_in, right_in, (((0,), (0,)), ((), ())), preferred_element_type=jnp.float32
    )


def dot_cols(left_in, right_in):
    return lax.dot_general(
        left_in, right_in, (((1,), (1,)), ((), ())), preferred_element_type=jnp.float32
    )


def per_device(
    tokens,
    segments,
    q_weight,
    k_weight,
    v_weight,
    o_weight,
    attn_gain,
    gate_weight,
    up_weight,
    down_weight,
    ffn_gain,
    cotangent,
):
    seq_count, block_len, width_d = tokens.shape
    seq_len = segments.shape[1]
    part_count = lax.axis_size("heads")
    row_count = seq_count * block_len
    local_heads = q_weight.shape[1] // HD
    local_kv = k_weight.shape[1] // HD
    group_size = local_heads // part_count
    slot_map = np.arange(part_count) * group_size // (local_heads // local_kv)
    span_rows = min(512, seq_len)
    block_count = seq_len // span_rows
    scale_by = 1.0 / math.sqrt(HD)
    column = jnp.arange(seq_len, dtype=jnp.int32)
    where_all = positions(segments)
    where_here = lax.dynamic_slice_in_dim(
        where_all, lax.axis_index("heads") * block_len, block_len, 1
    )
    full_q, full_k, full_v, full_o, gain_one, full_g, full_u, full_d, gain_two = (
        lax.all_gather(q_weight, ("fsdp", "heads"), axis=0, tiled=True),
        lax.all_gather(k_weight, ("fsdp", "heads"), axis=0, tiled=True),
        lax.all_gather(v_weight, ("fsdp", "heads"), axis=0, tiled=True),
        lax.all_gather(o_weight, ("fsdp", "heads"), axis=0, tiled=True),
        lax.all_gather(attn_gain, ("fsdp", "heads"), axis=0, tiled=True),
        lax.all_gather(gate_weight, ("fsdp", "heads"), axis=0, tiled=True),
        lax.all_gather(up_weight, ("fsdp", "heads"), axis=0, tiled=True),
        lax.all_gather(down_weight, ("fsdp", "heads"), axis=0, tiled=True),
        lax.all_gather(ffn_gain, ("fsdp", "heads"), axis=0, tiled=True),
    )
    gain_one_f = gain_one.astype(jnp.float32)
    gain_two_f = gain_two.astype(jnp.float32)
    tokens_f = tokens.reshape(row_count, width_d).astype(jnp.float32)
    normed_one = normed(tokens_f, gain_one_f).astype(jnp.bfloat16)
    query_pre = dot_plain(normed_one, full_q)
    key_pre = dot_plain(normed_one, full_k)
    value_pre = dot_plain(normed_one, full_v)
    queries = rotate(
        query_pre.reshape(seq_count, block_len, local_heads, HD), where_here, 1.0
    ).astype(jnp.bfloat16)
    key_rot = rotate(key_pre.reshape(seq_count, block_len, local_kv, HD), where_here, 1.0).astype(
        jnp.bfloat16
    )
    values = value_pre.astype(jnp.bfloat16).reshape(seq_count, block_len, local_kv, HD)
    kv_pairs = jnp.concatenate([key_rot, values], axis=3)[:, :, slot_map]
    head_q, head_kv = (
        lax.all_to_all(
            queries.reshape(seq_count, block_len, part_count, group_size * HD),
            "heads",
            split_axis=2,
            concat_axis=1,
            tiled=True,
        ),
        lax.all_to_all(kv_pairs, "heads", split_axis=2, concat_axis=1, tiled=True),
    )
    head_q = head_q.reshape(seq_count, seq_len, group_size, HD)
    head_k = head_kv[:, :, 0, :HD]
    head_v = head_kv[:, :, 0, HD:]

    def scores_of(number):
        begin_at = number * span_rows
        q_block = lax.dynamic_slice_in_dim(head_q, begin_at, span_rows, 1)
        seg_block = lax.dynamic_slice_in_dim(segments, begin_at, span_rows, 1)
        row_pos = begin_at + jnp.arange(span_rows, dtype=jnp.int32)
        scores = (
            jnp.einsum("sqhd,skd->shqk", q_block, head_k, preferred_element_type=jnp.float32)
            * scale_by
        )
        allowed = (seg_block[:, :, None] == segments[:, None, :]) & (
            row_pos[:, None] >= column[None, :]
        )[None]
        return (q_block, jnp.where(allowed[:, None], scores, NEG_FILL))

    def forward_block(number):
        q_block, scores = scores_of(number)
        peak_val = jnp.max(scores, axis=-1, keepdims=True)
        weights = jnp.exp(scores - peak_val)
        denom_sum = jnp.sum(weights, axis=-1, keepdims=True)
        probs_low = (weights / denom_sum).astype(jnp.bfloat16)
        mixed_out = jnp.einsum(
            "shqk,skd->sqhd", probs_low, head_v, preferred_element_type=jnp.float32
        )
        return (mixed_out.astype(jnp.bfloat16), (peak_val + jnp.log(denom_sum))[..., 0])

    mixed_all, log_sums = lax.map(forward_block, jnp.arange(block_count, dtype=jnp.int32))
    head_out = jnp.moveaxis(mixed_all, 0, 1).reshape(seq_count, seq_len, 1, group_size * HD)
    attended = (
        lax.all_to_all(shortened(head_out), "heads", split_axis=1, concat_axis=2, tiled=True)
        .astype(head_out.dtype)
        .reshape(row_count, local_heads * HD)
    )
    attn_part = dot_cols(attended, full_o)
    residual = tokens_f + lax.psum(attn_part, "tensor")
    normed_two = normed(residual, gain_two_f).astype(jnp.bfloat16)
    gate_pre = dot_plain(normed_two, full_g)
    up_pre = dot_plain(normed_two, full_u)
    hidden = (jax.nn.silu(gate_pre) * up_pre).astype(jnp.bfloat16)
    ffn_part = dot_cols(hidden, full_d)
    output = (
        (residual + lax.psum(ffn_part.astype(jnp.bfloat16), "tensor").astype(jnp.float32))
        .astype(jnp.bfloat16)
        .reshape(seq_count, block_len, width_d)
    )
    grad_out = cotangent.reshape(row_count, width_d)
    grad_out_f = grad_out.astype(jnp.float32)
    d_hidden = dot_plain(grad_out, full_d)
    down_grad = dot_rows(grad_out, hidden)
    sigmoid_g = jax.nn.sigmoid(gate_pre)
    d_gate = (d_hidden * up_pre * (sigmoid_g * (1.0 + gate_pre * (1.0 - sigmoid_g)))).astype(
        jnp.bfloat16
    )
    d_up = (d_hidden * gate_pre * sigmoid_g).astype(jnp.bfloat16)
    gate_grad = dot_rows(normed_two, d_gate)
    up_grad = dot_rows(normed_two, d_up)
    back_part = dot_cols(d_gate, full_g) + dot_cols(d_up, full_u)
    d_normed_two = lax.psum(back_part, "tensor")
    norm_value, norm_pull = jax.vjp(normed, residual, gain_two_f)
    d_resid_norm, gain_two_grad = norm_pull(d_normed_two)
    d_resid = grad_out_f + d_resid_norm
    ffn_grads = (
        lax.psum_scatter(
            gate_grad.astype(jnp.bfloat16), ("fsdp", "heads"), scatter_dimension=0, tiled=True
        ).astype(jnp.float32),
        lax.psum_scatter(
            up_grad.astype(jnp.bfloat16), ("fsdp", "heads"), scatter_dimension=0, tiled=True
        ).astype(jnp.float32),
        lax.psum_scatter(
            down_grad.astype(jnp.bfloat16), ("fsdp", "heads"), scatter_dimension=0, tiled=True
        ).astype(jnp.float32),
        lax.psum_scatter(
            gain_two_grad.astype(jnp.bfloat16), ("fsdp", "heads"), scatter_dimension=0, tiled=True
        ).astype(jnp.float32),
    )
    d_attn = d_resid.astype(jnp.bfloat16)
    o_weight_grad = dot_rows(d_attn, attended)
    d_attended = dot_plain(d_attn, full_o).astype(jnp.bfloat16)
    d_head = lax.all_to_all(
        d_attended.reshape(seq_count, block_len, part_count, group_size * HD),
        "heads",
        split_axis=2,
        concat_axis=1,
        tiled=True,
    )
    d_head = d_head.reshape(seq_count, seq_len, group_size, HD)

    def backward_block(sums_in, number):
        d_keys, d_values = sums_in
        q_block, scores = scores_of(number)
        probs_f = jnp.exp(scores - log_sums[number][..., None])
        d_block = lax.dynamic_slice_in_dim(d_head, number * span_rows, span_rows, 1)
        d_probs = jnp.einsum("sqhd,skd->shqk", d_block, head_v, preferred_element_type=jnp.float32)
        d_scores = (
            probs_f * (d_probs - jnp.sum(probs_f * d_probs, axis=-1, keepdims=True)) * scale_by
        ).astype(jnp.bfloat16)
        d_query = jnp.einsum(
            "shqk,skd->sqhd", d_scores, head_k, preferred_element_type=jnp.float32
        ).astype(jnp.bfloat16)
        d_keys = d_keys + jnp.einsum(
            "shqk,sqhd->skd", d_scores, q_block, preferred_element_type=jnp.float32
        )
        d_values = d_values + jnp.einsum(
            "shqk,sqhd->skd",
            probs_f.astype(jnp.bfloat16),
            d_block,
            preferred_element_type=jnp.float32,
        )
        return ((d_keys, d_values), d_query)

    zero_kv = jnp.zeros((seq_count, seq_len, HD), jnp.float32)
    (d_keys, d_values), d_query_all = lax.scan(
        backward_block, (zero_kv, zero_kv), jnp.arange(block_count, dtype=jnp.int32)
    )
    d_query_all = jnp.moveaxis(d_query_all, 0, 1).reshape(seq_count, seq_len, 1, group_size * HD)
    d_pairs = jnp.concatenate([d_keys, d_values], axis=2).astype(jnp.bfloat16)[:, :, None]
    back_q, back_kv = (
        lax.all_to_all(d_query_all, "heads", split_axis=1, concat_axis=2, tiled=True),
        lax.all_to_all(d_pairs, "heads", split_axis=1, concat_axis=2, tiled=True),
    )
    back_kv = jnp.sum(
        back_kv.astype(jnp.float32).reshape(
            seq_count, block_len, local_kv, part_count // local_kv, 2 * HD
        ),
        axis=3,
    )
    d_query_pre = (
        rotate(
            back_q.astype(jnp.float32).reshape(seq_count, block_len, local_heads, HD),
            where_here,
            -1.0,
        )
        .astype(jnp.bfloat16)
        .reshape(row_count, local_heads * HD)
    )
    d_key_pre = (
        rotate(back_kv[..., :HD], where_here, -1.0)
        .astype(jnp.bfloat16)
        .reshape(row_count, local_kv * HD)
    )
    d_value_pre = back_kv[..., HD:].astype(jnp.bfloat16).reshape(row_count, local_kv * HD)
    q_weight_grad = dot_rows(normed_one, d_query_pre)
    k_weight_grad = dot_rows(normed_one, d_key_pre)
    v_weight_grad = dot_rows(normed_one, d_value_pre)
    d_normed_one = lax.psum(
        (
            dot_cols(d_query_pre, full_q)
            + dot_cols(d_key_pre, full_k)
            + dot_cols(d_value_pre, full_v)
        ).astype(jnp.bfloat16),
        "tensor",
    ).astype(jnp.float32)
    norm_other, norm_back = jax.vjp(normed, tokens_f, gain_one_f)
    d_tokens_norm, gain_one_grad = norm_back(d_normed_one)
    input_grad = (d_resid + d_tokens_norm).reshape(seq_count, block_len, width_d)
    attn_grads = (
        lax.psum_scatter(
            q_weight_grad.astype(jnp.bfloat16), ("fsdp", "heads"), scatter_dimension=0, tiled=True
        ).astype(jnp.float32),
        lax.psum_scatter(
            k_weight_grad.astype(jnp.bfloat16), ("fsdp", "heads"), scatter_dimension=0, tiled=True
        ).astype(jnp.float32),
        lax.psum_scatter(
            v_weight_grad.astype(jnp.bfloat16), ("fsdp", "heads"), scatter_dimension=0, tiled=True
        ).astype(jnp.float32),
        lax.psum_scatter(
            o_weight_grad.astype(jnp.bfloat16), ("fsdp", "heads"), scatter_dimension=0, tiled=True
        ).astype(jnp.float32),
        lax.psum_scatter(
            gain_one_grad.astype(jnp.bfloat16), ("fsdp", "heads"), scatter_dimension=0, tiled=True
        ).astype(jnp.float32),
    )
    return (
        output,
        input_grad,
        attn_grads[0],
        attn_grads[1],
        attn_grads[2],
        attn_grads[3],
        attn_grads[4],
        ffn_grads[0],
        ffn_grads[1],
        ffn_grads[2],
        ffn_grads[3],
    )


def solution(mesh):
    return jax.shard_map(
        per_device,
        mesh=mesh,
        in_specs=(
            P("fsdp", "heads", None),
            P("fsdp", None),
            P(("fsdp", "heads"), "tensor"),
            P(("fsdp", "heads"), "tensor"),
            P(("fsdp", "heads"), "tensor"),
            P(("fsdp", "heads"), "tensor"),
            P(("fsdp", "heads")),
            P(("fsdp", "heads"), "tensor"),
            P(("fsdp", "heads"), "tensor"),
            P(("fsdp", "heads"), "tensor"),
            P(("fsdp", "heads")),
            P("fsdp", "heads", None),
        ),
        out_specs=(
            P("fsdp", "heads", None),
            P("fsdp", "heads", None),
            P(("fsdp", "heads"), "tensor"),
            P(("fsdp", "heads"), "tensor"),
            P(("fsdp", "heads"), "tensor"),
            P(("fsdp", "heads"), "tensor"),
            P(("fsdp", "heads")),
            P(("fsdp", "heads"), "tensor"),
            P(("fsdp", "heads"), "tensor"),
            P(("fsdp", "heads"), "tensor"),
            P(("fsdp", "heads")),
        ),
        check_vma=False,
    )
```

profile of v0, /device:TPU:0, one launch (start us, length us, event | category | flops | bytes accessed | tf_op | source)
XLA Modules:
  0.0 1935.9 jit_solution(1530565651915617410)
XLA Ops:
  86.5 13.5 all-to-all-done
  104.6 39.1 %while.28 = (s32[]{:T(128)}, bf16[2,4,512,2,64]{2,4,3,1,0:T(8,128)(2,1)}, f32[2,4,2,512]{3,2,1,0:T(2,128)S(1)}, s32[2]{0:T(128)S(1)}, s32[4,1024]{1,0:T(4,128)S(...) while((s32[]{:T(128)}, ...), condition=%wide.region_6.7_spmd.clone, body=%wide.region_3.6_spmd.clone.sunk | while | flops 1129050624 | bytes 62042312 | solution.py:170
  154.2 27.8 %all_to_all.81 = bf16[4,1024,1,128]{3,0,2,1:T(4,128)(2,1)S(1)} all-to-all(bf16[4,1024,1,128]{3,0,2,1:T(4,128)(2,1)S(1)} %reshape.399), channel_id=1, replica_groups=mesh['fsdp'=2,'heads'=4,'tensor'=4] {'heads'}, dimensions={1} | all-to-all | bytes 2097152 | tf_op jit(solution)/shard_map/all_to_all | solution.py:173
  200.4 281.0 %all-reduce.8.cloned.1.call-done = f32[1024,2048]{1,0:T(8,128)} async-done(((f32[1024,2048]{1,0:T(8,128)}), f32[1024,2048]{1,0:T(8,128)}) %all-reduce.8.cloned.1.call-update) | async-done | bytes 8388624 | tf_op jit(solution)/shard_map/psum | solution.py:178
  493.5 42.9 %all-gather.12.cloned.1.call-done = bf16[2048,2048]{1,0:T(8,128)(2,1)} async-done(((bf16[256,2048]{1,0:T(8,128)(2,1)}), bf16[2048,2048]{1,0:T(8,128)(2,1)}) %all-gather.12.cloned.1.call-update) | async-done | bytes 8388624 | tf_op jit(solution)/shard_map/all_gather | solution.py:111
  536.4 14.4 fusion.85
  550.8 41.6 %all-gather.14.cloned.1.call-done = bf16[2048,2048]{1,0:T(8,128)(2,1)} async-done(((bf16[256,2048]{1,0:T(8,128)(2,1)}), bf16[2048,2048]{1,0:T(8,128)(2,1)}) %all-gather.14.cloned.1.call-update) | async-done | bytes 8388624 | tf_op jit(solution)/shard_map/all_gather | solution.py:112
  592.4 14.4 fusion.86
  606.9 41.6 %all-gather.16.cloned.1.call-done = bf16[2048,2048]{1,0:T(8,128)(2,1)} async-done(((bf16[256,2048]{1,0:T(8,128)(2,1)}), bf16[2048,2048]{1,0:T(8,128)(2,1)}) %all-gather.16.cloned.1.call-update) | async-done | bytes 8388624 | tf_op jit(solution)/shard_map/all_gather | solution.py:113
  648.5 21.6 %multiply_convert_fusion = (bf16[1024,2048]{1,0:T(8,128)(2,1)}, bf16[1024,2048]{1,0:T(8,128)(2,1)}, bf16[1024,2048]{1,0:T(8,128)(2,1)}) fusion(f32[1024,2048]{1,0:T(8,128)} %fusion.85, f32[1024,2048]{1,0:T(8,128)} %fusion.86, bf16[1024,2048]{1,0:T(8,128)(2,1)} %bitcast.317, bf16[2048,2048]{1,0:T(8,128)(2,1)} %all-gather.16.cloned.1.call-done), kind=kOutput, calls=%fused_computation.90 | convolution fusion | flops 8623489024 | bytes 41943040 | tf_op jit(solution)/shard_map/dot_general | solution.py:60
  670.0 13.1 fusion.87
  683.2 12.8 convolution_add_fusion
  696.0 291.0 %all-reduce.10.cloned.1.call-done = f32[1024,2048]{1,0:T(8,128)} async-done(((f32[1024,2048]{1,0:T(8,128)}), f32[1024,2048]{1,0:T(8,128)}) %all-reduce.10.cloned.1.call-update) | async-done | bytes 8388624 | tf_op jit(solution)/shard_map/psum | solution.py:201
  1012.0 14.3 all-to-all-done.3
  1030.8 156.3 %while.29 = (s32[]{:T(128)}, f32[4,1024,64]{1,2,0:T(8,128)}, f32[4,1024,64]{1,2,0:T(8,128)S(1)}, bf16[2,4,512,2,64]{2,4,3,1,0:T(8,128)(2,1)}, s32[2]{0:T(128)S(1...) while((s32[]{:T(128)}, f32[4,1024,64]{1,2,0:T(8,128)}, ...), condition=%wide.region_14.15_spmd.clone, body=%wide.region_12.14_spmd.clone.sunk | while | flops 2749114880 | bytes 198275360 | solution.py:255
  1053.3 22.7 %fusion.155 = f32[4,1024,64]{1,2,0:T(8,128)} fusion(f32[4,2,512,1024]{3,2,1,0:T(8,128)} %fusion.153, f32[4,512,2,1024]{3,1,2,0:T(8,128)} %fusion.154, f32[4,1024,64]{1,2,0:T(8,128)} %get-tuple-element.543, pred[]{:T(512)S(6)} %compare.3, bf16[4,1024,2,64]{1,3,2,0:T(8,128)(2,1)} %get-tuple-element.564, s32[]{:T(128)S(6)} %select_n.76), kind=kOutput, calls=%fused_computation.41.clone.1 | convolution fusion | flops 558371840 | bytes 69730312 | tf_op jit(solution)/shard_map/while/body/eval_jaxpr/shqk,sqhd->skd/dot_general | solution.py:243
  1083.5 25.3 %fusion.157 = bf16[2,4,512,2,64]{2,4,3,1,0:T(8,128)(2,1)} fusion(bf16[2,4,512,2,64]{2,4,3,1,0:T(8,128)(2,1)} %get-tuple-element.545, s32[]{:T(128)S(6)} %copy.202, f32[4,2,512,1024]{3,2,1,0:T(8,128)} %fusion.153, f32[4,512,2,1024]{3,1,2,0:T(8,128)} %fusion.154, bf16[4,1024,64]{1,2,0:T(8,128)(2,1)S(1)} %get-tuple-element.565), kind=kOutput, calls=%fused_computation.46.clone.1 | convolution fusion | flops 558109696 | bytes 68157440 | tf_op jit(solution)/shard_map/while/body/eval_jaxpr/shqk,skd->sqhd/dot_general | solution.py:240
  1131.2 23.1 %fusion.155 = f32[4,1024,64]{1,2,0:T(8,128)} fusion(f32[4,2,512,1024]{3,2,1,0:T(8,128)} %fusion.153, f32[4,512,2,1024]{3,1,2,0:T(8,128)} %fusion.154, f32[4,1024,64]{1,2,0:T(8,128)} %get-tuple-element.543, pred[]{:T(512)S(6)} %compare.3, bf16[4,1024,2,64]{1,3,2,0:T(8,128)(2,1)} %get-tuple-element.564, s32[]{:T(128)S(6)} %select_n.76), kind=kOutput, calls=%fused_computation.41.clone.1 | convolution fusion | flops 558371840 | bytes 69730312 | tf_op jit(solution)/shard_map/while/body/eval_jaxpr/shqk,sqhd->skd/dot_general | solution.py:243
  1161.9 25.3 %fusion.157 = bf16[2,4,512,2,64]{2,4,3,1,0:T(8,128)(2,1)} fusion(bf16[2,4,512,2,64]{2,4,3,1,0:T(8,128)(2,1)} %get-tuple-element.545, s32[]{:T(128)S(6)} %copy.202, f32[4,2,512,1024]{3,2,1,0:T(8,128)} %fusion.153, f32[4,512,2,1024]{3,1,2,0:T(8,128)} %fusion.154, bf16[4,1024,64]{1,2,0:T(8,128)(2,1)S(1)} %get-tuple-element.565), kind=kOutput, calls=%fused_computation.46.clone.1 | convolution fusion | flops 558109696 | bytes 68157440 | tf_op jit(solution)/shard_map/while/body/eval_jaxpr/shqk,skd->sqhd/dot_general | solution.py:240
  1191.4 17.2 all_to_all.82
  1231.0 14.1 convolution_convert_fusion.1
  1245.1 14.0 convolution_convert_fusion
  1259.4 14.2 convert_bitcast_fusion
  1277.5 17.6 all_to_all.83
  1305.4 13.9 convolution_convert_fusion.2
  1334.4 73.2 %reduce-scatter.16.cloned.1.call-done = bf16[256,2048]{1,0:T(8,128)(2,1)} async-done(((bf16[2048,2048]{1,0:T(8,128)(2,1)}), bf16[256,2048]{1,0:T(8,128)(2,1)}) %reduce-scatter.16.cloned.1.call-update) | async-done | bytes 1048592 | tf_op jit(solution)/shard_map/reduce_scatter | solution.py:206
  1410.4 72.1 %reduce-scatter.18.cloned.1.call-done = bf16[256,2048]{1,0:T(8,128)(2,1)} async-done(((bf16[2048,2048]{1,0:T(8,128)(2,1)}), bf16[256,2048]{1,0:T(8,128)(2,1)}) %reduce-scatter.18.cloned.1.call-update) | async-done | bytes 1048592 | tf_op jit(solution)/shard_map/reduce_scatter | solution.py:209
  1485.3 72.0 %reduce-scatter.20.cloned.1.call-done = bf16[256,2048]{0,1:T(8,128)(2,1)} async-done(((bf16[2048,2048]{0,1:T(8,128)(2,1)}), bf16[256,2048]{0,1:T(8,128)(2,1)}) %reduce-scatter.20.cloned.1.call-update) | async-done | bytes 1048592 | tf_op jit(solution)/shard_map/reduce_scatter | solution.py:212
  1559.8 41.7 %reduce-scatter.8.cloned.1.call-done = bf16[256,512]{1,0:T(8,128)(2,1)} async-done(((bf16[2048,512]{1,0:T(8,128)(2,1)}), bf16[256,512]{1,0:T(8,128)(2,1)}) %reduce-scatter.8.cloned.1.call-update) | async-done | bytes 262160 | tf_op jit(solution)/shard_map/reduce_scatter | solution.py:300
  1603.4 292.1 %all-reduce.12.cloned.1.call-done = (bf16[1024,2048]{1,0:T(8,128)(2,1)}, bf16[1024,2048]{1,0:T(8,128)(2,1)}) async-done(((bf16[1024,2048]{1,0:T(8,128)(2,1)}, bf16[1024,2048]{1,0:T(8,128)(2,1)}), (bf16[1024,2048]{1,0:T(8,128)(2,1)}, bf16[1024,2048]{1,0:T(8,128)(2,1)})) %all-reduce.12.cloned.1.call-update) | async-done | bytes 8388624 | tf_op jit(solution)/shard_map/psum | solution.py:185
  1902.3 12.4 fusion.59
  1914.7 13.7 all-reduce.2
  (263 shorter events, 318.9 us)
Async XLA Ops:
  7.2 58.8 %all-gather.8.cloned.1.call-start = ((), (), s32[]{:S(2)}) async-start(), calls=%async_computation.13 | async-start | bytes 2359296 | tf_op jit(solution)/shard_map/all_gather | solution.py:106
  19.0 33.5 %copy-start.24 = (f32[8,1,256]{2,1,0:T(1,128)}, f32[8,1,256]{2,1,0:T(1,128)S(1)}, u32[]{:S(2)}) copy-start(f32[8,1,256]{2,1,0:T(1,128)S(1)} %convert_element_type.289) | copy-start | bytes 24580
  25.3 14.6 copy-start.29
  25.3 14.6 copy-start.26
  52.5 20.9 %copy-start.14 = (f32[4,256,32]{1,2,0:T(8,128)}, f32[4,256,32]{1,2,0:T(8,128)S(1)}, u32[]{:S(2)}) copy-start(f32[4,256,32]{1,2,0:T(8,128)S(1)} %get-tuple-element.363) | copy-start | bytes 393220
  62.1 18.2 all-to-all-start.1
  75.0 29.6 %copy-start.9 = (s32[4,1024]{1,0:T(4,128)S(1)}, s32[4,1024]{1,0:T(4,128)}, u32[]{:S(2)}) copy-start(s32[4,1024]{1,0:T(4,128)} %param.19) | copy-start | bytes 49156
  80.3 19.7 %all-to-all-start = ((bf16[4,256,4,128]{1,3,0,2:T(8,128)(2,1)}), bf16[4,256,4,128]{1,3,0,2:T(8,128)(2,1)}, u32[]{:S(2)}, u32[]{:S(2)}) async-start(bf16[4,256,4,128]{1,3,0,2:T(8,128)(2,1)} %copy.105), calls=%async_computation | async-start | bytes 2097152 | tf_op jit(solution)/shard_map/all_to_all | solution.py:132
  84.6 98.4 %all-gather.10.cloned.1.call-start = ((), (), s32[]{:S(2)}) async-start(), calls=%async_computation.14 | async-start | bytes 2359296 | tf_op jit(solution)/shard_map/all_gather | solution.py:109
  85.3 396.1 %all-reduce.8.cloned.1.call-start = ((), (), s32[]{:S(2)}) async-start(), calls=%async_computation.15 | async-start | bytes 16777216 | tf_op jit(solution)/shard_map/psum | solution.py:178
  143.7 47.0 %copy-start.4 = (bf16[4,1024,64]{1,2,0:T(8,128)(2,1)}, bf16[4,1024,64]{1,2,0:T(8,128)(2,1)S(1)}, u32[]{:S(2)}) copy-start(bf16[4,1024,64]{1,2,0:T(8,128)(2,1)S(1)} %get-tuple-element.593) | copy-start | bytes 1572868
  190.7 345.7 %all-gather.12.cloned.1.call-start = ((), (), s32[]{:S(2)}) async-start(), calls=%async_computation.16 | async-start | bytes 9437184 | tf_op jit(solution)/shard_map/all_gather | solution.py:111
  191.3 401.1 %all-gather.14.cloned.1.call-start = ((), (), s32[]{:S(2)}) async-start(), calls=%async_computation.17 | async-start | bytes 9437184 | tf_op jit(solution)/shard_map/all_gather | solution.py:112
  191.9 456.6 %all-gather.16.cloned.1.call-start = ((), (), s32[]{:S(2)}) async-start(), calls=%async_computation.18 | async-start | bytes 9437184 | tf_op jit(solution)/shard_map/all_gather | solution.py:113
  192.5 794.5 %all-reduce.10.cloned.1.call-start = ((), (), s32[]{:S(2)}) async-start(), calls=%async_computation.19 | async-start | bytes 16777216 | tf_op jit(solution)/shard_map/psum | solution.py:201
  670.0 13.1 copy-start.33
  1007.0 23.9 %copy-start.5 = (bf16[4,1024,64]{1,2,0:T(8,128)(2,1)S(1)}, bf16[4,1024,64]{1,2,0:T(8,128)(2,1)}, u32[]{:S(2)}) copy-start(bf16[4,1024,64]{1,2,0:T(8,128)(2,1)} %copy-done.4) | copy-start | bytes 1572868
  1008.4 17.9 all-to-all-start.3
  1012.0 316.5 %reduce-scatter.10.cloned.1.call-start = ((), (), s32[]{:S(2)}) async-start(), calls=%async_computation.21 | async-start | bytes 589824 | tf_op jit(solution)/shard_map/reduce_scatter | solution.py:303
  1191.4 20.3 %copy-start.15 = (f32[4,256,32]{1,2,0:T(8,128)S(1)}, f32[4,256,32]{1,2,0:T(8,128)}, u32[]{:S(2)}) copy-start(f32[4,256,32]{1,2,0:T(8,128)} %copy-done.14) | copy-start | bytes 393220
  1191.4 20.3 %copy-start.19 = (f32[4,256,32]{1,2,0:T(8,128)S(1)}, f32[4,256,32]{1,2,0:T(8,128)}, u32[]{:S(2)}) copy-start(f32[4,256,32]{1,2,0:T(8,128)} %get-tuple-element.361) | copy-start | bytes 393220
  1217.4 112.6 %reduce-scatter.12.cloned.1.call-start = ((), (), s32[]{:S(2)}) async-start(), calls=%async_computation.22 | async-start | bytes 589824 | tf_op jit(solution)/shard_map/reduce_scatter | solution.py:306
  1223.2 109.4 %reduce-scatter.14.cloned.1.call-start = ((), (), s32[]{:S(2)}) async-start(), calls=%async_computation.23 | async-start | bytes 2359296 | tf_op jit(solution)/shard_map/reduce_scatter | solution.py:309
  1230.5 177.1 %reduce-scatter.16.cloned.1.call-start = ((), (), s32[]{:S(2)}) async-start(), calls=%async_computation.24 | async-start | bytes 9437184 | tf_op jit(solution)/shard_map/reduce_scatter | solution.py:206
  1245.1 237.4 %reduce-scatter.18.cloned.1.call-start = ((), (), s32[]{:S(2)}) async-start(), calls=%async_computation.25 | async-start | bytes 9437184 | tf_op jit(solution)/shard_map/reduce_scatter | solution.py:209
  1259.2 298.1 %reduce-scatter.20.cloned.1.call-start = ((), (), s32[]{:S(2)}) async-start(), calls=%async_computation.26 | async-start | bytes 9437184 | tf_op jit(solution)/shard_map/reduce_scatter | solution.py:212
  1273.6 327.9 %reduce-scatter.8.cloned.1.call-start = ((), (), s32[]{:S(2)}) async-start(), calls=%async_computation.20 | async-start | bytes 2359296 | tf_op jit(solution)/shard_map/reduce_scatter | solution.py:300
  1305.1 14.2 copy-start.11
  1305.1 590.4 %all-reduce.12.cloned.1.call-start = ((), (), s32[]{:S(2)}) async-start(), calls=%async_computation.27 | async-start | bytes 16777216 | tf_op jit(solution)/shard_map/psum | solution.py:185
  1326.6 568.9 %copy-start.25 = (f32[8,1,256]{2,1,0:T(1,128)S(1)}, f32[8,1,256]{2,1,0:T(1,128)}, u32[]{:S(2)}) copy-start(f32[8,1,256]{2,1,0:T(1,128)} %copy-done.24) | copy-start | bytes 24580
  1326.6 568.9 %copy-start.27 = (f32[1024]{0:T(1024)S(1)}, f32[1024]{0:T(1024)}, u32[]{:S(2)}) copy-start(f32[1024]{0:T(1024)} %copy-done.26) | copy-start | bytes 12292
  1410.4 491.9 %copy-start.30 = (f32[1,2,4,128]{3,1,2,0:T(2,128)S(1)}, f32[1,2,4,128]{3,1,2,0:T(2,128)}, u32[]{:S(2)}) copy-start(f32[1,2,4,128]{3,1,2,0:T(2,128)} %copy-done.29) | copy-start | bytes 12292
  (23 other events, 119.6 us)
Sparse Core Ops, SparseCore 0:
  9.9 31.1 all-gather.7
  87.3 28.7 all-gather.9
  190.9 290.4 all-reduce.7
  483.1 53.2 all-gather.11
  538.1 54.2 all-gather.13
  594.2 54.2 all-gather.15
  696.1 290.8 all-reduce.9
  1217.5 32.1 reduce-scatter.9
  1253.4 34.3 reduce-scatter.11
  1291.4 41.0 reduce-scatter.13
  1336.0 71.5 reduce-scatter.15
  1410.9 71.5 reduce-scatter.17
  1485.9 71.2 reduce-scatter.19
  1560.4 41.1 reduce-scatter.7
  1604.6 290.8 all-reduce.11
where the time goes:
time: 1940 us
  waiting for transfers between devices  1290 us (66%)
  matrix products  345 us (18%)
  blocking collectives  115 us (6%)
  other arithmetic  93.9 us (5%)
  local copies, waits for them, and re-layouts  59.9 us (3%)
    psum x1, waiting for transfers between devices, per_device(): lax.psum(ffn_part.astype(jnp.bfloat16), 'tensor').astype(jnp.float32)  292 us
    psum x1, waiting for transfers between devices, per_device(): d_normed_two = lax.psum(back_part, 'tensor')  291 us
    psum x1, waiting for transfers between devices, per_device(): residual = tokens_f + lax.psum(attn_part, 'tensor')  281 us
    reduce_scatter x1, waiting for transfers between devices, per_device(): lax.psum_scatter(gate_grad.astype(jnp.bfloat16), ('fsdp', 'heads'), scatt...  73.2 us
    reduce_scatter x1, waiting for transfers between devices, per_device(): lax.psum_scatter(up_grad.astype(jnp.bfloat16), ('fsdp', 'heads'), scatter...  72.1 us
    reduce_scatter x1, waiting for transfers between devices, per_device(): lax.psum_scatter(down_grad.astype(jnp.bfloat16), ('fsdp', 'heads'), scatt...  72 us
    dot_general x7, matrix products, dot_rows(): lax.dot_general(left_in, right_in, (((0,), (0,)), ((), ())), preferred_el...  62 us
    dot_general x7, matrix products, dot_plain(): return jnp.dot(left_in, right_in, preferred_element_type=jnp.float32)  60 us
  transfers between devices with their start and end apart: 18, of which 14 were waited for; matrix products, arithmetic and copies ran while one was open for 12% of the time, Pallas kernels for 0%

commit v1 on v0

v1 whole, which is shorter than its diff:
```python
import functools
import math

import jax
import jax.numpy as jnp
import numpy as np
from jax import lax
from jax.experimental import pallas as pl
from jax.experimental.pallas import tpu as pltpu
from jax.sharding import PartitionSpec as P

HD = 64
EPSILON = 1e-05
ROPE_BASE = 500000.0
NEG_FILL = -1e30
LOG2E = math.log2(math.e)
BF = jnp.bfloat16
F32 = jnp.float32
CHUNKS = 2


def positions(segments):
    length_of = segments.shape[-1]
    column = jnp.arange(length_of, dtype=jnp.int32)
    before = jnp.concatenate([segments[..., :1] - 1, segments[..., :-1]], axis=-1)
    firsts = jnp.where(segments != before, column, jnp.zeros_like(column))
    starts = lax.cummax(firsts, axis=firsts.ndim - 1)
    return column - starts


def dot_plain(left_in, right_in):
    return jnp.dot(left_in, right_in, preferred_element_type=F32)


def dot_rows(left_in, right_in):
    return lax.dot_general(
        left_in, right_in, (((0,), (0,)), ((), ())), preferred_element_type=F32
    )


def dot_cols(left_in, right_in):
    return lax.dot_general(
        left_in, right_in, (((1,), (1,)), ((), ())), preferred_element_type=F32
    )


def line_sum(parts):
    count = parts.shape[0]
    me = lax.axis_index("tensor")

    def pick(j):
        return lax.dynamic_index_in_dim(parts, jnp.clip(j, 0, count - 1), 0, keepdims=False)

    from_left = from_right = None
    for t in range(1, count):
        to_right = pick(count - t + me)
        to_left = pick(t + me - count)
        if from_left is not None:
            to_right = (to_right.astype(F32) + from_left.astype(F32)).astype(BF)
            to_left = (to_left.astype(F32) + from_right.astype(F32)).astype(BF)
        from_left = lax.ppermute(to_right, "tensor", [(k, k + 1) for k in range(t)])
        from_right = lax.ppermute(
            to_left, "tensor", [(count - 1 - k, count - 2 - k) for k in range(t)]
        )
    return pick(me).astype(F32) + from_left.astype(F32) + from_right.astype(F32)


def line_gather(own):
    count = lax.axis_size("tensor")
    me = lax.axis_index("tensor")
    from_left = [None] * count
    from_right = [None] * count
    right = left = own
    for t in range(1, count):
        right = lax.ppermute(right, "tensor", [(k, k + 1) for k in range(t - 1, count - 1)])
        left = lax.ppermute(
            left, "tensor", [(count - 1 - k, count - 2 - k) for k in range(t - 1, count - 1)]
        )
        from_left[t], from_right[t] = right, left
    out = jnp.zeros((count,) + own.shape, own.dtype)
    out = lax.dynamic_update_index_in_dim(out, own, me, 0)
    for t in range(1, count):
        block = jnp.where(me >= t, from_left[t], from_right[count - t])
        out = lax.dynamic_update_index_in_dim(out, block, lax.rem(me - t + count, count), 0)
    return out


def pairs(count, bit):
    return [(k, k ^ bit) for k in range(count)]


def turn(values, cosine, sine):
    lane = lax.broadcasted_iota(jnp.int32, values.shape, 1)
    swapped = jnp.where(
        lax.rem(lane, 64) < 32, pltpu.roll(values, 96, 1), pltpu.roll(values, 32, 1)
    )
    return values * cosine + swapped * sine


def turn_kernel(turned, x_ref, cos_ref, sin_ref, out_ref):
    cosine, sine = cos_ref[...], sin_ref[...]
    for begin in range(0, x_ref.shape[1], 128):
        piece = x_ref[:, begin : begin + 128].astype(F32)
        if begin < turned:
            piece = turn(piece, cosine, sine)
        out_ref[:, begin : begin + 128] = piece.astype(out_ref.dtype)


def turn_call(x, cosine, sine, turned):
    rows, width = x.shape
    tile = min(256, rows)
    return pl.pallas_call(
        functools.partial(turn_kernel, turned),
        grid=(rows // tile,),
        in_specs=[
            pl.BlockSpec((tile, width), lambda i: (i, 0)),
            pl.BlockSpec((tile, 128), lambda i: (i, 0)),
            pl.BlockSpec((tile, 128), lambda i: (i, 0)),
        ],
        out_specs=pl.BlockSpec((tile, width), lambda i: (i, 0)),
        out_shape=jax.ShapeDtypeStruct((rows, width), BF),
        cost_estimate=pl.CostEstimate(
            flops=4 * rows * width, bytes_accessed=6 * rows * width, transcendentals=0
        ),
        name="turn",
    )(x, cosine, sine)


def attend_kernel(
    group, place_ref, q_ref, k0, k1, k2, k3, segq_ref, segk_ref, out_ref, lse_ref
):
    block = q_ref.shape[1]
    kv_heads = k0.shape[2] // (2 * HD)
    me = place_ref[0]
    scale = LOG2E / math.sqrt(HD)
    row = lax.broadcasted_iota(jnp.int32, (block, block), 0)
    col = lax.broadcasted_iota(jnp.int32, (block, block), 1)
    seg_q = segq_ref[0]
    refs = (k0, k1, k2, k3)
    bias = []
    for k in range(len(refs)):
        there = place_ref[1 + k]
        seg_k = segk_ref[0, :, pl.ds(pl.multiple_of(there * block, block), block)]
        ahead = (there - me) * block
        allowed = (seg_q == seg_k) & (row >= col + ahead)
        bias.append(jnp.where(allowed, 0.0, NEG_FILL))
    sums = []
    for g in range(kv_heads):
        keys = [r[0, :, g * HD : (g + 1) * HD] for r in refs]
        values = [r[0, :, (kv_heads + g) * HD : (kv_heads + g + 1) * HD] for r in refs]
        for j in range(group):
            head = g * group + j
            q = q_ref[0, :, head * HD : (head + 1) * HD]
            scores = [
                dot_cols(q, keys[k]) * scale + bias[k] for k in range(len(refs))
            ]
            peak = functools.reduce(jnp.maximum, scores)
            peak = jnp.max(peak, axis=1, keepdims=True)
            weights = [jnp.exp2(s - peak) for s in scores]
            total = functools.reduce(jnp.add, weights)
            total = jnp.sum(total, axis=1, keepdims=True)
            mixed = functools.reduce(
                jnp.add, [dot_plain(w.astype(BF), v) for w, v in zip(weights, values)]
            )
            out_ref[0, :, head * HD : (head + 1) * HD] = (mixed / total).astype(BF)
            sums.append(peak + jnp.log2(total))
    lane = lax.broadcasted_iota(jnp.int32, (block, 128), 1)
    stacked = jnp.zeros((block, 128), F32)
    for head, value in enumerate(sums):
        stacked = jnp.where(lane == head, value, stacked)
    lse_ref[0] = jnp.transpose(stacked)[: len(sums)]


def attend_call(place, q, blocks, seg_q, seg_k):
    seqs, block, width = q.shape
    heads = width // HD
    kv_width = blocks[0].shape[2]
    group = heads // (kv_width // (2 * HD))
    seq_len = seg_k.shape[2]
    keys = pl.BlockSpec((1, block, kv_width), lambda s, p: (s, 0, 0))
    work = seqs * heads * block * seq_len
    return pl.pallas_call(
        functools.partial(attend_kernel, group),
        grid_spec=pltpu.PrefetchScalarGridSpec(
            num_scalar_prefetch=1,
            grid=(seqs,),
            in_specs=[
                pl.BlockSpec((1, block, width), lambda s, p: (s, 0, 0)),
                keys,
                keys,
                keys,
                keys,
                pl.BlockSpec((1, block, 1), lambda s, p: (s, 0, 0)),
                pl.BlockSpec((1, 1, seq_len), lambda s, p: (s, 0, 0)),
            ],
            out_specs=[
                pl.BlockSpec((1, block, width), lambda s, p: (s, 0, 0)),
                pl.BlockSpec((1, heads, block), lambda s, p: (s, 0, 0)),
            ],
        ),
        out_shape=[
            jax.ShapeDtypeStruct((seqs, block, width), BF),
            jax.ShapeDtypeStruct((seqs, heads, block), F32),
        ],
        cost_estimate=pl.CostEstimate(
            flops=4 * work * HD * 4, bytes_accessed=6 * q.size, transcendentals=work
        ),
        name="attend",
    )(place, q, *blocks, seg_q, seg_k)


def attend_back_kernel(
    group,
    place_ref,
    q_ref,
    k0,
    k1,
    k2,
    k3,
    segq_ref,
    segk_ref,
    out_ref,
    grad_ref,
    lse_ref,
    dq_ref,
    d0,
    d1,
    d2,
    d3,
    bias_ref,
    dsc_ref,
):
    block = q_ref.shape[1]
    kv_heads = k0.shape[2] // (2 * HD)
    me = place_ref[0]
    scale = LOG2E / math.sqrt(HD)
    back_scale = 1.0 / math.sqrt(HD)
    refs, d_refs = (k0, k1, k2, k3), (d0, d1, d2, d3)
    key_row = lax.broadcasted_iota(jnp.int32, (block, block), 0)
    q_col = lax.broadcasted_iota(jnp.int32, (block, block), 1)
    seg_q = segq_ref[0]
    for k in range(len(refs)):
        there = place_ref[1 + k]
        seg_k = segk_ref[0, pl.ds(pl.multiple_of(there * block, block), block), :]
        ahead = (there - me) * block
        allowed = (seg_q == seg_k) & (q_col >= key_row + ahead)
        bias_ref[k] = jnp.where(allowed, 0.0, NEG_FILL)
    width = group * block
    product = out_ref[0].astype(F32) * grad_ref[0].astype(F32)
    total_heads = kv_heads * group
    feature = lax.broadcasted_iota(jnp.int32, (total_heads, product.shape[1]), 1)
    owner = lax.broadcasted_iota(jnp.int32, (total_heads, product.shape[1]), 0)
    picks = jnp.where(feature // HD == owner, 1.0, 0.0).astype(F32)
    deltas = lax.dot_general(
        picks,
        product,
        (((1,), (1,)), ((), ())),
        preferred_element_type=F32,
        precision=lax.Precision.HIGHEST,
    )
    for g in range(kv_heads):
        heads = range(g * group, (g + 1) * group)
        q = jnp.concatenate([q_ref[0, :, h * HD : (h + 1) * HD] for h in heads], 0)
        grad = jnp.concatenate([grad_ref[0, :, h * HD : (h + 1) * HD] for h in heads], 0)
        d_query = None
        for k in range(len(refs)):
            keys = refs[k][0, :, g * HD : (g + 1) * HD]
            values = refs[k][0, :, (kv_heads + g) * HD : (kv_heads + g + 1) * HD]
            scores = dot_cols(keys, q)
            d_probs = dot_cols(values, grad)
            probs_low = []
            for j, h in enumerate(heads):
                cols = slice(j * block, (j + 1) * block)
                probs = jnp.exp2(
                    scores[:, cols] * scale + (bias_ref[k] - lse_ref[0, h : h + 1, :])
                )
                probs_low.append(probs.astype(BF))
                dsc_ref[:, cols] = (
                    probs * (d_probs[:, cols] - deltas[h : h + 1, :])
                ).astype(BF)
            d_scores = dsc_ref[...]
            d_value = dot_plain(jnp.concatenate(probs_low, 1), grad)
            d_key = dot_plain(d_scores, q) * back_scale
            d_refs[k][0, :, g * HD : (g + 1) * HD] = d_key.astype(BF)
            d_refs[k][0, :, (kv_heads + g) * HD : (kv_heads + g + 1) * HD] = d_value.astype(BF)
            part = dot_rows(d_scores, keys)
            d_query = part if d_query is None else d_query + part
        d_query = d_query * back_scale
        for j, h in enumerate(heads):
            dq_ref[0, :, h * HD : (h + 1) * HD] = d_query[j * block : (j + 1) * block].astype(BF)


def attend_back_call(place, q, blocks, seg_q, seg_k, out, grad, lse):
    seqs, block, width = q.shape
    heads = width // HD
    kv_width = blocks[0].shape[2]
    group = heads // (kv_width // (2 * HD))
    seq_len = seg_k.shape[1]
    keys = pl.BlockSpec((1, block, kv_width), lambda s, p: (s, 0, 0))
    rows = pl.BlockSpec((1, block, width), lambda s, p: (s, 0, 0))
    work = seqs * heads * block * seq_len
    return pl.pallas_call(
        functools.partial(attend_back_kernel, group),
        grid_spec=pltpu.PrefetchScalarGridSpec(
            num_scalar_prefetch=1,
            grid=(seqs,),
            in_specs=[
                rows,
                keys,
                keys,
                keys,
                keys,
                pl.BlockSpec((1, 1, block), lambda s, p: (s, 0, 0)),
                pl.BlockSpec((1, seq_len, 1), lambda s, p: (s, 0, 0)),
                rows,
                rows,
                pl.BlockSpec((1, heads, block), lambda s, p: (s, 0, 0)),
            ],
            out_specs=[rows, keys, keys, keys, keys],
            scratch_shapes=[
                pltpu.VMEM((4, block, block), F32),
                pltpu.VMEM((block, group * block), BF),
            ],
        ),
        out_shape=[jax.ShapeDtypeStruct(q.shape, BF)]
        + [jax.ShapeDtypeStruct(blocks[0].shape, BF)] * 4,
        cost_estimate=pl.CostEstimate(
            flops=10 * work * HD * 4, bytes_accessed=12 * q.size, transcendentals=work
        ),
        name="attend_back",
    )(place, q, *blocks, seg_q, seg_k, out, grad, lse)


def inverse_rms(values):
    return lax.rsqrt(jnp.mean(values * values, axis=-1, keepdims=True) + EPSILON)


def norm_back(values, gain, incoming):
    scale = inverse_rms(values)
    gain_terms = jnp.sum(incoming * values * scale, axis=0)
    weighted = incoming * gain
    inner = jnp.mean(weighted * values, axis=-1, keepdims=True)
    return scale * weighted - values * (scale * scale * scale) * inner, gain_terms


def per_device(
    tokens,
    segments,
    q_weight,
    k_weight,
    v_weight,
    o_weight,
    attn_gain,
    gate_weight,
    up_weight,
    down_weight,
    ffn_gain,
    cotangent,
):
    seqs, block, width = tokens.shape
    seq_len = segments.shape[1]
    parts = lax.axis_size("heads")
    ways = lax.axis_size("tensor")
    owners = ("fsdp", "heads")
    here = lax.axis_index("heads")
    me = lax.axis_index("tensor")
    q_width, k_width = q_weight.shape[1], k_weight.shape[1]
    kv_width = 2 * k_width
    qkv_width = q_width + kv_width
    per_chunk = seqs // CHUNKS
    rows = per_chunk * block
    own_rows = rows // ways

    pad = jnp.zeros((q_weight.shape[0], 126), BF)
    packed = jnp.concatenate(
        [q_weight, k_weight, v_weight, attn_gain[:, None], ffn_gain[:, None], pad], axis=1
    )

    def gathered(shard):
        return lax.all_gather(shard, owners, axis=0, tiled=True)

    packed = gathered(packed)
    full_o = gathered(o_weight)
    full_g = gathered(gate_weight)
    full_u = gathered(up_weight)
    full_d = gathered(down_weight)
    full_qkv = packed[:, :qkv_width]
    gains = packed[:, qkv_width : qkv_width + 2].T.astype(F32)
    gain_one, gain_two = gains[0:1], gains[1:2]

    where_all = positions(segments)
    where_here = lax.dynamic_slice_in_dim(where_all, here * block, block, 1)
    seg_here = lax.dynamic_slice_in_dim(segments, here * block, block, 1)
    lane = np.arange(128)
    frequency = jnp.asarray(
        ROPE_BASE ** (-2.0 * (np.arange(128) % 32).astype(np.float32) / HD), F32
    )
    angles = where_here.reshape(seqs * block, 1).astype(F32) * frequency
    cosine = jnp.cos(angles)
    sine = jnp.sin(angles) * jnp.asarray(np.where(lane % 64 < 32, -1.0, 1.0), F32)
    place = jnp.stack([here] + [here ^ k for k in range(parts)]).astype(jnp.int32)

    def chunk_of(x, c):
        return lax.slice_in_dim(x, c * per_chunk, (c + 1) * per_chunk, axis=0)

    def own(x):
        return lax.dynamic_slice_in_dim(x, me * own_rows, own_rows, 0)

    state = []
    for c in range(CHUNKS):
        s = {}
        tok = chunk_of(tokens, c).reshape(rows, width)
        tok_f = tok.astype(F32)
        s["tok"] = tok
        s["normed_one"] = (tok_f * inverse_rms(tok_f) * gain_one).astype(BF)
        s["cos"] = lax.slice_in_dim(cosine, c * rows, (c + 1) * rows, axis=0)
        s["sin"] = lax.slice_in_dim(sine, c * rows, (c + 1) * rows, axis=0)
        kv = turn_call(
            dot_plain(s["normed_one"], full_qkv[:, q_width:]), s["cos"], s["sin"], k_width
        ).reshape(per_chunk, block, kv_width)
        kv2 = lax.ppermute(kv, "heads", pairs(parts, 2))
        kv1 = lax.ppermute(kv, "heads", pairs(parts, 1))
        kv3 = lax.ppermute(kv2, "heads", pairs(parts, 1))
        s["kv"] = (kv, kv1, kv2, kv3)
        s["q"] = turn_call(
            dot_plain(s["normed_one"], full_qkv[:, :q_width]), s["cos"], s["sin"], q_width
        ).reshape(per_chunk, block, q_width)
        state.append(s)
    for c, s in enumerate(state):
        seg_q = chunk_of(seg_here, c)
        seg_k = chunk_of(segments, c)
        s["attended"], s["lse"] = attend_call(
            place, s["q"], s["kv"], seg_q[:, :, None], seg_k[:, None, :]
        )
        s["seg"] = (seg_q[:, None, :], seg_k[:, :, None])
        attn = dot_cols(s["attended"].reshape(rows, q_width), full_o).astype(BF)
        s["residual"] = own(s["tok"]).astype(F32) + line_sum(
            attn.reshape(ways, own_rows, width)
        )
        normed_two = (s["residual"] * inverse_rms(s["residual"]) * gain_two).astype(BF)
        s["normed_two"] = line_gather(normed_two).reshape(rows, width)
    for c, s in enumerate(state):
        cot = chunk_of(cotangent, c).reshape(rows, width)
        gate = dot_plain(s["normed_two"], full_g)
        up = dot_plain(s["normed_two"], full_u)
        sig = jax.nn.sigmoid(gate)
        s["hidden"] = (gate * sig * up).astype(BF)
        d_hidden = dot_plain(cot, full_d)
        s["d_gate"] = (d_hidden * up * (sig * (1.0 + gate * (1.0 - sig)))).astype(BF)
        s["d_up"] = (d_hidden * gate * sig).astype(BF)
        back = (dot_cols(s["d_gate"], full_g) + dot_cols(s["d_up"], full_u)).astype(BF)
        d_normed_two = line_sum(back.reshape(ways, own_rows, width))
        d_norm, s["gain_two"] = norm_back(s["residual"], gain_two, d_normed_two)
        s["d_resid"] = own(cot).astype(F32) + d_norm
        s["d_attn"] = line_gather(s["d_resid"].astype(BF)).reshape(rows, width)
        ffn = dot_cols(s["hidden"], full_d).astype(BF)
        out = s["residual"] + line_sum(ffn.reshape(ways, own_rows, width))
        s["output"] = line_gather(out.astype(BF)).reshape(per_chunk, block, width)

    def joined(name):
        return jnp.concatenate([s[name] for s in state], axis=0)

    def scattered(grad):
        return lax.psum_scatter(
            grad.astype(BF), owners, scatter_dimension=0, tiled=True
        ).astype(F32)

    cot_rows = cotangent.reshape(seqs * block, width)
    n_two = joined("normed_two")
    down_grad = scattered(dot_rows(cot_rows, joined("hidden")))
    gate_grad = scattered(dot_rows(n_two, joined("d_gate")))
    up_grad = scattered(dot_rows(n_two, joined("d_up")))

    for c, s in enumerate(state):
        d_attended = dot_plain(s["d_attn"], full_o).astype(BF).reshape(per_chunk, block, q_width)
        dq, b0, b1, b2, b3 = attend_back_call(
            place, s["q"], s["kv"], s["seg"][0], s["seg"][1], s["attended"], d_attended, s["lse"]
        )
        from3 = lax.ppermute(b3, "heads", pairs(parts, 1))
        from1 = lax.ppermute(b1, "heads", pairs(parts, 1))
        far = (b2.astype(F32) + from3.astype(F32)).astype(BF)
        from2 = lax.ppermute(far, "heads", pairs(parts, 2))
        d_kv = b0.astype(F32) + from1.astype(F32) + from2.astype(F32)
        d_q = turn_call(dq.reshape(rows, q_width), s["cos"], -s["sin"], q_width)
        d_kv = turn_call(d_kv.reshape(rows, kv_width), s["cos"], -s["sin"], k_width)
        s["d_qkv"] = jnp.concatenate([d_q, d_kv], axis=1)
        back = dot_cols(s["d_qkv"], full_qkv).astype(BF)
        d_normed_one = line_sum(back.reshape(ways, own_rows, width))
        d_norm, s["gain_one"] = norm_back(own(s["tok"]).astype(F32), gain_one, d_normed_one)
        s["input_grad"] = (
            line_gather((s["d_resid"] + d_norm).astype(BF))
            .astype(F32)
            .reshape(per_chunk, block, width)
        )
    attended = joined("attended").reshape(seqs * block, q_width)
    o_grad = scattered(dot_rows(joined("d_attn"), attended))
    qkv_grad = scattered(dot_rows(joined("normed_one"), joined("d_qkv")))
    gain_grads = jnp.stack(
        [sum(s["gain_one"] for s in state), sum(s["gain_two"] for s in state)]
    )
    gain_grads = lax.psum(gain_grads, ("fsdp", "heads", "tensor"))
    share = attn_gain.shape[0]
    index = lax.axis_index("fsdp") * parts + here
    gain_grads = lax.dynamic_slice_in_dim(gain_grads, index * share, share, 1)
    return (
        joined("output"),
        joined("input_grad"),
        qkv_grad[:, :q_width],
        qkv_grad[:, q_width : q_width + k_width],
        qkv_grad[:, q_width + k_width :],
        o_grad,
        gain_grads[0],
        gate_grad,
        up_grad,
        down_grad,
        gain_grads[1],
    )


def solution(mesh):
    rows = P("fsdp", "heads", None)
    matrix = P(("fsdp", "heads"), "tensor")
    vector = P(("fsdp", "heads"))
    return jax.shard_map(
        per_device,
        mesh=mesh,
        in_specs=(
            rows,
            P("fsdp", None),
            matrix,
            matrix,
            matrix,
            matrix,
            vector,
            matrix,
            matrix,
            matrix,
            vector,
            rows,
        ),
        out_specs=(
            rows,
            rows,
            matrix,
            matrix,
            matrix,
            matrix,
            vector,
            matrix,
            matrix,
            matrix,
            vector,
        ),
        check_vma=False,
    )
```

time: 1940 us -> 969 us (0.50)
  waiting for transfers between devices: 1290 us -> 251 us
  starting transfers between devices: 12.9 us -> 245 us
  matrix products: 345 us -> 190 us
  Pallas kernels: 0 us -> 74.1 us
  blocking collectives: 115 us -> 43.9 us
  local copies, waits for them, and re-layouts: 59.9 us -> 39.5 us
    psum x3 -> x0, waiting for transfers between devices: 864 us -> none  [the longest x1 292 us: per_device(): lax.psum(ffn_part.astype(jnp.bfloat16), 'tensor').astype(jnp.float32)]
    reduce_scatter x7 -> x5, waiting for transfers between devices: 260 us -> 0.01 us  [scattered(): lax.psum_scatter(grad.astype(BF), owners, scatter_dimension=0, tiled=True)]
    ppermute x0 -> x108, starting transfers between devices: none -> 244 us  [the longest x24 99.8 us: line_sum(): from_left = lax.ppermute(to_right, 'tensor', [(k, k + 1) for k in range(t)])]
    ppermute x0 -> x108, waiting for transfers between devices: none -> 228 us  [the longest x24 92.7 us: line_gather(): lax.ppermute(left, 'tensor', [(count - 1 - k, count - 2 - k) for k in ran...]
    dot_general x21 -> x12, matrix products: 229 us -> 81.8 us  [dot_plain(): return jnp.dot(left_in, right_in, preferred_element_type=F32)]
    all_gather x5, waiting for transfers between devices: 126 us -> 19.6 us  [gathered(): return lax.all_gather(shard, owners, axis=0, tiled=True)]
    pallas_call x0 -> x12, Pallas kernels: none -> 74.1 us  [the longest x2 32.7 us: attend_back_call(): pl.pallas_call(functools.partial(attend_back_kernel, group), grid_spec=pl...]
    all_to_all x3 -> x0, blocking collectives: 62.6 us -> none  [the longest x1 27.8 us: per_device(): lax.all_to_all(shortened(head_out), 'heads', split_axis=1, concat_axis=2,...]
  transfers between devices with their start and end apart: 18 -> 118, of which waited for: 14 -> 43; matrix products, arithmetic and copies ran while one was open for 12% -> 28% of each run, Pallas kernels for 0% -> 8%
where the time goes in v1:
time: 969 us; the launch traced here: 951 us
  waiting for transfers between devices  251 us (26%)
  starting transfers between devices  245 us (25%)
  matrix products  190 us (20%)
  other arithmetic  92.2 us (10%)
  Pallas kernels  74.1 us (8%)
  blocking collectives  43.9 us (5%)
  local copies, waits for them, and re-layouts  39.5 us (4%)
  between operations  16.6 us (2%)
    ppermute x24, starting transfers between devices, line_sum(): from_left = lax.ppermute(to_right, 'tensor', [(k, k + 1) for k in range(t)])  99.8 us
    ppermute x24, waiting for transfers between devices, line_gather(): lax.ppermute(left, 'tensor', [(count - 1 - k, count - 2 - k) for k in ran...  92.7 us
    ppermute x24, waiting for transfers between devices, line_sum(): from_left = lax.ppermute(to_right, 'tensor', [(k, k + 1) for k in range(t)])  85.9 us
    dot_general x12, matrix products, dot_plain(): return jnp.dot(left_in, right_in, preferred_element_type=F32)  81.8 us
    ppermute x24, starting transfers between devices, line_gather(): lax.ppermute(right, 'tensor', [(k, k + 1) for k in range(t - 1, count - 1)])  81.2 us
    dot_general x10, matrix products, dot_cols(): lax.dot_general(left_in, right_in, (((1,), (1,)), ((), ())), preferred_el...  57 us
    dot_general x5, matrix products, dot_rows(): lax.dot_general(left_in, right_in, (((0,), (0,)), ((), ())), preferred_el...  51 us
    psum x1, blocking collectives, per_device(): gain_grads = lax.psum(gain_grads, ('fsdp', 'heads', 'tensor'))  43.9 us
  transfers between devices with their start and end apart: 118, of which 43 were waited for; matrix products, arithmetic and copies ran while one was open for 28% of the time, Pallas kernels for 8%

profile of v1, /device:TPU:0, one launch (start us, length us, event | category | flops | bytes accessed | tf_op | source)
XLA Modules:
  0.0 951.4 jit_solution(7715801127114840654)
XLA Ops:
  28.3 19.6 %all-gather.6.cloned.1.call-done = bf16[2048,896]{1,0:T(8,128)(2,1)} async-done(((bf16[256,896]{1,0:T(8,128)(2,1)}), bf16[2048,896]{1,0:T(8,128)(2,1)}) %all-gather.6.cloned.1.call-update) | async-done | bytes 3670032 | tf_op jit(solution)/shard_map/all_gather | solution.py:380
  80.3 11.9 %attend.2 = (bf16[2,256,512]{2,1,0:T(8,128)(2,1)}, f32[2,8,256]{2,1,0:T(8,128)}) custom-call(s32[5]{0:T(128)} %stack.25.place_ref, bf16[2,256,512]{2,1,0:T(8,128)(2,1)} %bitcast.440, bf16[2,256,256]{2,1,0:T(8,128)(2,1)} %bitcast.448, bf16[2,256,256]{2,1,0:T(8,128)(2,1)} %copy-done.57, bf16[2,256,256]{2,1,0:T(8,128)(2,1)} %copy-done.56, ...), custom_call_target="tpu_custom_call" | custom-call | flops 4294967296 | bytes 1572864 | tf_op jit(solution)/shard_map/attend/pallas_call | solution.py:182
  99.8 11.4 %attend.3 = (bf16[2,256,512]{2,1,0:T(8,128)(2,1)}, f32[2,8,256]{2,1,0:T(8,128)}) custom-call(s32[5]{0:T(128)} %stack.25.place_ref, bf16[2,256,512]{2,1,0:T(8,128)(2,1)} %bitcast.443, bf16[2,256,256]{2,1,0:T(8,128)(2,1)} %bitcast.452, bf16[2,256,256]{2,1,0:T(8,128)(2,1)} %collective-permute-done.27.k1, bf16[2,256,256]{2,1,0:T(8,128)(2,1)} %copy-done.59, ...), custom_call_target="tpu_custom_call" | custom-call | flops 4294967296 | bytes 1572864 | tf_op jit(solution)/shard_map/attend/pallas_call | solution.py:182
  194.1 10.9 %collective-permute-start.9 = (bf16[128,2048]{1,0:T(8,128)(2,1)S(1)}, bf16[128,2048]{1,0:T(8,128)(2,1)}, u32[]{:S(2)}, u32[]{:S(2)}) collective-permute-start(bf16[128,2048]{1,0:T(8,128)(2,1)S(1)} %get-tuple-element.86), channel_id=1, source_target_pairs={{0,1},{1,2},{2,3},{4,5},{5,6},{6,7},{8,9},{9,10},{10,11},{12,13},{... | collective-permute-start | bytes 1572872 | tf_op jit(solution)/shard_map/ppermute | solution.py:75
  218.0 7.2 collective-permute-done.36
  227.9 9.2 collective-permute-done.38
  265.7 10.5 %fusion.129 = f32[512,2048]{1,0:T(8,128)} fusion(bf16[512,2048]{1,0:T(8,128)(2,1)} %bitcast.431, bf16[2048,2048]{1,0:T(8,128)(2,1)} %all-gather.12.cloned.1.call-done), kind=kOutput, calls=%fused_computation.296 | convolution fusion | flops 4294967296 | bytes 14680064 | tf_op jit(solution)/shard_map/dot_general | solution.py:32
  276.2 10.5 %fusion.132 = f32[512,2048]{1,0:T(8,128)} fusion(bf16[512,2048]{1,0:T(8,128)(2,1)} %bitcast.421, bf16[2048,2048]{1,0:T(8,128)(2,1)} %all-gather.14.cloned.1.call-done), kind=kOutput, calls=%fused_computation.299 | convolution fusion | flops 4294967296 | bytes 14680064 | tf_op jit(solution)/shard_map/dot_general | solution.py:32
  286.8 14.4 %multiply_convert_fusion = (bf16[512,2048]{1,0:T(8,128)(2,1)S(1)}, bf16[512,2048]{1,0:T(8,128)(2,1)S(1)}, bf16[512,2048]{1,0:T(8,128)(2,1)}) fusion(f32[512,2048]{1,0:T(8,128)} %fusion.132, f32[512,2048]{1,0:T(8,128)} %fusion.129, bf16[512,2048]{1,0:T(8,128)(2,1)} %bitcast.432, bf16[2048,2048]{1,0:T(8,128)(2,1)} %all-gather.10.cloned.1.call-done), kind=kOutput, calls=%fused_computation.24 | convolution fusion | flops 4311744512 | bytes 25165824 | tf_op jit(solution)/shard_map/dot_general | solution.py:32
  305.8 8.4 add_convert_fusion
  327.9 11.2 %multiply_convert_fusion.2 = (bf16[512,2048]{1,0:T(8,128)(2,1)S(1)}, bf16[512,2048]{1,0:T(8,128)(2,1)S(1)}, bf16[512,2048]{1,0:T(8,128)(2,1)}) fusion(f32[512,2048]{1,0:T(8,128)S(1)} %fusion.130, f32[512,2048]{1,0:T(8,128)S(1)} %fusion.128, bf16[512,2048]{1,0:T(8,128)(2,1)S(1)} %bitcast.430, bf16[2048,2048]{1,0:T(8,128)(2,1)} %all-gather.10.cloned.1.call-done), kind=kOutput, calls=%fused_computation.27 | convolution fusion | flops 4311744512 | bytes 25165824 | tf_op jit(solution)/shard_map/dot_general | solution.py:32
  339.1 8.5 fusion.131
  347.5 8.4 add_convert_fusion.1
  360.5 9.2 collective-permute-done.54
  426.0 10.0 %collective-permute-start.87 = (bf16[128,2048]{1,0:T(8,128)(2,1)S(1)}, bf16[128,2048]{1,0:T(8,128)(2,1)}, u32[]{:S(2)}, u32[]{:S(2)}) collective-permute-start(bf16[128,2048]{1,0:T(8,128)(2,1)S(1)} %get-tuple-element.81), channel_id=1, source_target_pairs={{0,1},{1,2},{2,3},{4,5},{5,6},{6,7},{8,9},{9,10},{10,11},{12,13},{... | collective-permute-start | bytes 1572872 | tf_op jit(solution)/shard_map/ppermute | solution.py:75
  440.5 7.4 collective-permute-start.60
  460.8 8.5 collective-permute-done.89
  482.5 9.2 collective-permute-done.90
  511.8 16.1 %attend_back.3 = (bf16[2,256,512]{2,1,0:T(8,128)(2,1)}, bf16[2,256,256]{2,1,0:T(8,128)(2,1)}, bf16[2,256,256]{2,1,0:T(8,128)(2,1)}, bf16[2,256,256]{2,1,0:T(8,128)(2,1)}, bf16[2,256,256]{2,1,0:T(8,128)(2,1)}) custom-call(s32[5]{0:T(128)} %stack.25.place_ref, bf16[2,256,512]{2,1,0:T(8,128)(2,1)} %bitcast.444, bf16[2,256,256]{2,1,0:T(8,128)(2,1)} %bitcast.453, ...), custom_call_target="tpu_custom_call" | custom-call | flops 10737418240 | bytes 3145728 | tf_op jit(solution)/shard_map/attend_back/pallas_call | solution.py:302
  532.7 16.6 %attend_back.2 = (bf16[2,256,512]{2,1,0:T(8,128)(2,1)}, bf16[2,256,256]{2,1,0:T(8,128)(2,1)}, bf16[2,256,256]{2,1,0:T(8,128)(2,1)}, bf16[2,256,256]{2,1,0:T(8,128)(2,1)}, bf16[2,256,256]{2,1,0:T(8,128)(2,1)}) custom-call(s32[5]{0:T(128)} %stack.25.place_ref, bf16[2,256,512]{2,1,0:T(8,128)(2,1)} %bitcast.441, bf16[2,256,256]{2,1,0:T(8,128)(2,1)} %bitcast.449, ...), custom_call_target="tpu_custom_call" | custom-call | flops 10737418240 | bytes 3145728 | tf_op jit(solution)/shard_map/attend_back/pallas_call | solution.py:302
  570.2 7.8 fusion.17
  578.0 14.3 %convolution_convert_fusion = bf16[2048,2048]{1,0:T(8,128)(2,1)} fusion(bf16[512,2048]{1,0:T(8,128)(2,1)} %copy-done.60, bf16[512,2048]{1,0:T(8,128)(2,1)} %copy-done.61, bf16[512,2048]{1,0:T(8,128)(2,1)} %bitcast.433, bf16[512,2048]{1,0:T(8,128)(2,1)} %bitcast.427), kind=kOutput, calls=%fused_computation.1 | convolution fusion | flops 8610906112 | bytes 16777216 | tf_op jit(solution)/shard_map/dot_general | solution.py:36
  592.4 14.1 %convolution_convert_fusion.1 = bf16[2048,2048]{1,0:T(8,128)(2,1)} fusion(bf16[512,2048]{1,0:T(8,128)(2,1)} %copy-done.62, bf16[512,2048]{1,0:T(8,128)(2,1)} %copy-done.63, bf16[512,2048]{1,0:T(8,128)(2,1)} %bitcast.434, bf16[512,2048]{1,0:T(8,128)(2,1)} %bitcast.428), kind=kOutput, calls=%fused_computation.2 | convolution fusion | flops 8610906112 | bytes 16777216 | tf_op jit(solution)/shard_map/dot_general | solution.py:36
  606.8 8.7 convolution_convert_fusion.6
  618.2 8.1 convolution_convert_fusion.4
  688.0 11.1 %convert_bitcast_fusion = bf16[2048,2048]{0,1:T(8,128)(2,1)} fusion(bf16[1024,2048]{1,0:T(8,128)(2,1)S(1)} %bitcast.418, bf16[512,2048]{1,0:T(8,128)(2,1)S(1)} %copy-done.65, bf16[512,2048]{1,0:T(8,128)(2,1)S(1)} %copy-done.66), kind=kOutput, calls=%fused_computation | convolution fusion | flops 8602517504 | bytes 16777216 | tf_op jit(solution)/shard_map/dot_general | solution.py:36
  699.2 16.9 %collective-permute-start.21 = (bf16[128,2048]{1,0:T(8,128)(2,1)}, bf16[128,2048]{1,0:T(8,128)(2,1)S(1)}, u32[]{:S(2)}, u32[]{:S(2)}) collective-permute-start(bf16[128,2048]{1,0:T(8,128)(2,1)} %get-tuple-element.84), channel_id=1, source_target_pairs={{0,1},{1,2},{2,3},{4,5},{5,6},{6,7},{8,9},{9,10},{10,11},{12,13},{... | collective-permute-start | bytes 1572872 | tf_op jit(solution)/shard_map/ppermute | solution.py:75
  780.7 13.6 %collective-permute-start.98 = (bf16[128,2048]{1,0:T(8,128)(2,1)S(1)}, bf16[128,2048]{1,0:T(8,128)(2,1)S(1)}, u32[]{:S(2)}, u32[]{:S(2)}) collective-permute-start(bf16[128,2048]{1,0:T(8,128)(2,1)S(1)} %get-tuple-element.114), channel_id=1, source_target_pairs={{0,1},{1,2},{2,3},{4,5},{5,6},{6,7},{8,9},{9,10},{10,11},{12,13},{... | collective-permute-start | bytes 1572872 | tf_op jit(solution)/shard_map/ppermute | solution.py:61
  821.1 7.8 collective-permute-start.75
  852.9 8.5 collective-permute-done.77
  865.2 43.9 %psum.7 = f32[2,2048]{1,0:T(2,128)S(1)} all-reduce(f32[2,2048]{1,0:T(2,128)S(1)} %pad_maximum_fusion.5), channel_id=1, replica_groups=mesh['fsdp'=2,'heads'=4,'tensor'=4] {'fsdp','heads','tensor'}, use_global_device_ids=true, to_apply=%region_18.19 | all-reduce | flops 4096 | bytes 32768 | tf_op jit(solution)/shard_map/psum | solution.py:501
  918.3 8.9 collective-permute-done.105
  (530 shorter events, 551.9 us)
Async XLA Ops:
  7.2 40.8 %all-gather.6.cloned.1.call-start = ((), (), s32[]{:S(2)}) async-start(), calls=%async_computation.5 | async-start | bytes 4128768 | tf_op jit(solution)/shard_map/all_gather | solution.py:380
  10.7 81.5 %all-gather.8.cloned.1.call-start = ((), (), s32[]{:S(2)}) async-start(), calls=%async_computation.6 | async-start | bytes 2359296 | tf_op jit(solution)/shard_map/all_gather | solution.py:380
  11.4 254.3 %all-gather.12.cloned.1.call-start = ((), (), s32[]{:S(2)}) async-start(), calls=%async_computation.8 | async-start | bytes 9437184 | tf_op jit(solution)/shard_map/all_gather | solution.py:380
  12.2 264.1 %all-gather.14.cloned.1.call-start = ((), (), s32[]{:S(2)}) async-start(), calls=%async_computation.9 | async-start | bytes 9437184 | tf_op jit(solution)/shard_map/all_gather | solution.py:380
  12.7 274.0 %all-gather.10.cloned.1.call-start = ((), (), s32[]{:S(2)}) async-start(), calls=%async_computation.7 | async-start | bytes 9437184 | tf_op jit(solution)/shard_map/all_gather | solution.py:380
  13.3 896.4 %reduce-scatter.8.cloned.1.call-start = ((), (), s32[]{:S(2)}) async-start(), calls=%async_computation.11 | async-start | bytes 2359296 | tf_op jit(solution)/shard_map/reduce_scatter | solution.py:464
  65.5 34.3 %collective-permute-start.27 = (bf16[2,256,256]{2,1,0:T(8,128)(2,1)}, bf16[2,256,256]{2,1,0:T(8,128)(2,1)}, u32[]{:S(2)}, u32[]{:S(2)}) collective-permute-start(bf16[2,256,256]{2,1,0:T(8,128)(2,1)} %bitcast.451), channel_id=1, source_target_pairs={{0,4},{4,0},{8,12},{12,8},{1,5},{5,1},{9,13},{13,9},{2,6},{6,2},{1... | collective-permute-start | bytes 786440 | tf_op jit(solution)/shard_map/ppermute | solution.py:422
  182.1 26.9 %collective-permute-start.10 = (bf16[128,2048]{1,0:T(8,128)(2,1)S(1)}, bf16[128,2048]{1,0:T(8,128)(2,1)S(1)}, u32[]{:S(2)}, u32[]{:S(2)}) collective-permute-start(bf16[128,2048]{1,0:T(8,128)(2,1)S(1)} %get-tuple-element.86), channel_id=1, source_target_pairs={{3,2},{2,1},{1,0},{7,6},{6,5},{5,4},{11,10},{10,9},{9,8},{15,14},{... | collective-permute-start | bytes 1572872 | tf_op jit(solution)/shard_map/ppermute | solution.py:76
  314.4 43.9 %collective-permute-start.81 = (bf16[128,2048]{1,0:T(8,128)(2,1)S(1)}, bf16[128,2048]{1,0:T(8,128)(2,1)S(1)}, u32[]{:S(2)}, u32[]{:S(2)}) collective-permute-start(bf16[128,2048]{1,0:T(8,128)(2,1)S(1)} %get-tuple-element.121), channel_id=1, source_target_pairs={{0,1},{4,5},{8,9},{12,13},{16,17},{20,21},{24,25},{28,29}} | collective-permute-start | bytes 1572872 | tf_op jit(solution)/shard_map/ppermute | solution.py:61
  450.0 26.0 %collective-permute-start.91 = (bf16[128,2048]{1,0:T(8,128)(2,1)}, bf16[128,2048]{1,0:T(8,128)(2,1)}, u32[]{:S(2)}, u32[]{:S(2)}) collective-permute-start(bf16[128,2048]{1,0:T(8,128)(2,1)} %collective-permute-done.87), channel_id=1, source_target_pairs={{1,2},{2,3},{5,6},{6,7},{9,10},{10,11},{13,14},{14,15},{17,18},{18... | collective-permute-start | bytes 1572872 | tf_op jit(solution)/shard_map/ppermute | solution.py:75
  476.0 24.5 %collective-permute-start.92 = (bf16[128,2048]{1,0:T(8,128)(2,1)}, bf16[128,2048]{1,0:T(8,128)(2,1)S(1)}, u32[]{:S(2)}, u32[]{:S(2)}) collective-permute-start(bf16[128,2048]{1,0:T(8,128)(2,1)} %collective-permute-done.91), channel_id=1, source_target_pairs={{2,3},{6,7},{10,11},{14,15},{18,19},{22,23},{26,27},{30,31}} | collective-permute-start | bytes 1572872 | tf_op jit(solution)/shard_map/ppermute | solution.py:75
  507.3 425.6 %reduce-scatter.6.cloned.1.call-start = ((), (), s32[]{:S(2)}) async-start(), calls=%async_computation.10 | async-start | bytes 3538944 | tf_op jit(solution)/shard_map/reduce_scatter | solution.py:464
  578.0 358.3 %reduce-scatter.12.cloned.1.call-start = ((), (), s32[]{:S(2)}) async-start(), calls=%async_computation.13 | async-start | bytes 9437184 | tf_op jit(solution)/shard_map/reduce_scatter | solution.py:464
  592.4 346.7 %reduce-scatter.10.cloned.1.call-start = ((), (), s32[]{:S(2)}) async-start(), calls=%async_computation.12 | async-start | bytes 9437184 | tf_op jit(solution)/shard_map/reduce_scatter | solution.py:464
  606.6 335.2 %reduce-scatter.14.cloned.1.call-start = ((), (), s32[]{:S(2)}) async-start(), calls=%async_computation.14 | async-start | bytes 9437184 | tf_op jit(solution)/shard_map/reduce_scatter | solution.py:464
  633.7 26.6 %collective-permute-start.45 = (bf16[128,2048]{1,0:T(8,128)(2,1)}, bf16[128,2048]{1,0:T(8,128)(2,1)}, u32[]{:S(2)}, u32[]{:S(2)}) collective-permute-start(bf16[128,2048]{1,0:T(8,128)(2,1)} %get-tuple-element.134), channel_id=1, source_target_pairs={{3,2},{7,6},{11,10},{15,14},{19,18},{23,22},{27,26},{31,30}} | collective-permute-start | bytes 1572872 | tf_op jit(solution)/shard_map/ppermute | solution.py:62
  655.8 24.6 %collective-permute-start.17 = (bf16[128,2048]{1,0:T(8,128)(2,1)}, bf16[128,2048]{1,0:T(8,128)(2,1)S(1)}, u32[]{:S(2)}, u32[]{:S(2)}) collective-permute-start(bf16[128,2048]{1,0:T(8,128)(2,1)} %get-tuple-element.123), channel_id=1, source_target_pairs={{0,1},{1,2},{2,3},{4,5},{5,6},{6,7},{8,9},{9,10},{10,11},{12,13},{... | collective-permute-start | bytes 1572872 | tf_op jit(solution)/shard_map/ppermute | solution.py:61
  670.4 45.6 %collective-permute-start.44 = (bf16[128,2048]{1,0:T(8,128)(2,1)}, bf16[128,2048]{1,0:T(8,128)(2,1)}, u32[]{:S(2)}, u32[]{:S(2)}) collective-permute-start(bf16[128,2048]{1,0:T(8,128)(2,1)} %get-tuple-element.131), channel_id=1, source_target_pairs={{0,1},{1,2},{2,3},{4,5},{5,6},{6,7},{8,9},{9,10},{10,11},{12,13},{... | collective-permute-start | bytes 1572872 | tf_op jit(solution)/shard_map/ppermute | solution.py:61
  679.2 36.9 %collective-permute-start.47 = (bf16[128,2048]{1,0:T(8,128)(2,1)}, bf16[128,2048]{1,0:T(8,128)(2,1)}, u32[]{:S(2)}, u32[]{:S(2)}) collective-permute-start(bf16[128,2048]{1,0:T(8,128)(2,1)} %fusion.73), channel_id=1, source_target_pairs={{3,2},{2,1},{1,0},{7,6},{6,5},{5,4},{11,10},{10,9},{9,8},{15,14},{... | collective-permute-start | bytes 1572872 | tf_op jit(solution)/shard_map/ppermute | solution.py:62
  686.3 33.7 %collective-permute-start.22 = (bf16[128,2048]{1,0:T(8,128)(2,1)}, bf16[128,2048]{1,0:T(8,128)(2,1)}, u32[]{:S(2)}, u32[]{:S(2)}) collective-permute-start(bf16[128,2048]{1,0:T(8,128)(2,1)} %get-tuple-element.84), channel_id=1, source_target_pairs={{3,2},{2,1},{1,0},{7,6},{6,5},{5,4},{11,10},{10,9},{9,8},{15,14},{... | collective-permute-start | bytes 1572872 | tf_op jit(solution)/shard_map/ppermute | solution.py:76
  699.2 45.8 %collective-permute-start.21 = (bf16[128,2048]{1,0:T(8,128)(2,1)}, bf16[128,2048]{1,0:T(8,128)(2,1)S(1)}, u32[]{:S(2)}, u32[]{:S(2)}) collective-permute-start(bf16[128,2048]{1,0:T(8,128)(2,1)} %get-tuple-element.84), channel_id=1, source_target_pairs={{0,1},{1,2},{2,3},{4,5},{5,6},{6,7},{8,9},{9,10},{10,11},{12,13},{... | collective-permute-start | bytes 1572872 | tf_op jit(solution)/shard_map/ppermute | solution.py:75
  732.4 31.2 %collective-permute-start.48 = (bf16[128,2048]{1,0:T(8,128)(2,1)S(1)}, bf16[128,2048]{1,0:T(8,128)(2,1)S(1)}, u32[]{:S(2)}, u32[]{:S(2)}) collective-permute-start(bf16[128,2048]{1,0:T(8,128)(2,1)S(1)} %get-tuple-element.90), channel_id=1, source_target_pairs={{0,1},{1,2},{2,3},{4,5},{5,6},{6,7},{8,9},{9,10},{10,11},{12,13},{... | collective-permute-start | bytes 1572872 | tf_op jit(solution)/shard_map/ppermute | solution.py:75
  742.2 26.6 %collective-permute-start.50 = (bf16[128,2048]{1,0:T(8,128)(2,1)S(1)}, bf16[128,2048]{1,0:T(8,128)(2,1)S(1)}, u32[]{:S(2)}, u32[]{:S(2)}) collective-permute-start(bf16[128,2048]{1,0:T(8,128)(2,1)S(1)} %collective-permute-done.49), channel_id=1, source_target_pairs={{2,1},{1,0},{6,5},{5,4},{10,9},{9,8},{14,13},{13,12},{18,17},{17,1... | collective-permute-start | bytes 1572872 | tf_op jit(solution)/shard_map/ppermute | solution.py:76
  744.9 24.6 %collective-permute-start.99 = (bf16[128,2048]{1,0:T(8,128)(2,1)S(1)}, bf16[128,2048]{1,0:T(8,128)(2,1)S(1)}, u32[]{:S(2)}, u32[]{:S(2)}) collective-permute-start(bf16[128,2048]{1,0:T(8,128)(2,1)S(1)} %get-tuple-element.117), channel_id=1, source_target_pairs={{3,2},{7,6},{11,10},{15,14},{19,18},{23,22},{27,26},{31,30}} | collective-permute-start | bytes 1572872 | tf_op jit(solution)/shard_map/ppermute | solution.py:62
  769.6 32.5 %collective-permute-start.52 = (bf16[128,2048]{1,0:T(8,128)(2,1)S(1)}, bf16[128,2048]{1,0:T(8,128)(2,1)S(1)}, u32[]{:S(2)}, u32[]{:S(2)}) collective-permute-start(bf16[128,2048]{1,0:T(8,128)(2,1)S(1)} %collective-permute-done.48), channel_id=1, source_target_pairs={{1,2},{2,3},{5,6},{6,7},{9,10},{10,11},{13,14},{14,15},{17,18},{18... | collective-permute-start | bytes 1572872 | tf_op jit(solution)/shard_map/ppermute | solution.py:75
  773.4 27.1 %collective-permute-start.51 = (bf16[128,2048]{1,0:T(8,128)(2,1)S(1)}, bf16[128,2048]{1,0:T(8,128)(2,1)S(1)}, u32[]{:S(2)}, u32[]{:S(2)}) collective-permute-start(bf16[128,2048]{1,0:T(8,128)(2,1)S(1)} %collective-permute-done.50), channel_id=1, source_target_pairs={{1,0},{5,4},{9,8},{13,12},{17,16},{21,20},{25,24},{29,28}} | collective-permute-start | bytes 1572872 | tf_op jit(solution)/shard_map/ppermute | solution.py:76
  802.0 30.2 %collective-permute-start.26 = (bf16[128,2048]{1,0:T(8,128)(2,1)S(1)}, bf16[128,2048]{1,0:T(8,128)(2,1)S(1)}, u32[]{:S(2)}, u32[]{:S(2)}) collective-permute-start(bf16[128,2048]{1,0:T(8,128)(2,1)S(1)} %collective-permute-done.25), channel_id=1, source_target_pairs={{2,3},{6,7},{10,11},{14,15},{18,19},{22,23},{26,27},{30,31}} | collective-permute-start | bytes 1572872 | tf_op jit(solution)/shard_map/ppermute | solution.py:75
  803.1 38.3 %collective-permute-start.53 = (bf16[128,2048]{1,0:T(8,128)(2,1)S(1)}, bf16[128,2048]{1,0:T(8,128)(2,1)S(1)}, u32[]{:S(2)}, u32[]{:S(2)}) collective-permute-start(bf16[128,2048]{1,0:T(8,128)(2,1)S(1)} %collective-permute-done.52), channel_id=1, source_target_pairs={{2,3},{6,7},{10,11},{14,15},{18,19},{22,23},{26,27},{30,31}} | collective-permute-start | bytes 1572872 | tf_op jit(solution)/shard_map/ppermute | solution.py:75
  841.6 70.0 %collective-permute-start.79 = (bf16[128,2048]{1,0:T(8,128)(2,1)}, bf16[128,2048]{1,0:T(8,128)(2,1)}, u32[]{:S(2)}, u32[]{:S(2)}) collective-permute-start(bf16[128,2048]{1,0:T(8,128)(2,1)} %collective-permute-done.75), channel_id=1, source_target_pairs={{1,2},{2,3},{5,6},{6,7},{9,10},{10,11},{13,14},{14,15},{17,18},{18... | collective-permute-start | bytes 1572872 | tf_op jit(solution)/shard_map/ppermute | solution.py:75
  850.1 62.1 %collective-permute-start.104 = (bf16[128,2048]{1,0:T(8,128)(2,1)S(1)}, bf16[128,2048]{1,0:T(8,128)(2,1)}, u32[]{:S(2)}, u32[]{:S(2)}) collective-permute-start(bf16[128,2048]{1,0:T(8,128)(2,1)S(1)} %collective-permute-done.103), channel_id=1, source_target_pairs={{2,1},{1,0},{6,5},{5,4},{10,9},{9,8},{14,13},{13,12},{18,17},{17,1... | collective-permute-start | bytes 1572872 | tf_op jit(solution)/shard_map/ppermute | solution.py:76
  851.4 62.1 %collective-permute-start.106 = (bf16[128,2048]{1,0:T(8,128)(2,1)S(1)}, bf16[128,2048]{1,0:T(8,128)(2,1)}, u32[]{:S(2)}, u32[]{:S(2)}) collective-permute-start(bf16[128,2048]{1,0:T(8,128)(2,1)S(1)} %collective-permute-done.102), channel_id=1, source_target_pairs={{1,2},{2,3},{5,6},{6,7},{9,10},{10,11},{13,14},{14,15},{17,18},{18... | collective-permute-start | bytes 1572872 | tf_op jit(solution)/shard_map/ppermute | solution.py:75
  861.5 52.8 %collective-permute-start.78 = (bf16[128,2048]{1,0:T(8,128)(2,1)}, bf16[128,2048]{1,0:T(8,128)(2,1)}, u32[]{:S(2)}, u32[]{:S(2)}) collective-permute-start(bf16[128,2048]{1,0:T(8,128)(2,1)} %collective-permute-done.77), channel_id=1, source_target_pairs={{1,0},{5,4},{9,8},{13,12},{17,16},{21,20},{25,24},{29,28}} | collective-permute-start | bytes 1572872 | tf_op jit(solution)/shard_map/ppermute | solution.py:76
  (155 other events, 2417.6 us)
Sparse Core Ops, SparseCore 0:
  10.8 37.0 all-gather.5
  49.8 31.4 all-gather.7
  83.2 54.2 all-gather.11
  139.2 54.2 all-gather.13
  195.2 54.2 all-gather.9
  507.4 42.1 reduce-scatter.7
  578.1 46.7 reduce-scatter.5
  628.3 71.4 reduce-scatter.11
  703.3 71.4 reduce-scatter.9
  778.2 71.2 reduce-scatter.13

commit v2 on v1

--- a/solution.py
+++ b/solution.py
@@ -44,45 +44,107 @@
     )
 
 
-def line_sum(parts):
-    count = parts.shape[0]
-    me = lax.axis_index("tensor")
-
-    def pick(j):
-        return lax.dynamic_index_in_dim(parts, jnp.clip(j, 0, count - 1), 0, keepdims=False)
-
-    from_left = from_right = None
-    for t in range(1, count):
-        to_right = pick(count - t + me)
-        to_left = pick(t + me - count)
-        if from_left is not None:
-            to_right = (to_right.astype(F32) + from_left.astype(F32)).astype(BF)
-            to_left = (to_left.astype(F32) + from_right.astype(F32)).astype(BF)
-        from_left = lax.ppermute(to_right, "tensor", [(k, k + 1) for k in range(t)])
-        from_right = lax.ppermute(
-            to_left, "tensor", [(count - 1 - k, count - 2 - k) for k in range(t)]
-        )
-    return pick(me).astype(F32) + from_left.astype(F32) + from_right.astype(F32)
-
-
-def line_gather(own):
-    count = lax.axis_size("tensor")
-    me = lax.axis_index("tensor")
-    from_left = [None] * count
-    from_right = [None] * count
-    right = left = own
-    for t in range(1, count):
-        right = lax.ppermute(right, "tensor", [(k, k + 1) for k in range(t - 1, count - 1)])
-        left = lax.ppermute(
-            left, "tensor", [(count - 1 - k, count - 2 - k) for k in range(t - 1, count - 1)]
-        )
-        from_left[t], from_right[t] = right, left
-    out = jnp.zeros((count,) + own.shape, own.dtype)
-    out = lax.dynamic_update_index_in_dim(out, own, me, 0)
-    for t in range(1, count):
-        block = jnp.where(me >= t, from_left[t], from_right[count - t])
-        out = lax.dynamic_update_index_in_dim(out, block, lax.rem(me - t + count, count), 0)
-    return out
+class LineSum:
+    def __init__(self, parts):
+        self.parts = parts
+        self.step = 1
+        self.from_left = self.from_right = None
+
+    def pick(self, j):
+        last = self.parts.shape[0] - 1
+        return lax.dynamic_index_in_dim(self.parts, jnp.clip(j, 0, last), 0, keepdims=False)
+
+    def sends(self):
+        count, t = self.parts.shape[0], self.step
+        me = lax.axis_index("tensor")
+        to_right = self.pick(count - t + me)
+        to_left = self.pick(t + me - count)
+        if self.from_left is not None:
+            to_right = (to_right.astype(F32) + self.from_left.astype(F32)).astype(BF)
+            to_left = (to_left.astype(F32) + self.from_right.astype(F32)).astype(BF)
+        return [
+            (to_right, "tensor", [(k, k + 1) for k in range(t)]),
+            (to_left, "tensor", [(count - 1 - k, count - 2 - k) for k in range(t)]),
+        ]
+
+    def take(self, moved):
+        self.from_left, self.from_right = moved
+        self.step += 1
+
+    def result(self):
+        own = self.pick(lax.axis_index("tensor"))
+        return own.astype(F32) + self.from_left.astype(F32) + self.from_right.astype(F32)
+
+
+class LineGather:
+    def __init__(self, own):
+        self.own = self.right = self.left = own
+        self.step = 1
+        self.from_left, self.from_right = {}, {}
+
+    def sends(self):
+        count, t = lax.axis_size("tensor"), self.step
+        steps = range(t - 1, count - 1)
+        return [
+            (self.right, "tensor", [(k, k + 1) for k in steps]),
+            (self.left, "tensor", [(count - 1 - k, count - 2 - k) for k in steps]),
+        ]
+
+    def take(self, moved):
+        self.right, self.left = moved
+        self.from_left[self.step], self.from_right[self.step] = moved
+        self.step += 1
+
+    def result(self):
+        count, me = lax.axis_size("tensor"), lax.axis_index("tensor")
+        out = jnp.zeros((count,) + self.own.shape, self.own.dtype)
+        out = lax.dynamic_update_index_in_dim(out, self.own, me, 0)
+        for t in range(1, count):
+            block = jnp.where(me >= t, self.from_left[t], self.from_right[count - t])
+            out = lax.dynamic_update_index_in_dim(out, block, lax.rem(me - t + count, count), 0)
+        return out
+
+
+class Butterfly:
+    def __init__(self, value, axes):
+        self.value = value
+        self.moves = []
+        for axis in axes:
+            bit = 1
+            while bit < lax.axis_size(axis):
+                self.moves.append((axis, pairs(lax.axis_size(axis), bit)))
+                bit *= 2
+
+    def sends(self):
+        axis, pattern = self.moves.pop(0)
+        return [(self.value, axis, pattern)]
+
+    def take(self, moved):
+        self.value = self.value + moved[0]
+
+
+class Clock:
+    def __init__(self):
+        self.last = ()
+
+    def expect(self, value):
+        self.last += (value,)
+
+    def slot(self, tasks, work=None, args=()):
+        sends = [task.sends() for task in tasks]
+        flat = [send for group in sends for send in group]
+        before = len(self.last)
+        gated = lax.optimization_barrier(
+            tuple(self.last) + tuple(s[0] for s in flat) + tuple(args)
+        )[before:]
+        moved = [lax.ppermute(g, s[1], s[2]) for g, s in zip(gated, flat)]
+        done = tuple(work(*gated[len(flat) :])) if work else ()
+        self.last = tuple(moved) + done
+        at = 0
+        for task, group in zip(tasks, sends):
+            task.take(moved[at : at + len(group)])
+            at += len(group)
+        return done
 
 
 def pairs(count, bit):
@@ -406,12 +468,16 @@
     def own(x):
         return lax.dynamic_slice_in_dim(x, me * own_rows, own_rows, 0)
 
+    def blocks(x):
+        return x.reshape(ways, own_rows, width)
+
     state = []
     for c in range(CHUNKS):
         s = {}
         tok = chunk_of(tokens, c).reshape(rows, width)
         tok_f = tok.astype(F32)
         s["tok"] = tok
+        s["cot"] = chunk_of(cotangent, c).reshape(rows, width)
         s["normed_one"] = (tok_f * inverse_rms(tok_f) * gain_one).astype(BF)
         s["cos"] = lax.slice_in_dim(cosine, c * rows, (c + 1) * rows, axis=0)
         s["sin"] = lax.slice_in_dim(sine, c * rows, (c + 1) * rows, axis=0)
@@ -425,57 +491,51 @@
         s["q"] = turn_call(
             dot_plain(s["normed_one"], full_qkv[:, :q_width]), s["cos"], s["sin"], q_width
         ).reshape(per_chunk, block, q_width)
+        seg_q, seg_k = chunk_of(seg_here, c), chunk_of(segments, c)
+        s["seg_fwd"] = (seg_q[:, :, None], seg_k[:, None, :])
+        s["seg_back"] = (seg_q[:, None, :], seg_k[:, :, None])
         state.append(s)
-    for c, s in enumerate(state):
-        seg_q = chunk_of(seg_here, c)
-        seg_k = chunk_of(segments, c)
-        s["attended"], s["lse"] = attend_call(
-            place, s["q"], s["kv"], seg_q[:, :, None], seg_k[:, None, :]
+    first, second = state
+
+    def attend(s, q):
+        attended, lse = attend_call(place, q, s["kv"], *s["seg_fwd"])
+        s["attended"], s["lse"] = attended, lse
+        attn = dot_cols(attended.reshape(rows, q_width), full_o).astype(BF)
+        return attended, lse, attn
+
+    def enter_ffn(s, summed):
+        s["residual"] = own(s["tok"]).astype(F32) + summed
+        return (s["residual"] * inverse_rms(s["residual"]) * gain_two).astype(BF)
+
+    def ffn_up(normed_two):
+        return dot_plain(normed_two, full_g), dot_plain(normed_two, full_u)
+
+    def ffn_mid(gate, up, cot):
+        sig = jax.nn.sigmoid(gate)
+        hidden = (gate * sig * up).astype(BF)
+        d_hidden = dot_plain(cot, full_d)
+        d_gate = (d_hidden * up * (sig * (1.0 + gate * (1.0 - sig)))).astype(BF)
+        d_up = (d_hidden * gate * sig).astype(BF)
+        return hidden, d_gate, d_up
+
+    def ffn_back(d_gate, d_up):
+        return ((dot_cols(d_gate, full_g) + dot_cols(d_up, full_u)).astype(BF),)
+
+    def ffn_out(hidden):
+        return (dot_cols(hidden, full_d).astype(BF),)
+
+    def leave_ffn(s, summed):
+        d_norm, s["gain_two"] = norm_back(s["residual"], gain_two, summed)
+        s["d_resid"] = own(s["cot"]).astype(F32) + d_norm
+        return s["d_resid"].astype(BF)
+
+    def attend_back(s, d_attn):
+        d_attended = dot_plain(d_attn, full_o).astype(BF).reshape(per_chunk, block, q_width)
+        return attend_back_call(
+            place, s["q"], s["kv"], *s["seg_back"], s["attended"], d_attended, s["lse"]
         )
-        s["seg"] = (seg_q[:, None, :], seg_k[:, :, None])
-        attn = dot_cols(s["attended"].reshape(rows, q_width), full_o).astype(BF)
-        s["residual"] = own(s["tok"]).astype(F32) + line_sum(
-            attn.reshape(ways, own_rows, width)
-        )
-        normed_two = (s["residual"] * inverse_rms(s["residual"]) * gain_two).astype(BF)
-        s["normed_two"] = line_gather(normed_two).reshape(rows, width)
-    for c, s in enumerate(state):
-        cot = chunk_of(cotangent, c).reshape(rows, width)
-        gate = dot_plain(s["normed_two"], full_g)
-        up = dot_plain(s["normed_two"], full_u)
-        sig = jax.nn.sigmoid(gate)
-        s["hidden"] = (gate * sig * up).astype(BF)
-        d_hidden = dot_plain(cot, full_d)
-        s["d_gate"] = (d_hidden * up * (sig * (1.0 + gate * (1.0 - sig)))).astype(BF)
-        s["d_up"] = (d_hidden * gate * sig).astype(BF)
-        back = (dot_cols(s["d_gate"], full_g) + dot_cols(s["d_up"], full_u)).astype(BF)
-        d_normed_two = line_sum(back.reshape(ways, own_rows, width))
-        d_norm, s["gain_two"] = norm_back(s["residual"], gain_two, d_normed_two)
-        s["d_resid"] = own(cot).astype(F32) + d_norm
-        s["d_attn"] = line_gather(s["d_resid"].astype(BF)).reshape(rows, width)
-        ffn = dot_cols(s["hidden"], full_d).astype(BF)
-        out = s["residual"] + line_sum(ffn.reshape(ways, own_rows, width))
-        s["output"] = line_gather(out.astype(BF)).reshape(per_chunk, block, width)
-
-    def joined(name):
-        return jnp.concatenate([s[name] for s in state], axis=0)
-
-    def scattered(grad):
-        return lax.psum_scatter(
-            grad.astype(BF), owners, scatter_dimension=0, tiled=True
-        ).astype(F32)
-
-    cot_rows = cotangent.reshape(seqs * block, width)
-    n_two = joined("normed_two")
-    down_grad = scattered(dot_rows(cot_rows, joined("hidden")))
-    gate_grad = scattered(dot_rows(n_two, joined("d_gate")))
-    up_grad = scattered(dot_rows(n_two, joined("d_up")))
-
-    for c, s in enumerate(state):
-        d_attended = dot_plain(s["d_attn"], full_o).astype(BF).reshape(per_chunk, block, q_width)
-        dq, b0, b1, b2, b3 = attend_back_call(
-            place, s["q"], s["kv"], s["seg"][0], s["seg"][1], s["attended"], d_attended, s["lse"]
-        )
+
+    def project_back(s, dq, b0, b1, b2, b3):
         from3 = lax.ppermute(b3, "heads", pairs(parts, 1))
         from1 = lax.ppermute(b1, "heads", pairs(parts, 1))
         far = (b2.astype(F32) + from3.astype(F32)).astype(BF)
@@ -483,37 +543,151 @@
         d_kv = b0.astype(F32) + from1.astype(F32) + from2.astype(F32)
         d_q = turn_call(dq.reshape(rows, q_width), s["cos"], -s["sin"], q_width)
         d_kv = turn_call(d_kv.reshape(rows, kv_width), s["cos"], -s["sin"], k_width)
-        s["d_qkv"] = jnp.concatenate([d_q, d_kv], axis=1)
-        back = dot_cols(s["d_qkv"], full_qkv).astype(BF)
-        d_normed_one = line_sum(back.reshape(ways, own_rows, width))
-        d_norm, s["gain_one"] = norm_back(own(s["tok"]).astype(F32), gain_one, d_normed_one)
-        s["input_grad"] = (
-            line_gather((s["d_resid"] + d_norm).astype(BF))
-            .astype(F32)
-            .reshape(per_chunk, block, width)
-        )
-    attended = joined("attended").reshape(seqs * block, q_width)
-    o_grad = scattered(dot_rows(joined("d_attn"), attended))
-    qkv_grad = scattered(dot_rows(joined("normed_one"), joined("d_qkv")))
-    gain_grads = jnp.stack(
-        [sum(s["gain_one"] for s in state), sum(s["gain_two"] for s in state)]
-    )
-    gain_grads = lax.psum(gain_grads, ("fsdp", "heads", "tensor"))
+        d_qkv = jnp.concatenate([d_q, d_kv], axis=1)
+        return d_qkv, dot_cols(d_qkv, full_qkv).astype(BF)
+
+    def leave_attention(s, summed):
+        d_norm, s["gain_one"] = norm_back(own(s["tok"]).astype(F32), gain_one, summed)
+        return (s["d_resid"] + d_norm).astype(BF)
+
+    def scattered(grad):
+        return lax.psum_scatter(grad, owners, scatter_dimension=0, tiled=True)
+
+    def weight_grad(*halves):
+        left = jnp.concatenate(halves[:CHUNKS], axis=0)
+        right = jnp.concatenate(halves[CHUNKS:], axis=0)
+        return (dot_rows(left, right).astype(BF),)
+
+    def of_both(*names):
+        return tuple(s[name] for name in names for s in state)
+
+    axes = ("tensor", "heads", "fsdp")
+    clock = Clock()
+    slot = clock.slot
+
+    _, _, attn = attend(first, first["q"])
+    sum_a0 = LineSum(blocks(attn))
+    second["attended"], second["lse"], attn = slot(
+        [sum_a0], functools.partial(attend, second), (second["q"],)
+    )
+    sum_a1 = LineSum(blocks(attn))
+    slot([sum_a0])
+    slot([sum_a0])
+    gather_a0 = LineGather(enter_ffn(first, sum_a0.result()))
+    slot([gather_a0])
+    slot([gather_a0, sum_a1])
+    slot([gather_a0, sum_a1])
+    first["normed_two"] = gather_a0.result().reshape(rows, width)
+    gate, up = slot([sum_a1], ffn_up, (first["normed_two"],))
+    gather_a1 = LineGather(enter_ffn(second, sum_a1.result()))
+    first["hidden"], first["d_gate"], first["d_up"] = slot(
+        [gather_a1], ffn_mid, (gate, up, first["cot"])
+    )
+    (back,) = slot([gather_a1], ffn_back, (first["d_gate"], first["d_up"]))
+    sum_d0 = LineSum(blocks(back))
+    (ffn,) = slot([gather_a1, sum_d0], ffn_out, (first["hidden"],))
+    sum_f0 = LineSum(blocks(ffn))
+    second["normed_two"] = gather_a1.result().reshape(rows, width)
+    gate, up = slot([sum_d0], ffn_up, (second["normed_two"],))
+    second["hidden"], second["d_gate"], second["d_up"] = slot(
+        [sum_d0], ffn_mid, (gate, up, second["cot"])
+    )
+    gather_d0 = LineGather(leave_ffn(first, sum_d0.result()))
+    (back,) = slot([gather_d0], ffn_back, (second["d_gate"], second["d_up"]))
+    sum_d1 = LineSum(blocks(back))
+    (grad,) = slot(
+        [gather_d0, sum_d1],
+        weight_grad,
+        of_both("cot", "hidden"),
+    )
+    down_grad = scattered(grad)
+    (grad,) = slot([gather_d0, sum_d1], weight_grad, of_both("normed_two", "d_gate"))
+    gate_grad = scattered(grad)
+    first["d_attn"] = gather_d0.result().reshape(rows, width)
+    (grad,) = slot([sum_d1], weight_grad, of_both("normed_two", "d_up"))
+    up_grad = scattered(grad)
+    gather_d1 = LineGather(leave_ffn(second, sum_d1.result()))
+    gains_two = Butterfly(first["gain_two"] + second["gain_two"], axes)
+    pieces = slot(
+        [gather_d1, gains_two], functools.partial(attend_back, first), (first["d_attn"],)
+    )
+    first["d_qkv"], back = slot(
+        [gather_d1, sum_f0, gains_two], functools.partial(project_back, first), pieces
+    )
+    sum_n0 = LineSum(blocks(back))
+    (ffn,) = slot([gather_d1, sum_f0, gains_two], ffn_out, (second["hidden"],))
+    sum_f1 = LineSum(blocks(ffn))
+    second["d_attn"] = gather_d1.result().reshape(rows, width)
+    pieces = slot(
+        [sum_f0, gains_two], functools.partial(attend_back, second), (second["d_attn"],)
+    )
+    clock.expect(down_grad)
+    gather_f0 = LineGather((first["residual"] + sum_f0.result()).astype(BF))
+    second["d_qkv"], back = slot(
+        [gather_f0, gains_two], functools.partial(project_back, second), pieces
+    )
+    sum_n1 = LineSum(blocks(back))
+    (grad,) = slot(
+        [gather_f0, sum_n0], weight_grad, of_both("normed_one", "d_qkv")
+    )
+    qkv_grad = scattered(grad)
+    for s in state:
+        s["attended_rows"] = s["attended"].reshape(rows, q_width)
+    (grad,) = slot([gather_f0, sum_n0], weight_grad, of_both("d_attn", "attended_rows"))
+    o_grad = scattered(grad)
+    first["output"] = gather_f0.result()
+    slot([sum_n0])
+    gather_n0 = LineGather(leave_attention(first, sum_n0.result()))
+    slot([gather_n0])
+    slot([gather_n0, sum_n1])
+    slot([gather_n0, sum_n1])
+    first["input_grad"] = gather_n0.result()
+    clock.expect(gate_grad)
+    slot([sum_n1])
+    gather_n1 = LineGather(leave_attention(second, sum_n1.result()))
+    gains_one = Butterfly(first["gain_one"] + second["gain_one"], axes)
+    slot([gather_n1, gains_one])
+    slot([gather_n1, sum_f1, gains_one])
+    slot([gather_n1, sum_f1, gains_one])
+    second["input_grad"] = gather_n1.result()
+    slot([sum_f1, gains_one])
+    clock.expect(up_grad)
+    gather_f1 = LineGather((second["residual"] + sum_f1.result()).astype(BF))
+    slot([gather_f1, gains_one])
+    slot([gather_f1])
+    slot([gather_f1])
+    second["output"] = gather_f1.result()
+    while gains_one.moves:
+        slot([gains_one])
+    while gains_two.moves:
+        slot([gains_two])
+
+    qkv_grad, o_grad, down_grad, gate_grad, up_grad = (
+        g.astype(F32) for g in (qkv_grad, o_grad, down_grad, gate_grad, up_grad)
+    )
     share = attn_gain.shape[0]
     index = lax.axis_index("fsdp") * parts + here
-    gain_grads = lax.dynamic_slice_in_dim(gain_grads, index * share, share, 1)
+
+    def owned(gain):
+        return lax.dynamic_slice_in_dim(gain, index * share, share, 0)
+
+    def whole(name):
+        return jnp.concatenate(
+            [s[name].reshape(per_chunk, block, width) for s in state], axis=0
+        )
+
     return (
-        joined("output"),
-        joined("input_grad"),
+        whole("output"),
+        whole("input_grad").astype(F32),
         qkv_grad[:, :q_width],
         qkv_grad[:, q_width : q_width + k_width],
         qkv_grad[:, q_width + k_width :],
         o_grad,
-        gain_grads[0],
+        owned(gains_one.value),
         gate_grad,
         up_grad,
         down_grad,
-        gain_grads[1],
+        owned(gains_two.value),
     )
 
 

time: 969 us -> 898 us (0.927)
  blocking collectives: 43.9 us -> 0 us
  waiting for transfers between devices: 251 us -> 212 us
  starting transfers between devices: 245 us -> 216 us
  other arithmetic: 92.2 us -> 117 us
  matrix products: 190 us -> 204 us
    psum x1 -> x0, blocking collectives: 43.9 us -> none  [per_device(): gain_grads = lax.psum(gain_grads, ('fsdp', 'heads', 'tensor'))]
    ppermute x102 -> x112, waiting for transfers between devices: 228 us -> 189 us  [the longest x106 184 us: slot(): moved = [lax.ppermute(g, s[1], s[2]) for g, s in zip(gated, flat)]]
    ppermute x102 -> x112, starting transfers between devices: 241 us -> 213 us  [the longest x106 210 us: slot(): moved = [lax.ppermute(g, s[1], s[2]) for g, s in zip(gated, flat)]]
    dynamic_update_slice x32, other arithmetic: 30.8 us -> 45.1 us  [the longest x24 29.1 us: result(): lax.dynamic_update_index_in_dim(out, block, lax.rem(me - t + count, count...]
    dot_general x10, matrix products: 57 us -> 71 us  [dot_cols(): lax.dot_general(left_in, right_in, (((1,), (1,)), ((), ())), preferred_el...]
    convert_element_type x29 -> x23, other arithmetic: 31.3 us -> 40.5 us  [the longest x16 24.4 us: sends(): to_left = (to_left.astype(F32) + self.from_right.astype(F32)).astype(BF)]
  transfers between devices with their start and end apart: 118 -> 128, of which waited for: 43 -> 43; matrix products, arithmetic and copies ran while one was open for 28% -> 38% of each run, Pallas kernels for 8% -> 8%
where the time goes in v2:
time: 898 us; the launch traced here: 887 us
  starting transfers between devices  216 us (24%)
  waiting for transfers between devices  212 us (24%)
  matrix products  204 us (23%)
  other arithmetic  117 us (13%)
  Pallas kernels  73.8 us (8%)
  local copies, waits for them, and re-layouts  47.4 us (5%)
  between operations  16.7 us (2%)
    ppermute x106, starting transfers between devices, slot(): moved = [lax.ppermute(g, s[1], s[2]) for g, s in zip(gated, flat)]  210 us
    ppermute x106, waiting for transfers between devices, slot(): moved = [lax.ppermute(g, s[1], s[2]) for g, s in zip(gated, flat)]  184 us
    dot_general x12, matrix products, dot_plain(): return jnp.dot(left_in, right_in, preferred_element_type=F32)  84 us
    dot_general x10, matrix products, dot_cols(): lax.dot_general(left_in, right_in, (((1,), (1,)), ((), ())), preferred_el...  71 us
    dot_general x5, matrix products, dot_rows(): lax.dot_general(left_in, right_in, (((0,), (0,)), ((), ())), preferred_el...  48.9 us
    pallas_call x2, Pallas kernels, attend_back_call(): pl.pallas_call(functools.partial(attend_back_kernel, group), grid_spec=pl...  32.6 us
    dynamic_update_slice x24, other arithmetic, result(): lax.dynamic_update_index_in_dim(out, block, lax.rem(me - t + count, count...  29.1 us
    convert_element_type x16, other arithmetic, sends(): to_left = (to_left.astype(F32) + self.from_right.astype(F32)).astype(BF)  24.4 us
  transfers between devices with their start and end apart: 128, of which 43 were waited for; matrix products, arithmetic and copies ran while one was open for 38% of the time, Pallas kernels for 8%

profile of v2, /device:TPU:0, one launch (start us, length us, event | category | flops | bytes accessed | tf_op | source)
XLA Modules:
  0.0 886.8 jit_solution(13417147270981795000)
XLA Ops:
  28.3 19.6 %all-gather.6.cloned.1.call-done = bf16[2048,896]{1,0:T(8,128)(2,1)} async-done(((bf16[256,896]{1,0:T(8,128)(2,1)}), bf16[2048,896]{1,0:T(8,128)(2,1)}) %all-gather.6.cloned.1.call-update) | async-done | bytes 3670032 | tf_op jit(solution)/shard_map/all_gather | solution.py:442
  79.9 11.9 %attend.2 = (bf16[2,256,512]{2,1,0:T(8,128)(2,1)}, f32[2,8,256]{2,1,0:T(8,128)}) custom-call(s32[5]{0:T(128)} %stack.20.place_ref, bf16[2,256,512]{2,1,0:T(8,128)(2,1)} %bitcast.411, bf16[2,256,256]{2,1,0:T(8,128)(2,1)} %bitcast.419, bf16[2,256,256]{2,1,0:T(8,128)(2,1)} %copy-done.92, bf16[2,256,256]{2,1,0:T(8,128)(2,1)} %copy-done.91, ...), custom_call_target="tpu_custom_call" | custom-call | flops 4294967296 | bytes 1572864 | tf_op jit(solution)/shard_map/attend/pallas_call | solution.py:244
  100.9 11.4 %attend.3 = (bf16[2,256,512]{2,1,0:T(8,128)(2,1)}, f32[2,8,256]{2,1,0:T(8,128)}) custom-call(s32[5]{0:T(128)} %stack.20.place_ref, bf16[2,256,512]{2,1,0:T(8,128)(2,1)} %bitcast.409, bf16[2,256,256]{2,1,0:T(8,128)(2,1)} %bitcast.415, bf16[2,256,256]{2,1,0:T(8,128)(2,1)} %collective-permute-done.5.k1, bf16[2,256,256]{2,1,0:T(8,128)(2,1)} %copy-done.90, ...), custom_call_target="tpu_custom_call" | custom-call | flops 4294967296 | bytes 1572864 | tf_op jit(solution)/shard_map/attend/pallas_call | solution.py:244
  122.1 10.6 %collective-permute-done.8 = bf16[128,2048]{1,0:T(8,128)(2,1)S(1)} collective-permute-done((bf16[128,2048]{1,0:T(8,128)(2,1)}, bf16[128,2048]{1,0:T(8,128)(2,1)S(1)}, u32[]{:S(2)}, u32[]{:S(2)}) %collective-permute-start.8) | collective-permute-done | bytes 524320 | tf_op jit(solution)/shard_map/ppermute | solution.py:140
  141.9 9.1 %collective-permute-done.10 = bf16[128,2048]{1,0:T(8,128)(2,1)S(1)} collective-permute-done((bf16[128,2048]{1,0:T(8,128)(2,1)S(1)}, bf16[128,2048]{1,0:T(8,128)(2,1)S(1)}, u32[]{:S(2)}, u32[]{:S(2)}) %collective-permute-start.10) | collective-permute-done | bytes 524320 | tf_op jit(solution)/shard_map/ppermute | solution.py:140
  162.1 8.4 collective-permute-done.12
  179.8 6.4 collective-permute-done.16
  229.8 10.7 %fusion.127 = f32[512,2048]{1,0:T(8,128)} fusion(bf16[512,2048]{1,0:T(8,128)(2,1)} %bitcast.401, bf16[2048,2048]{1,0:T(8,128)(2,1)} %all-gather.10.cloned.1.call-done), kind=kOutput, calls=%fused_computation.294 | convolution fusion | flops 4294967296 | bytes 14680064 | tf_op jit(solution)/shard_map/dot_general | solution.py:32
  240.4 10.7 %fusion.128 = f32[512,2048]{1,0:T(8,128)} fusion(bf16[512,2048]{1,0:T(8,128)(2,1)} %bitcast.402, bf16[2048,2048]{1,0:T(8,128)(2,1)} %all-gather.12.cloned.1.call-done), kind=kOutput, calls=%fused_computation.295 | convolution fusion | flops 4294967296 | bytes 14680064 | tf_op jit(solution)/shard_map/dot_general | solution.py:32
  254.8 14.2 %multiply_convert_fusion.3 = (bf16[512,2048]{1,0:T(8,128)(2,1)S(1)}, bf16[512,2048]{1,0:T(8,128)(2,1)}, bf16[512,2048]{1,0:T(8,128)(2,1)}) fusion(f32[512,2048]{1,0:T(8,128)} %fusion.127, f32[512,2048]{1,0:T(8,128)} %fusion.128, bf16[512,2048]{1,0:T(8,128)(2,1)} %bitcast.396, bf16[2048,2048]{1,0:T(8,128)(2,1)} %all-gather.14.cloned.1.call-done), kind=kOutput, calls=%fused_computation.37 | convolution fusion | flops 4311744512 | bytes 25165824 | tf_op jit(solution)/shard_map/dot_general | solution.py:32
  271.0 9.8 %fusion.129 = f32[512,2048]{1,0:T(8,128)} fusion(bf16[512,2048]{1,0:T(8,128)(2,1)S(1)} %get-tuple-element.247, bf16[2048,2048]{1,0:T(8,128)(2,1)} %all-gather.12.cloned.1.call-done), kind=kOutput, calls=%fused_computation.296 | convolution fusion | flops 4294967296 | bytes 14680064 | tf_op jit(solution)/shard_map/dot_general | solution.py:42
  280.9 9.8 %add_convert_fusion.1 = bf16[512,2048]{1,0:T(8,128)(2,1)S(1)} fusion(f32[512,2048]{1,0:T(8,128)} %fusion.129, bf16[512,2048]{1,0:T(8,128)(2,1)} %get-tuple-element.241, bf16[2048,2048]{1,0:T(8,128)(2,1)} %all-gather.10.cloned.1.call-done), kind=kOutput, calls=%fused_computation.36 | convolution fusion | flops 4297064448 | bytes 16777216 | tf_op jit(solution)/shard_map/dot_general | solution.py:42
  292.8 6.5 collective-permute-start.30
  300.4 7.4 convolution_convert_fusion.6
  313.6 10.5 %fusion.130 = f32[512,2048]{1,0:T(8,128)} fusion(bf16[512,2048]{1,0:T(8,128)(2,1)} %bitcast.48, bf16[2048,2048]{1,0:T(8,128)(2,1)} %all-gather.10.cloned.1.call-done), kind=kOutput, calls=%fused_computation.297 | convolution fusion | flops 4294967296 | bytes 14680064 | tf_op jit(solution)/shard_map/dot_general | solution.py:32
  324.1 7.6 fusion.131
  337.8 9.7 %multiply_convert_fusion = (bf16[512,2048]{1,0:T(8,128)(2,1)S(1)}, bf16[512,2048]{1,0:T(8,128)(2,1)}, bf16[512,2048]{1,0:T(8,128)(2,1)}) fusion(f32[512,2048]{1,0:T(8,128)} %fusion.130, f32[512,2048]{1,0:T(8,128)} %fusion.131, bf16[512,2048]{1,0:T(8,128)(2,1)S(1)} %bitcast.394, bf16[2048,2048]{1,0:T(8,128)(2,1)S(1)} %bitcast.430), kind=kOutput, calls=%fused_computation.32 | convolution fusion | flops 4311744512 | bytes 25165824 | tf_op jit(solution)/shard_map/dot_general | solution.py:32
  359.1 7.0 fusion.132
  366.1 9.6 %add_convert_fusion = bf16[512,2048]{1,0:T(8,128)(2,1)} fusion(f32[512,2048]{1,0:T(8,128)S(1)} %fusion.132, bf16[512,2048]{1,0:T(8,128)(2,1)S(1)} %copy-done.96, bf16[2048,2048]{1,0:T(8,128)(2,1)} %all-gather.10.cloned.1.call-done), kind=kOutput, calls=%fused_computation.31 | convolution fusion | flops 4297064448 | bytes 16777216 | tf_op jit(solution)/shard_map/dot_general | solution.py:42
  378.2 11.4 %convolution_convert_fusion.2 = bf16[2048,2048]{1,0:T(8,128)(2,1)} fusion(bf16[512,2048]{1,0:T(8,128)(2,1)S(1)} %bitcast.395, bf16[512,2048]{1,0:T(8,128)(2,1)S(1)} %bitcast.398, bf16[512,2048]{1,0:T(8,128)(2,1)S(1)} %copy-done.101, bf16[512,2048]{1,0:T(8,128)(2,1)S(1)} %copy-done.103), kind=kOutput, calls=%fused_computation.2 | convolution fusion | flops 8610906112 | bytes 16777216 | tf_op jit(solution)/shard_map/dot_general | solution.py:36
  407.4 13.7 %convolution_convert_fusion.1 = bf16[2048,2048]{1,0:T(8,128)(2,1)} fusion(bf16[512,2048]{1,0:T(8,128)(2,1)} %bitcast.48, bf16[512,2048]{1,0:T(8,128)(2,1)S(1)} %bitcast.403, bf16[512,2048]{1,0:T(8,128)(2,1)} %get-tuple-element.242, bf16[512,2048]{1,0:T(8,128)(2,1)} %get-tuple-element.241), kind=kOutput, calls=%fused_computation.1 | convolution fusion | flops 8610906112 | bytes 16777216 | tf_op jit(solution)/shard_map/dot_general | solution.py:36
  446.3 13.4 %convolution_convert_fusion = bf16[2048,2048]{1,0:T(8,128)(2,1)} fusion(bf16[512,2048]{1,0:T(8,128)(2,1)} %bitcast.48, bf16[512,2048]{1,0:T(8,128)(2,1)S(1)} %bitcast.404, bf16[512,2048]{1,0:T(8,128)(2,1)S(1)} %copy-done.100, bf16[512,2048]{1,0:T(8,128)(2,1)S(1)} %copy-done.98), kind=kOutput, calls=%fused_computation | convolution fusion | flops 8610906112 | bytes 16777216 | tf_op jit(solution)/shard_map/dot_general | solution.py:36
  478.5 16.5 %attend_back.2 = (bf16[2,256,512]{2,1,0:T(8,128)(2,1)}, bf16[2,256,256]{2,1,0:T(8,128)(2,1)}, bf16[2,256,256]{2,1,0:T(8,128)(2,1)}, bf16[2,256,256]{2,1,0:T(8,128)(2,1)}, bf16[2,256,256]{2,1,0:T(8,128)(2,1)}) custom-call(s32[5]{0:T(128)} %stack.20.place_ref, bf16[2,256,512]{2,1,0:T(8,128)(2,1)} %bitcast.412, bf16[2,256,256]{2,1,0:T(8,128)(2,1)} %bitcast.420, ...), custom_call_target="tpu_custom_call" | custom-call | flops 10737418240 | bytes 3145728 | tf_op jit(solution)/shard_map/attend_back/pallas_call | solution.py:364
  538.8 9.2 %convolution_convert_fusion.4 = bf16[512,2048]{1,0:T(8,128)(2,1)} fusion(bf16[512,2048]{1,0:T(8,128)(2,1)S(1)} %copy-done.102, bf16[2048,2048]{1,0:T(8,128)(2,1)} %all-gather.14.cloned.1.call-done), kind=kOutput, calls=%fused_computation.48 | convolution fusion | flops 4296015872 | bytes 12582912 | tf_op jit(solution)/shard_map/dot_general | solution.py:42
  561.8 16.1 %attend_back.3 = (bf16[2,256,512]{2,1,0:T(8,128)(2,1)}, bf16[2,256,256]{2,1,0:T(8,128)(2,1)}, bf16[2,256,256]{2,1,0:T(8,128)(2,1)}, bf16[2,256,256]{2,1,0:T(8,128)(2,1)}, bf16[2,256,256]{2,1,0:T(8,128)(2,1)}) custom-call(s32[5]{0:T(128)} %stack.20.place_ref, bf16[2,256,512]{2,1,0:T(8,128)(2,1)} %bitcast.410, bf16[2,256,256]{2,1,0:T(8,128)(2,1)} %bitcast.416, ...), custom_call_target="tpu_custom_call" | custom-call | flops 10737418240 | bytes 3145728 | tf_op jit(solution)/shard_map/attend_back/pallas_call | solution.py:364
  655.5 7.4 collective-permute-done.81
  699.4 6.4 collective-permute-done.86
  716.0 6.6 collective-permute-done.90
  767.9 8.9 collective-permute-done.99
  776.8 9.5 %collective-permute-start.105 = (bf16[128,2048]{1,0:T(8,128)(2,1)S(1)}, bf16[128,2048]{1,0:T(8,128)(2,1)S(1)}, u32[]{:S(2)}, u32[]{:S(2)}) collective-permute-start(bf16[128,2048]{1,0:T(8,128)(2,1)S(1)} %get-tuple-element.332), channel_id=1, source_target_pairs={{0,1},{1,2},{4,5},{5,6},{8,9},{9,10},{12,13},{13,14},{16,17},{17,1... | collective-permute-start | bytes 1572872 | tf_op jit(solution)/shard_map/ppermute | solution.py:140
  794.3 10.6 %collective-permute-done.104 = bf16[128,2048]{1,0:T(8,128)(2,1)S(1)} collective-permute-done((bf16[128,2048]{1,0:T(8,128)(2,1)S(1)}, bf16[128,2048]{1,0:T(8,128)(2,1)S(1)}, u32[]{:S(2)}, u32[]{:S(2)}) %collective-permute-start.104) | collective-permute-done | bytes 524320 | tf_op jit(solution)/shard_map/ppermute | solution.py:140
  850.5 11.1 %collective-permute-done.115 = bf16[128,2048]{1,0:T(8,128)(2,1)S(1)} collective-permute-done((bf16[128,2048]{1,0:T(8,128)(2,1)}, bf16[128,2048]{1,0:T(8,128)(2,1)S(1)}, u32[]{:S(2)}, u32[]{:S(2)}) %collective-permute-start.115) | collective-permute-done | bytes 524320 | tf_op jit(solution)/shard_map/ppermute | solution.py:140
  (631 shorter events, 538.7 us)
Async XLA Ops:
  7.2 40.8 %all-gather.6.cloned.1.call-start = ((), (), s32[]{:S(2)}) async-start(), calls=%async_computation.5 | async-start | bytes 4128768 | tf_op jit(solution)/shard_map/all_gather | solution.py:442
  10.7 81.2 %all-gather.8.cloned.1.call-start = ((), (), s32[]{:S(2)}) async-start(), calls=%async_computation.6 | async-start | bytes 2359296 | tf_op jit(solution)/shard_map/all_gather | solution.py:442
  11.4 218.4 %all-gather.10.cloned.1.call-start = ((), (), s32[]{:S(2)}) async-start(), calls=%async_computation.7 | async-start | bytes 9437184 | tf_op jit(solution)/shard_map/all_gather | solution.py:442
  12.2 228.3 %all-gather.12.cloned.1.call-start = ((), (), s32[]{:S(2)}) async-start(), calls=%async_computation.8 | async-start | bytes 9437184 | tf_op jit(solution)/shard_map/all_gather | solution.py:442
  12.7 242.1 %all-gather.14.cloned.1.call-start = ((), (), s32[]{:S(2)}) async-start(), calls=%async_computation.9 | async-start | bytes 9437184 | tf_op jit(solution)/shard_map/all_gather | solution.py:442
  13.3 569.7 %reduce-scatter.6.cloned.1.call-start = ((), (), s32[]{:S(2)}) async-start(), calls=%async_computation.10 | async-start | bytes 9437184 | tf_op jit(solution)/shard_map/reduce_scatter | solution.py:554
  59.3 19.8 %collective-permute-start = (bf16[2,256,256]{2,1,0:T(8,128)(2,1)}, bf16[2,256,256]{2,1,0:T(8,128)(2,1)S(1)}, u32[]{:S(2)}, u32[]{:S(2)}) collective-permute-start(bf16[2,256,256]{2,1,0:T(8,128)(2,1)} %bitcast.418), channel_id=1, source_target_pairs={{0,4},{4,0},{8,12},{12,8},{1,5},{5,1},{9,13},{13,9},{2,6},{6,2},{1... | collective-permute-start | bytes 786440 | tf_op jit(solution)/shard_map/ppermute | solution.py:488
  64.8 36.2 %collective-permute-start.5 = (bf16[2,256,256]{2,1,0:T(8,128)(2,1)}, bf16[2,256,256]{2,1,0:T(8,128)(2,1)}, u32[]{:S(2)}, u32[]{:S(2)}) collective-permute-start(bf16[2,256,256]{2,1,0:T(8,128)(2,1)} %bitcast.414), channel_id=1, source_target_pairs={{0,4},{4,0},{8,12},{12,8},{1,5},{5,1},{9,13},{13,9},{2,6},{6,2},{1... | collective-permute-start | bytes 786440 | tf_op jit(solution)/shard_map/ppermute | solution.py:488
  78.8 22.2 %collective-permute-start.7 = (bf16[2,256,256]{2,1,0:T(8,128)(2,1)S(1)}, bf16[2,256,256]{2,1,0:T(8,128)(2,1)}, u32[]{:S(2)}, u32[]{:S(2)}) collective-permute-start(bf16[2,256,256]{2,1,0:T(8,128)(2,1)S(1)} %collective-permute-done.6.k2), channel_id=1, source_target_pairs={{0,4},{4,0},{8,12},{12,8},{1,5},{5,1},{9,13},{13,9},{2,6},{6,2},{1... | collective-permute-start | bytes 786440 | tf_op jit(solution)/shard_map/ppermute | solution.py:489
  96.1 20.6 %collective-permute-start.3 = (bf16[128,2048]{1,0:T(8,128)(2,1)}, bf16[128,2048]{1,0:T(8,128)(2,1)S(1)}, u32[]{:S(2)}, u32[]{:S(2)}) collective-permute-start(bf16[128,2048]{1,0:T(8,128)(2,1)} %get-tuple-element.179), channel_id=1, source_target_pairs={{0,1},{4,5},{8,9},{12,13},{16,17},{20,21},{24,25},{28,29}} | collective-permute-start | bytes 1572872 | tf_op jit(solution)/shard_map/ppermute | solution.py:140
  269.0 21.8 %collective-permute-start.26 = (bf16[128,2048]{1,0:T(8,128)(2,1)S(1)}, bf16[128,2048]{1,0:T(8,128)(2,1)S(1)}, u32[]{:S(2)}, u32[]{:S(2)}) collective-permute-start(bf16[128,2048]{1,0:T(8,128)(2,1)S(1)} %collective-permute-done.24), channel_id=1, source_target_pairs={{1,2},{2,3},{5,6},{6,7},{9,10},{10,11},{13,14},{14,15},{17,18},{18... | collective-permute-start | bytes 1572872 | tf_op jit(solution)/shard_map/ppermute | solution.py:140
  269.7 21.1 %collective-permute-start.27 = (bf16[128,2048]{1,0:T(8,128)(2,1)S(1)}, bf16[128,2048]{1,0:T(8,128)(2,1)S(1)}, u32[]{:S(2)}, u32[]{:S(2)}) collective-permute-start(bf16[128,2048]{1,0:T(8,128)(2,1)S(1)} %collective-permute-done.25), channel_id=1, source_target_pairs={{2,1},{1,0},{6,5},{5,4},{10,9},{9,8},{14,13},{13,12},{18,17},{17,1... | collective-permute-start | bytes 1572872 | tf_op jit(solution)/shard_map/ppermute | solution.py:140
  311.0 20.7 %collective-permute-start.32 = (bf16[128,2048]{1,0:T(8,128)(2,1)S(1)}, bf16[128,2048]{1,0:T(8,128)(2,1)S(1)}, u32[]{:S(2)}, u32[]{:S(2)}) collective-permute-start(bf16[128,2048]{1,0:T(8,128)(2,1)S(1)} %get-tuple-element.215), channel_id=1, source_target_pairs={{0,1},{1,2},{4,5},{5,6},{8,9},{9,10},{12,13},{13,14},{16,17},{17,1... | collective-permute-start | bytes 1572872 | tf_op jit(solution)/shard_map/ppermute | solution.py:140
  312.7 19.0 %collective-permute-start.33 = (bf16[128,2048]{1,0:T(8,128)(2,1)S(1)}, bf16[128,2048]{1,0:T(8,128)(2,1)S(1)}, u32[]{:S(2)}, u32[]{:S(2)}) collective-permute-start(bf16[128,2048]{1,0:T(8,128)(2,1)S(1)} %get-tuple-element.216), channel_id=1, source_target_pairs={{3,2},{2,1},{7,6},{6,5},{11,10},{10,9},{15,14},{14,13},{19,18},{18... | collective-permute-start | bytes 1572872 | tf_op jit(solution)/shard_map/ppermute | solution.py:140
  352.0 26.1 %collective-permute-start.36 = (bf16[128,2048]{1,0:T(8,128)(2,1)S(1)}, bf16[128,2048]{1,0:T(8,128)(2,1)S(1)}, u32[]{:S(2)}, u32[]{:S(2)}) collective-permute-start(bf16[128,2048]{1,0:T(8,128)(2,1)S(1)} %get-tuple-element.224), channel_id=1, source_target_pairs={{0,1},{1,2},{2,3},{4,5},{5,6},{6,7},{8,9},{9,10},{10,11},{12,13},{... | collective-permute-start | bytes 1572872 | tf_op jit(solution)/shard_map/ppermute | solution.py:140
  357.7 20.5 %collective-permute-start.37 = (bf16[128,2048]{1,0:T(8,128)(2,1)S(1)}, bf16[128,2048]{1,0:T(8,128)(2,1)S(1)}, u32[]{:S(2)}, u32[]{:S(2)}) collective-permute-start(bf16[128,2048]{1,0:T(8,128)(2,1)S(1)} %get-tuple-element.224), channel_id=1, source_target_pairs={{3,2},{2,1},{1,0},{7,6},{6,5},{5,4},{11,10},{10,9},{9,8},{15,14},{... | collective-permute-start | bytes 1572872 | tf_op jit(solution)/shard_map/ppermute | solution.py:140
  389.6 326.4 %reduce-scatter.8.cloned.1.call-start = ((), (), s32[]{:S(2)}) async-start(), calls=%async_computation.11 | async-start | bytes 9437184 | tf_op jit(solution)/shard_map/reduce_scatter | solution.py:554
  421.1 332.9 %reduce-scatter.10.cloned.1.call-start = ((), (), s32[]{:S(2)}) async-start(), calls=%async_computation.12 | async-start | bytes 9437184 | tf_op jit(solution)/shard_map/reduce_scatter | solution.py:554
  442.5 21.2 %collective-permute-start.46 = (bf16[128,2048]{1,0:T(8,128)(2,1)}, bf16[128,2048]{1,0:T(8,128)(2,1)S(1)}, u32[]{:S(2)}, u32[]{:S(2)}) collective-permute-start(bf16[128,2048]{1,0:T(8,128)(2,1)} %get-tuple-element.243), channel_id=1, source_target_pairs={{0,1},{1,2},{2,3},{4,5},{5,6},{6,7},{8,9},{9,10},{10,11},{12,13},{... | collective-permute-start | bytes 1572872 | tf_op jit(solution)/shard_map/ppermute | solution.py:140
  444.0 19.7 %collective-permute-start.47 = (bf16[128,2048]{1,0:T(8,128)(2,1)}, bf16[128,2048]{1,0:T(8,128)(2,1)S(1)}, u32[]{:S(2)}, u32[]{:S(2)}) collective-permute-start(bf16[128,2048]{1,0:T(8,128)(2,1)} %get-tuple-element.244), channel_id=1, source_target_pairs={{3,2},{2,1},{1,0},{7,6},{6,5},{5,4},{11,10},{10,9},{9,8},{15,14},{... | collective-permute-start | bytes 1572872 | tf_op jit(solution)/shard_map/ppermute | solution.py:140
  468.6 26.4 %collective-permute-start.50 = (f32[2048]{0:T(1024)S(1)}, f32[2048]{0:T(1024)S(1)}, u32[]{:S(2)}, u32[]{:S(2)}) collective-permute-start(f32[2048]{0:T(1024)S(1)} %add.575), channel_id=1, source_target_pairs={{0,1},{1,0},{2,3},{3,2},{4,5},{5,4},{6,7},{7,6},{8,9},{9,8},{10,11... | collective-permute-start | bytes 24584 | tf_op jit(solution)/shard_map/ppermute | solution.py:140
  470.7 24.3 %collective-permute-start.48 = (bf16[128,2048]{1,0:T(8,128)(2,1)}, bf16[128,2048]{1,0:T(8,128)(2,1)S(1)}, u32[]{:S(2)}, u32[]{:S(2)}) collective-permute-start(bf16[128,2048]{1,0:T(8,128)(2,1)} %get-tuple-element.250), channel_id=1, source_target_pairs={{0,1},{1,2},{2,3},{4,5},{5,6},{6,7},{8,9},{9,10},{10,11},{12,13},{... | collective-permute-start | bytes 1572872 | tf_op jit(solution)/shard_map/ppermute | solution.py:140
  472.6 22.4 %collective-permute-start.49 = (bf16[128,2048]{1,0:T(8,128)(2,1)}, bf16[128,2048]{1,0:T(8,128)(2,1)S(1)}, u32[]{:S(2)}, u32[]{:S(2)}) collective-permute-start(bf16[128,2048]{1,0:T(8,128)(2,1)} %get-tuple-element.250), channel_id=1, source_target_pairs={{3,2},{2,1},{1,0},{7,6},{6,5},{5,4},{11,10},{10,9},{9,8},{15,14},{... | collective-permute-start | bytes 1572872 | tf_op jit(solution)/shard_map/ppermute | solution.py:140
  495.1 20.5 %collective-permute-start.56 = (bf16[2,256,256]{2,1,0:T(8,128)(2,1)}, bf16[2,256,256]{2,1,0:T(8,128)(2,1)}, u32[]{:S(2)}, u32[]{:S(2)}) collective-permute-start(bf16[2,256,256]{2,1,0:T(8,128)(2,1)} %get-tuple-element.266), channel_id=1, source_target_pairs={{0,4},{4,0},{8,12},{12,8},{1,5},{5,1},{9,13},{13,9},{2,6},{6,2},{1... | collective-permute-start | bytes 786440 | tf_op jit(solution)/shard_map/ppermute | solution.py:540
  507.3 305.9 %reduce-scatter.14.cloned.1.call-start = ((), (), s32[]{:S(2)}) async-start(), calls=%async_computation.14 | async-start | bytes 2359296 | tf_op jit(solution)/shard_map/reduce_scatter | solution.py:554
  507.4 19.8 %collective-permute-start.53 = (bf16[128,2048]{1,0:T(8,128)(2,1)}, bf16[128,2048]{1,0:T(8,128)(2,1)}, u32[]{:S(2)}, u32[]{:S(2)}) collective-permute-start(bf16[128,2048]{1,0:T(8,128)(2,1)} %get-tuple-element.261), channel_id=1, source_target_pairs={{0,1},{4,5},{8,9},{12,13},{16,17},{20,21},{24,25},{28,29}} | collective-permute-start | bytes 1572872 | tf_op jit(solution)/shard_map/ppermute | solution.py:140
  550.9 27.0 %collective-permute-start.66 = (f32[2048]{0:T(1024)S(1)}, f32[2048]{0:T(1024)S(1)}, u32[]{:S(2)}, u32[]{:S(2)}) collective-permute-start(f32[2048]{0:T(1024)S(1)} %add.585), channel_id=1, source_target_pairs={{0,8},{4,12},{8,0},{12,4},{1,9},{5,13},{9,1},{13,5},{2,10},{6,14},... | collective-permute-start | bytes 24584 | tf_op jit(solution)/shard_map/ppermute | solution.py:140
  552.1 25.9 %collective-permute-start.64 = (bf16[128,2048]{1,0:T(8,128)(2,1)}, bf16[128,2048]{1,0:T(8,128)(2,1)S(1)}, u32[]{:S(2)}, u32[]{:S(2)}) collective-permute-start(bf16[128,2048]{1,0:T(8,128)(2,1)} %get-tuple-element.275), channel_id=1, source_target_pairs={{0,1},{1,2},{2,3},{4,5},{5,6},{6,7},{8,9},{9,10},{10,11},{12,13},{... | collective-permute-start | bytes 1572872 | tf_op jit(solution)/shard_map/ppermute | solution.py:140
  558.4 19.6 %collective-permute-start.65 = (bf16[128,2048]{1,0:T(8,128)(2,1)S(1)}, bf16[128,2048]{1,0:T(8,128)(2,1)}, u32[]{:S(2)}, u32[]{:S(2)}) collective-permute-start(bf16[128,2048]{1,0:T(8,128)(2,1)S(1)} %get-tuple-element.276), channel_id=1, source_target_pairs={{3,2},{2,1},{1,0},{7,6},{6,5},{5,4},{11,10},{10,9},{9,8},{15,14},{... | collective-permute-start | bytes 1572872 | tf_op jit(solution)/shard_map/ppermute | solution.py:140
  588.7 21.0 %collective-permute-start.69 = (f32[2048]{0:T(1024)S(1)}, f32[2048]{0:T(1024)S(1)}, u32[]{:S(2)}, u32[]{:S(2)}) collective-permute-start(f32[2048]{0:T(1024)S(1)} %add.589), channel_id=1, source_target_pairs={{0,16},{16,0},{1,17},{17,1},{2,18},{18,2},{3,19},{19,3},{4,20},{20... | collective-permute-start | bytes 24584 | tf_op jit(solution)/shard_map/ppermute | solution.py:140
  589.8 20.0 %collective-permute-start.67 = (bf16[128,2048]{1,0:T(8,128)(2,1)S(1)}, bf16[128,2048]{1,0:T(8,128)(2,1)S(1)}, u32[]{:S(2)}, u32[]{:S(2)}) collective-permute-start(bf16[128,2048]{1,0:T(8,128)(2,1)S(1)} %get-tuple-element.285), channel_id=1, source_target_pairs={{0,1},{1,2},{2,3},{4,5},{5,6},{6,7},{8,9},{9,10},{10,11},{12,13},{... | collective-permute-start | bytes 1572872 | tf_op jit(solution)/shard_map/ppermute | solution.py:140
  695.8 138.1 %reduce-scatter.12.cloned.1.call-start = ((), (), s32[]{:S(2)}) async-start(), calls=%async_computation.13 | async-start | bytes 3538944 | tf_op jit(solution)/shard_map/reduce_scatter | solution.py:554
  (204 other events, 2301.1 us)
Sparse Core Ops, SparseCore 0:
  10.8 37.1 all-gather.5
  49.8 31.4 all-gather.7
  83.2 54.2 all-gather.9
  139.2 54.2 all-gather.11
  195.3 54.2 all-gather.13
  389.7 72.1 reduce-scatter.5
  466.0 77.1 reduce-scatter.7
  546.6 77.1 reduce-scatter.9
  695.9 40.8 reduce-scatter.13
  746.1 46.2 reduce-scatter.11

commit v3 on v2

--- a/solution.py
+++ b/solution.py
@@ -96,13 +96,88 @@
         self.step += 1
 
     def result(self):
-        count, me = lax.axis_size("tensor"), lax.axis_index("tensor")
-        out = jnp.zeros((count,) + self.own.shape, self.own.dtype)
-        out = lax.dynamic_update_index_in_dim(out, self.own, me, 0)
-        for t in range(1, count):
-            block = jnp.where(me >= t, self.from_left[t], self.from_right[count - t])
-            out = lax.dynamic_update_index_in_dim(out, block, lax.rem(me - t + count, count), 0)
+        count = lax.axis_size("tensor")
+        steps = range(1, count)
+        return place_call(
+            self.own, [self.from_left[t] for t in steps], [self.from_right[t] for t in steps]
+        )
+
+
+class Both:
+    def __init__(self, gather, total):
+        self.gather, self.total = gather, total
+
+    def sends(self):
+        me, count = lax.axis_index("tensor"), lax.axis_size("tensor")
+        first = self.gather.step - 1
+        out = []
+        for rank, whole, part in zip(
+            (me, count - 1 - me), self.gather.sends(), self.total.sends()
+        ):
+            value = jnp.where(rank >= first, whole[0], part[0])
+            out.append((value, "tensor", sorted(whole[2] + part[2])))
         return out
+
+    def take(self, moved):
+        self.gather.take(moved)
+        self.total.take(moved)
+
+
+FLIP = [(0, 1), (1, 0)]
+
+
+class NearGather:
+    def __init__(self, shard):
+        self.shard = shard
+        self.step = 1
+        self.near = lax.axis_size("fsdp") == 2 and lax.axis_size("yy") == 2
+
+    def sends(self):
+        if not self.near:
+            return []
+        half = self.shard.shape[0] // 2
+        if self.step == 1:
+            return [(self.shard, "fsdp", FLIP), (self.shard, "yy", FLIP)]
+        if self.step == 2:
+            return [(self.by_y[:half], "fsdp", FLIP), (self.by_x[half:], "yy", FLIP)]
+        self.mine = jnp.concatenate([self.shard, self.by_y, self.by_x, self.lo, self.hi], axis=0)
+        return [(self.mine, "core", FLIP)]
+
+    def take(self, moved):
+        if self.near:
+            if self.step == 1:
+                self.by_x, self.by_y = moved
+            elif self.step == 2:
+                self.lo, self.hi = moved
+            else:
+                (self.other,) = moved
+        self.step += 1
+
+    def result(self):
+        if not self.near:
+            return lax.all_gather(self.shard, ("fsdp", "yy", "core"), axis=0, tiled=True)
+        return spread_call(self.mine, self.other)
+
+
+class KeyExchange:
+    def __init__(self, kv):
+        self.kv = kv
+        self.step = 1
+
+    def sends(self):
+        if self.step == 1:
+            return [(self.kv, "yy", FLIP), (self.kv, "core", FLIP)]
+        return [(self.kv2, "core", FLIP)]
+
+    def take(self, moved):
+        if self.step == 1:
+            self.kv2, self.kv1 = moved
+        else:
+            (self.kv3,) = moved
+        self.step += 1
+
+    def result(self):
+        return self.kv, self.kv1, self.kv2, self.kv3
 
 
 class Butterfly:
@@ -157,6 +232,159 @@
         lax.rem(lane, 64) < 32, pltpu.roll(values, 96, 1), pltpu.roll(values, 32, 1)
     )
     return values * cosine + swapped * sine
+
+
+def place_kernel(count, me_ref, *refs):
+    own, from_left, from_right = refs[0], refs[1:count], refs[count : 2 * count - 1]
+    out = refs[2 * count - 1]
+    me = me_ref[0]
+    for k in range(count):
+        todo = [(me == k, own)]
+        for t in range(1, count):
+            if k + t < count:
+                todo.append((me == k + t, from_left[t - 1]))
+            if k - t >= 0:
+                todo.append((me == k - t, from_right[t - 1]))
+        for chosen, source in todo:
+
+            @pl.when(chosen)
+            def _(source=source, k=k):
+                out[k] = source[...]
+
+
+def place_call(own, from_left, from_right):
+    count = len(from_left) + 1
+    rows, width = own.shape
+    tile = min(64, rows)
+    me = lax.axis_index("tensor").astype(jnp.int32)[None]
+    return pl.pallas_call(
+        functools.partial(place_kernel, count),
+        grid_spec=pltpu.PrefetchScalarGridSpec(
+            num_scalar_prefetch=1,
+            grid=(rows // tile,),
+            in_specs=[pl.BlockSpec((tile, width), lambda i, p: (i, 0))] * (2 * count - 1),
+            out_specs=pl.BlockSpec((count, tile, width), lambda i, p: (0, i, 0)),
+        ),
+        out_shape=jax.ShapeDtypeStruct((count,) + own.shape, own.dtype),
+        cost_estimate=pl.CostEstimate(
+            flops=0, bytes_accessed=6 * count * own.size, transcendentals=0
+        ),
+        name="place",
+    )(me, own, *from_left, *from_right)
+
+
+def spread_kernel(at_ref, mine_ref, other_ref, out_ref):
+    for core in range(2):
+
+        @pl.when(at_ref[1] == core)
+        def _(core=core):
+            out_ref[0, core] = mine_ref[0]
+            out_ref[0, 1 - core] = other_ref[0]
+
+
+def spread_call(mine, other):
+    rows, width = mine.shape[0] // 4, mine.shape[1]
+    chip = lax.axis_index("fsdp") * 2 + lax.axis_index("yy")
+    at = jnp.stack([chip, lax.axis_index("core")]).astype(jnp.int32)
+    block = pl.BlockSpec((1, rows, width), lambda i, at: (jnp.bitwise_xor(i, at[0]), 0, 0))
+    out = pl.pallas_call(
+        spread_kernel,
+        grid_spec=pltpu.PrefetchScalarGridSpec(
+            num_scalar_prefetch=1,
+            grid=(4,),
+            in_specs=[block, block],
+            out_specs=pl.BlockSpec((1, 2, rows, width), lambda i, at: (i, 0, 0, 0)),
+        ),
+        out_shape=jax.ShapeDtypeStruct((4, 2, rows, width), mine.dtype),
+        cost_estimate=pl.CostEstimate(
+            flops=0, bytes_accessed=8 * mine.size, transcendentals=0
+        ),
+        name="spread",
+    )(at, mine.reshape(4, rows, width), other.reshape(4, rows, width))
+    return out.reshape(8 * rows, width)
+
+
+def ffn_kernel(x_ref, cot_ref, g_ref, u_ref, d_ref, hidden_ref, d_gate_ref, d_up_ref):
+    x = x_ref[...]
+    gate = dot_plain(x, g_ref[...])
+    up = dot_plain(x, u_ref[...])
+    d_hidden = dot_plain(cot_ref[...], d_ref[...])
+    sig = jax.nn.sigmoid(gate)
+    act = gate * sig
+    hidden_ref[...] = (act * up).astype(BF)
+    d_up_ref[...] = (d_hidden * act).astype(BF)
+    d_gate_ref[...] = (d_hidden * up * (sig * (1.0 + gate * (1.0 - sig)))).astype(BF)
+
+
+def ffn_call(x, cot, g, u, d):
+    rows, width = x.shape
+    units = g.shape[1]
+    tile = min(256, units)
+    whole = pl.BlockSpec((rows, width), lambda i: (0, 0))
+    weight = pl.BlockSpec((width, tile), lambda i: (0, i))
+    part = pl.BlockSpec((rows, tile), lambda i: (0, i))
+    return pl.pallas_call(
+        ffn_kernel,
+        grid=(units // tile,),
+        in_specs=[whole, whole, weight, weight, weight],
+        out_specs=[part] * 3,
+        out_shape=[jax.ShapeDtypeStruct((rows, units), BF)] * 3,
+        cost_estimate=pl.CostEstimate(
+            flops=6 * rows * width * units,
+            bytes_accessed=6 * width * units + 6 * rows * units,
+            transcendentals=rows * units,
+        ),
+        name="ffn",
+    )(x, cot, g, u, d)
+
+
+def product_kernel(count, *refs):
+    total = None
+    for k in range(count):
+        part = dot_plain(refs[k][...], refs[count + k][...])
+        total = part if total is None else total + part
+    refs[2 * count][...] = total.astype(BF)
+
+
+def product_call(lefts, rights):
+    count = len(lefts)
+    rows, depth = lefts[0].shape
+    width = rights[0].shape[1]
+    tile = min(512, width)
+    return pl.pallas_call(
+        functools.partial(product_kernel, count),
+        grid=(width // tile,),
+        in_specs=[pl.BlockSpec((rows, depth), lambda i: (0, 0))] * count
+        + [pl.BlockSpec((depth, tile), lambda i: (0, i))] * count,
+        out_specs=pl.BlockSpec((rows, tile), lambda i: (0, i)),
+        out_shape=jax.ShapeDtypeStruct((rows, width), BF),
+        cost_estimate=pl.CostEstimate(
+            flops=2 * count * rows * depth * width,
+            bytes_accessed=2 * count * depth * (rows + width),
+            transcendentals=0,
+        ),
+        name="product",
+    )(*lefts, *rights)
+
+
+def transpose_kernel(x_ref, out_ref):
+    out_ref[...] = jnp.transpose(x_ref[...])
+
+
+def transpose_call(x):
+    rows, columns = x.shape
+    tile = min(256, rows)
+    return pl.pallas_call(
+        transpose_kernel,
+        grid=(rows // tile,),
+        in_specs=[pl.BlockSpec((tile, columns), lambda i: (i, 0))],
+        out_specs=pl.BlockSpec((columns, tile), lambda i: (0, i)),
+        out_shape=jax.ShapeDtypeStruct((columns, rows), x.dtype),
+        cost_estimate=pl.CostEstimate(
+            flops=0, bytes_accessed=4 * x.size, transcendentals=0
+        ),
+        name="turn_over",
+    )(x)
 
 
 def turn_kernel(turned, x_ref, cos_ref, sin_ref, out_ref):
@@ -419,12 +647,13 @@
     ffn_gain,
     cotangent,
 ):
+    heads_axes = ("yy", "core")
     seqs, block, width = tokens.shape
     seq_len = segments.shape[1]
-    parts = lax.axis_size("heads")
+    parts = lax.axis_size(heads_axes)
     ways = lax.axis_size("tensor")
-    owners = ("fsdp", "heads")
-    here = lax.axis_index("heads")
+    owners = ("fsdp",) + heads_axes
+    here = lax.axis_index(heads_axes)
     me = lax.axis_index("tensor")
     q_width, k_width = q_weight.shape[1], k_weight.shape[1]
     kv_width = 2 * k_width
@@ -442,13 +671,9 @@
         return lax.all_gather(shard, owners, axis=0, tiled=True)
 
     packed = gathered(packed)
-    full_o = gathered(o_weight)
     full_g = gathered(gate_weight)
     full_u = gathered(up_weight)
     full_d = gathered(down_weight)
-    full_qkv = packed[:, :qkv_width]
-    gains = packed[:, qkv_width : qkv_width + 2].T.astype(F32)
-    gain_one, gain_two = gains[0:1], gains[1:2]
 
     where_all = positions(segments)
     where_here = lax.dynamic_slice_in_dim(where_all, here * block, block, 1)
@@ -475,30 +700,43 @@
     for c in range(CHUNKS):
         s = {}
         tok = chunk_of(tokens, c).reshape(rows, width)
-        tok_f = tok.astype(F32)
         s["tok"] = tok
         s["cot"] = chunk_of(cotangent, c).reshape(rows, width)
-        s["normed_one"] = (tok_f * inverse_rms(tok_f) * gain_one).astype(BF)
         s["cos"] = lax.slice_in_dim(cosine, c * rows, (c + 1) * rows, axis=0)
         s["sin"] = lax.slice_in_dim(sine, c * rows, (c + 1) * rows, axis=0)
-        kv = turn_call(
-            dot_plain(s["normed_one"], full_qkv[:, q_width:]), s["cos"], s["sin"], k_width
-        ).reshape(per_chunk, block, kv_width)
-        kv2 = lax.ppermute(kv, "heads", pairs(parts, 2))
-        kv1 = lax.ppermute(kv, "heads", pairs(parts, 1))
-        kv3 = lax.ppermute(kv2, "heads", pairs(parts, 1))
-        s["kv"] = (kv, kv1, kv2, kv3)
-        s["q"] = turn_call(
-            dot_plain(s["normed_one"], full_qkv[:, :q_width]), s["cos"], s["sin"], q_width
-        ).reshape(per_chunk, block, q_width)
         seg_q, seg_k = chunk_of(seg_here, c), chunk_of(segments, c)
         s["seg_fwd"] = (seg_q[:, :, None], seg_k[:, None, :])
         s["seg_back"] = (seg_q[:, None, :], seg_k[:, :, None])
         state.append(s)
     first, second = state
 
-    def attend(s, q):
-        attended, lse = attend_call(place, q, s["kv"], *s["seg_fwd"])
+    clock = Clock()
+    slot = clock.slot
+    gather_o = NearGather(o_weight)
+    slot([gather_o])
+    slot([gather_o])
+    slot([gather_o])
+    full_o = gather_o.result()
+    full_qkv = packed[:, :qkv_width]
+    gains = packed[:, qkv_width : qkv_width + 2].T.astype(F32)
+    gain_one, gain_two = gains[0:1], gains[1:2]
+
+    def project_kv(s, tok):
+        tok_f = tok.astype(F32)
+        normed = (tok_f * inverse_rms(tok_f) * gain_one).astype(BF)
+        kv = turn_call(dot_plain(normed, full_qkv[:, q_width:]), s["cos"], s["sin"], k_width)
+        return normed, kv.reshape(per_chunk, block, kv_width)
+
+    def project_q(s, normed):
+        q = turn_call(dot_plain(normed, full_qkv[:, :q_width]), s["cos"], s["sin"], q_width)
+        return (q.reshape(per_chunk, block, q_width),)
+
+    def project(s, tok):
+        normed, kv = project_kv(s, tok)
+        return (normed, kv) + project_q(s, normed)
+
+    def attend(s, q, *kv):
+        attended, lse = attend_call(place, q, kv, *s["seg_fwd"])
         s["attended"], s["lse"] = attended, lse
         attn = dot_cols(attended.reshape(rows, q_width), full_o).astype(BF)
         return attended, lse, attn
@@ -507,22 +745,19 @@
         s["residual"] = own(s["tok"]).astype(F32) + summed
         return (s["residual"] * inverse_rms(s["residual"]) * gain_two).astype(BF)
 
-    def ffn_up(normed_two):
-        return dot_plain(normed_two, full_g), dot_plain(normed_two, full_u)
-
-    def ffn_mid(gate, up, cot):
-        sig = jax.nn.sigmoid(gate)
-        hidden = (gate * sig * up).astype(BF)
-        d_hidden = dot_plain(cot, full_d)
-        d_gate = (d_hidden * up * (sig * (1.0 + gate * (1.0 - sig)))).astype(BF)
-        d_up = (d_hidden * gate * sig).astype(BF)
-        return hidden, d_gate, d_up
+    turned = {}
+
+    def turn_over(weight):
+        return (transpose_call(weight),)
+
+    def ffn_mid(normed_two, cot):
+        return ffn_call(normed_two, cot, full_g, full_u, full_d)
 
     def ffn_back(d_gate, d_up):
-        return ((dot_cols(d_gate, full_g) + dot_cols(d_up, full_u)).astype(BF),)
+        return (product_call((d_gate, d_up), (turned["g"], turned["u"])),)
 
     def ffn_out(hidden):
-        return (dot_cols(hidden, full_d).astype(BF),)
+        return (product_call((hidden,), (turned["d"],)),)
 
     def leave_ffn(s, summed):
         d_norm, s["gain_two"] = norm_back(s["residual"], gain_two, summed)
@@ -536,10 +771,10 @@
         )
 
     def project_back(s, dq, b0, b1, b2, b3):
-        from3 = lax.ppermute(b3, "heads", pairs(parts, 1))
-        from1 = lax.ppermute(b1, "heads", pairs(parts, 1))
+        from3 = lax.ppermute(b3, "core", FLIP)
+        from1 = lax.ppermute(b1, "core", FLIP)
         far = (b2.astype(F32) + from3.astype(F32)).astype(BF)
-        from2 = lax.ppermute(far, "heads", pairs(parts, 2))
+        from2 = lax.ppermute(far, "yy", FLIP)
         d_kv = b0.astype(F32) + from1.astype(F32) + from2.astype(F32)
         d_q = turn_call(dq.reshape(rows, q_width), s["cos"], -s["sin"], q_width)
         d_kv = turn_call(d_kv.reshape(rows, kv_width), s["cos"], -s["sin"], k_width)
@@ -554,105 +789,118 @@
         return lax.psum_scatter(grad, owners, scatter_dimension=0, tiled=True)
 
     def weight_grad(*halves):
-        left = jnp.concatenate(halves[:CHUNKS], axis=0)
-        right = jnp.concatenate(halves[CHUNKS:], axis=0)
+        left = jnp.concatenate(halves[:-CHUNKS], axis=0)
+        right = jnp.concatenate(halves[-CHUNKS:], axis=0)
         return (dot_rows(left, right).astype(BF),)
 
     def of_both(*names):
         return tuple(s[name] for name in names for s in state)
 
-    axes = ("tensor", "heads", "fsdp")
-    clock = Clock()
-    slot = clock.slot
-
-    _, _, attn = attend(first, first["q"])
+    def leave_layer(s, ffn):
+        mine = own(ffn).astype(F32) + s["residual"]
+        ffn = lax.dynamic_update_slice_in_dim(ffn, mine.astype(BF), me * own_rows, 0)
+        s["output"] = lax.psum(ffn, "tensor")
+
+    axes = ("tensor", "core", "yy", "fsdp")
+    first["normed_one"], kv = slot(
+        [], functools.partial(project_kv, first), (first["tok"],)
+    )
+    keys = KeyExchange(kv)
+    (first["q"],) = slot(
+        [keys], functools.partial(project_q, first), (first["normed_one"],)
+    )
+    slot([keys])
+    first["kv"] = keys.result()
+    first["attended"], first["lse"], attn = slot(
+        [], functools.partial(attend, first), (first["q"],) + first["kv"]
+    )
     sum_a0 = LineSum(blocks(attn))
+    second["normed_one"], kv, second["q"] = slot(
+        [sum_a0], functools.partial(project, second), (second["tok"],)
+    )
+    keys = KeyExchange(kv)
+    slot([sum_a0, keys])
+    slot([sum_a0, keys])
+    second["kv"] = keys.result()
+    gather_a0 = LineGather(enter_ffn(first, sum_a0.result()))
     second["attended"], second["lse"], attn = slot(
-        [sum_a0], functools.partial(attend, second), (second["q"],)
+        [gather_a0], functools.partial(attend, second), (second["q"],) + second["kv"]
     )
     sum_a1 = LineSum(blocks(attn))
-    slot([sum_a0])
-    slot([sum_a0])
-    gather_a0 = LineGather(enter_ffn(first, sum_a0.result()))
-    slot([gather_a0])
-    slot([gather_a0, sum_a1])
-    slot([gather_a0, sum_a1])
+    (turned["g"],) = slot([Both(gather_a0, sum_a1)], turn_over, (full_g,))
+    (turned["u"],) = slot([Both(gather_a0, sum_a1)], turn_over, (full_u,))
     first["normed_two"] = gather_a0.result().reshape(rows, width)
-    gate, up = slot([sum_a1], ffn_up, (first["normed_two"],))
+    first["hidden"], first["d_gate"], first["d_up"] = slot(
+        [sum_a1], ffn_mid, (first["normed_two"], first["cot"])
+    )
     gather_a1 = LineGather(enter_ffn(second, sum_a1.result()))
-    first["hidden"], first["d_gate"], first["d_up"] = slot(
-        [gather_a1], ffn_mid, (gate, up, first["cot"])
-    )
     (back,) = slot([gather_a1], ffn_back, (first["d_gate"], first["d_up"]))
     sum_d0 = LineSum(blocks(back))
-    (ffn,) = slot([gather_a1, sum_d0], ffn_out, (first["hidden"],))
-    sum_f0 = LineSum(blocks(ffn))
+    (turned["d"],) = slot([Both(gather_a1, sum_d0)], turn_over, (full_d,))
+    (ffn,) = slot([Both(gather_a1, sum_d0)], ffn_out, (first["hidden"],))
+    leave_layer(first, ffn)
     second["normed_two"] = gather_a1.result().reshape(rows, width)
-    gate, up = slot([sum_d0], ffn_up, (second["normed_two"],))
     second["hidden"], second["d_gate"], second["d_up"] = slot(
-        [sum_d0], ffn_mid, (gate, up, second["cot"])
+        [sum_d0], ffn_mid, (second["normed_two"], second["cot"])
     )
     gather_d0 = LineGather(leave_ffn(first, sum_d0.result()))
     (back,) = slot([gather_d0], ffn_back, (second["d_gate"], second["d_up"]))
     sum_d1 = LineSum(blocks(back))
     (grad,) = slot(
-        [gather_d0, sum_d1],
+        [Both(gather_d0, sum_d1)],
         weight_grad,
-        of_both("cot", "hidden"),
+        (cotangent.reshape(seqs * block, width),) + of_both("hidden"),
     )
     down_grad = scattered(grad)
-    (grad,) = slot([gather_d0, sum_d1], weight_grad, of_both("normed_two", "d_gate"))
+    (grad,) = slot([Both(gather_d0, sum_d1)], weight_grad, of_both("normed_two", "d_gate"))
     gate_grad = scattered(grad)
     first["d_attn"] = gather_d0.result().reshape(rows, width)
-    (grad,) = slot([sum_d1], weight_grad, of_both("normed_two", "d_up"))
-    up_grad = scattered(grad)
+    pieces = slot([sum_d1], functools.partial(attend_back, first), (first["d_attn"],))
     gather_d1 = LineGather(leave_ffn(second, sum_d1.result()))
     gains_two = Butterfly(first["gain_two"] + second["gain_two"], axes)
-    pieces = slot(
-        [gather_d1, gains_two], functools.partial(attend_back, first), (first["d_attn"],)
-    )
     first["d_qkv"], back = slot(
-        [gather_d1, sum_f0, gains_two], functools.partial(project_back, first), pieces
+        [gather_d1, gains_two], functools.partial(project_back, first), pieces
     )
     sum_n0 = LineSum(blocks(back))
-    (ffn,) = slot([gather_d1, sum_f0, gains_two], ffn_out, (second["hidden"],))
+    (grad,) = slot(
+        [Both(gather_d1, sum_n0), gains_two], weight_grad, of_both("normed_two", "d_up")
+    )
+    up_grad = scattered(grad)
+    (ffn,) = slot([Both(gather_d1, sum_n0), gains_two], ffn_out, (second["hidden"],))
     sum_f1 = LineSum(blocks(ffn))
     second["d_attn"] = gather_d1.result().reshape(rows, width)
     pieces = slot(
-        [sum_f0, gains_two], functools.partial(attend_back, second), (second["d_attn"],)
-    )
-    clock.expect(down_grad)
-    gather_f0 = LineGather((first["residual"] + sum_f0.result()).astype(BF))
+        [sum_n0, gains_two], functools.partial(attend_back, second), (second["d_attn"],)
+    )
+    gather_n0 = LineGather(leave_attention(first, sum_n0.result()))
     second["d_qkv"], back = slot(
-        [gather_f0, gains_two], functools.partial(project_back, second), pieces
+        [gather_n0, gains_two], functools.partial(project_back, second), pieces
     )
     sum_n1 = LineSum(blocks(back))
+    clock.expect(first["output"])
     (grad,) = slot(
-        [gather_f0, sum_n0], weight_grad, of_both("normed_one", "d_qkv")
+        [Both(gather_n0, sum_n1)], weight_grad, of_both("normed_one", "d_qkv")
     )
     qkv_grad = scattered(grad)
     for s in state:
         s["attended_rows"] = s["attended"].reshape(rows, q_width)
-    (grad,) = slot([gather_f0, sum_n0], weight_grad, of_both("d_attn", "attended_rows"))
+    (grad,) = slot(
+        [Both(gather_n0, sum_n1)], weight_grad, of_both("d_attn", "attended_rows")
+    )
     o_grad = scattered(grad)
-    first["output"] = gather_f0.result()
-    slot([sum_n0])
-    gather_n0 = LineGather(leave_attention(first, sum_n0.result()))
-    slot([gather_n0])
-    slot([gather_n0, sum_n1])
-    slot([gather_n0, sum_n1])
     first["input_grad"] = gather_n0.result()
-    clock.expect(gate_grad)
     slot([sum_n1])
     gather_n1 = LineGather(leave_attention(second, sum_n1.result()))
     gains_one = Butterfly(first["gain_one"] + second["gain_one"], axes)
     slot([gather_n1, gains_one])
-    slot([gather_n1, sum_f1, gains_one])
-    slot([gather_n1, sum_f1, gains_one])
+    clock.expect(down_grad)
+    slot([Both(gather_n1, sum_f1), gains_one])
+    slot([Both(gather_n1, sum_f1), gains_one])
     second["input_grad"] = gather_n1.result()
+    clock.expect(gate_grad)
     slot([sum_f1, gains_one])
+    gather_f1 = LineGather((second["residual"] + sum_f1.result()).astype(BF))
     clock.expect(up_grad)
-    gather_f1 = LineGather((second["residual"] + sum_f1.result()).astype(BF))
     slot([gather_f1, gains_one])
     slot([gather_f1])
     slot([gather_f1])
@@ -692,9 +940,13 @@
 
 
 def solution(mesh):
-    rows = P("fsdp", "heads", None)
-    matrix = P(("fsdp", "heads"), "tensor")
-    vector = P(("fsdp", "heads"))
+    sizes = mesh.shape
+    split = (sizes["fsdp"], sizes["heads"] // 2, 2, sizes["tensor"])
+    mesh = jax.sharding.Mesh(mesh.devices.reshape(split), ("fsdp", "yy", "core", "tensor"))
+    heads = ("yy", "core")
+    rows = P("fsdp", heads, None)
+    matrix = P(("fsdp",) + heads, "tensor")
+    vector = P(("fsdp",) + heads)
     return jax.shard_map(
         per_device,
         mesh=mesh,

time: 898 us -> 851 us (0.948)
  Pallas kernels: 73.8 us -> 217 us
  matrix products: 204 us -> 90.6 us
  starting transfers between devices: 216 us -> 172 us
  local copies, waits for them, and re-layouts: 47.4 us -> 31.8 us
  other arithmetic: 117 us -> 105 us
    pallas_call x0 -> x17, Pallas kernels: none -> 143 us  [the longest x4 45.6 us: product_call(): pl.pallas_call(functools.partial(product_kernel, count), grid=(width // t...]
    dot_general x12 -> x6, matrix products: 84 us -> 23.6 us  [dot_plain(): return jnp.dot(left_in, right_in, preferred_element_type=F32)]
    dot_general x10 -> x4, matrix products: 71 us -> 15 us  [dot_cols(): lax.dot_general(left_in, right_in, (((1,), (1,)), ((), ())), preferred_el...]
    dynamic_update_slice x32 -> x1, other arithmetic: 45.1 us -> 1.95 us  [leave_layer(): lax.dynamic_update_slice_in_dim(ffn, mine.astype(BF), me * own_rows, 0)]
    ppermute x106 -> x81, starting transfers between devices: 210 us -> 167 us  [slot(): moved = [lax.ppermute(g, s[1], s[2]) for g, s in zip(gated, flat)]]
    select_n x0 -> x12, other arithmetic: none -> 28.3 us  [sends(): value = jnp.where(rank >= first, whole[0], part[0])]
    convert_element_type x1 -> x9, other arithmetic: 2.21 us -> 14.5 us  [the longest x2 6.14 us: leave_ffn(): return s['d_resid'].astype(BF)]
    squeeze x8 -> x1, local copies, waits for them, and re-layouts: 10.5 us -> 1.01 us  [pick(): lax.dynamic_index_in_dim(self.parts, jnp.clip(j, 0, last), 0, keepdims=Fa...]
  transfers between devices with their start and end apart: 128 -> 97, of which waited for: 43 -> 45; matrix products, arithmetic and copies ran while one was open for 38% -> 24% of each run, Pallas kernels for 8% -> 25%
where the time goes in v3:
time: 851 us; the launch traced here: 838 us
  Pallas kernels  217 us (25%)
  waiting for transfers between devices  205 us (24%)
  starting transfers between devices  172 us (20%)
  other arithmetic  105 us (12%)
  matrix products  90.6 us (11%)
  local copies, waits for them, and re-layouts  31.8 us (4%)
  between operations  16.1 us (2%)
    ppermute x81, waiting for transfers between devices, slot(): moved = [lax.ppermute(g, s[1], s[2]) for g, s in zip(gated, flat)]  186 us
    ppermute x81, starting transfers between devices, slot(): moved = [lax.ppermute(g, s[1], s[2]) for g, s in zip(gated, flat)]  167 us
    dot_general x5, matrix products, dot_rows(): lax.dot_general(left_in, right_in, (((0,), (0,)), ((), ())), preferred_el...  52 us
    pallas_call x4, Pallas kernels, product_call(): pl.pallas_call(functools.partial(product_kernel, count), grid=(width // t...  45.6 us
    pallas_call x2, Pallas kernels, ffn_call(): pl.pallas_call(ffn_kernel, grid=(units // tile,), in_specs=[whole, whole,...  41 us
    pallas_call x2, Pallas kernels, attend_back_call(): pl.pallas_call(functools.partial(attend_back_kernel, group), grid_spec=pl...  33.1 us
    pallas_call x3, Pallas kernels, transpose_call(): pl.pallas_call(transpose_kernel, grid=(rows // tile,), in_specs=[pl.Block...  29.9 us
    select_n x12, other arithmetic, sends(): value = jnp.where(rank >= first, whole[0], part[0])  28.3 us
  transfers between devices with their start and end apart: 97, of which 45 were waited for; matrix products, arithmetic and copies ran while one was open for 24% of the time, Pallas kernels for 25%

profile of v3, /device:TPU:0, one launch (start us, length us, event | category | flops | bytes accessed | tf_op | source)
XLA Modules:
  0.0 838.4 jit_solution(12373796591445216873)
XLA Ops:
  38.1 12.5 %all-gather.5.cloned.1.call-done = bf16[2048,896]{1,0:T(8,128)(2,1)} async-done(((bf16[256,896]{1,0:T(8,128)(2,1)}), bf16[2048,896]{1,0:T(8,128)(2,1)}) %all-gather.5.cloned.1.call-update) | async-done | bytes 3670032 | tf_op jit(solution)/shard_map/all_gather | solution.py:671
  80.2 11.7 %attend.2 = (bf16[2,256,512]{2,1,0:T(8,128)(2,1)}, f32[2,8,256]{2,1,0:T(8,128)}) custom-call(s32[5]{0:T(128)} %stack.29.place_ref, bf16[2,256,512]{2,1,0:T(8,128)(2,1)} %bitcast.315, bf16[2,256,256]{2,1,0:T(8,128)(2,1)} %bitcast.323, bf16[2,256,256]{2,1,0:T(8,128)(2,1)} %copy-done.74, bf16[2,256,256]{2,1,0:T(8,128)(2,1)} %copy-done.73, ...), custom_call_target="tpu_custom_call" | custom-call | flops 4294967296 | bytes 1572864 | tf_op jit(solution)/shard_map/attend/pallas_call | solution.py:472
  122.1 8.3 collective-permute-done.10
  134.1 6.0 collective-permute-start.14
  142.9 6.2 collective-permute-done.14
  161.1 11.4 %attend.3 = (bf16[2,256,512]{2,1,0:T(8,128)(2,1)}, f32[2,8,256]{2,1,0:T(8,128)}) custom-call(s32[5]{0:T(128)} %stack.29.place_ref, bf16[2,256,512]{2,1,0:T(8,128)(2,1)} %bitcast.313, bf16[2,256,256]{2,1,0:T(8,128)(2,1)} %bitcast.317, bf16[2,256,256]{2,1,0:T(8,128)(2,1)} %copy-done.72, bf16[2,256,256]{2,1,0:T(8,128)(2,1)} %copy-done.71, ...), custom_call_target="tpu_custom_call" | custom-call | flops 4294967296 | bytes 1572864 | tf_op jit(solution)/shard_map/attend/pallas_call | solution.py:472
  185.9 10.0 %turn_over.3.refs_2_ = bf16[2048,2048]{1,0:T(8,128)(2,1)} custom-call(bf16[2048,2048]{1,0:T(8,128)(2,1)} %all-gather.7.cloned.1.call-done.x_ref.g_ref), custom_call_target="tpu_custom_call" | custom-call | bytes 16777216 | tf_op jit(solution)/shard_map/turn_over/pallas_call | solution.py:377
  211.0 10.0 %turn_over.4.refs_3_ = bf16[2048,2048]{1,0:T(8,128)(2,1)} custom-call(bf16[2048,2048]{1,0:T(8,128)(2,1)} %all-gather.9.cloned.1.call-done.x_ref.u_ref), custom_call_target="tpu_custom_call" | custom-call | bytes 16777216 | tf_op jit(solution)/shard_map/turn_over/pallas_call | solution.py:377
  233.7 20.5 %ffn.2 = (bf16[512,2048]{1,0:T(8,128)(2,1)}, bf16[512,2048]{1,0:T(8,128)(2,1)}, bf16[512,2048]{1,0:T(8,128)(2,1)}) custom-call(bf16[512,2048]{1,0:T(8,128)(2,1)} %bitcast.292, bf16[512,2048]{1,0:T(8,128)(2,1)} %bitcast.290, bf16[2048,2048]{1,0:T(8,128)(2,1)} %all-gather.7.cloned.1.call-done.x_ref.g_ref, ...), custom_call_target="tpu_custom_call" | custom-call | flops 12884901888 | bytes 31457280 | tf_op jit(solution)/shard_map/ffn/pallas_call | solution.py:326
  263.8 13.8 %product.4 = bf16[512,2048]{1,0:T(8,128)(2,1)} custom-call(bf16[512,2048]{1,0:T(8,128)(2,1)} %get-tuple-element.248.refs_0_, bf16[512,2048]{1,0:T(8,128)(2,1)} %get-tuple-element.271.refs_1_, bf16[2048,2048]{1,0:T(8,128)(2,1)} %turn_over.3.refs_2_, bf16[2048,2048]{1,0:T(8,128)(2,1)} %turn_over.4.refs_3_), custom_call_target="tpu_custom_call" | custom-call | flops 8589934592 | bytes 20971520 | tf_op jit(solution)/shard_map/product/pallas_call | solution.py:354
  287.1 9.9 %turn_over.5.refs_1_ = bf16[2048,2048]{1,0:T(8,128)(2,1)} custom-call(bf16[2048,2048]{1,0:T(8,128)(2,1)} %all-gather.11.cloned.1.call-done.d_ref.x_ref), custom_call_target="tpu_custom_call" | custom-call | bytes 16777216 | tf_op jit(solution)/shard_map/turn_over/pallas_call | solution.py:377
  306.7 8.8 %product.5 = bf16[512,2048]{1,0:T(8,128)(2,1)} custom-call(bf16[512,2048]{1,0:T(8,128)(2,1)} %get-tuple-element.242.refs_0_, bf16[2048,2048]{1,0:T(8,128)(2,1)} %turn_over.5.refs_1_), custom_call_target="tpu_custom_call" | custom-call | flops 4294967296 | bytes 10485760 | tf_op jit(solution)/shard_map/product/pallas_call | solution.py:354
  329.8 20.5 %ffn.3 = (bf16[512,2048]{1,0:T(8,128)(2,1)}, bf16[512,2048]{1,0:T(8,128)(2,1)}, bf16[512,2048]{1,0:T(8,128)(2,1)}) custom-call(bf16[512,2048]{1,0:T(8,128)(2,1)} %bitcast.297, bf16[512,2048]{1,0:T(8,128)(2,1)} %bitcast.288, bf16[2048,2048]{1,0:T(8,128)(2,1)} %all-gather.7.cloned.1.call-done.x_ref.g_ref, ...), custom_call_target="tpu_custom_call" | custom-call | flops 12884901888 | bytes 31457280 | tf_op jit(solution)/shard_map/ffn/pallas_call | solution.py:326
  360.9 14.2 %product.6 = bf16[512,2048]{1,0:T(8,128)(2,1)} custom-call(bf16[512,2048]{1,0:T(8,128)(2,1)} %get-tuple-element.249.refs_0_, bf16[512,2048]{1,0:T(8,128)(2,1)} %get-tuple-element.272.refs_1_, bf16[2048,2048]{1,0:T(8,128)(2,1)} %turn_over.3.refs_2_, bf16[2048,2048]{1,0:T(8,128)(2,1)} %turn_over.4.refs_3_), custom_call_target="tpu_custom_call" | custom-call | flops 8589934592 | bytes 20971520 | tf_op jit(solution)/shard_map/product/pallas_call | solution.py:354
  375.1 5.6 collective-permute-done.33.refs_1_
  387.1 13.8 %convolution_convert_fusion.2 = bf16[2048,2048]{1,0:T(8,128)(2,1)} fusion(bf16[1024,2048]{1,0:T(8,128)(2,1)} %bitcast.287, bf16[512,2048]{1,0:T(8,128)(2,1)S(1)} %copy-done.82, bf16[512,2048]{1,0:T(8,128)(2,1)} %get-tuple-element.242.refs_0_), kind=kOutput, calls=%fused_computation.2 | convolution fusion | flops 8602517504 | bytes 16777216 | tf_op jit(solution)/shard_map/dot_general | solution.py:36
  404.2 21.8 %collective-permute-done.35.refs_2_ = bf16[128,2048]{1,0:T(8,128)(2,1)S(1)} collective-permute-done((bf16[128,2048]{1,0:T(8,128)(2,1)}, bf16[128,2048]{1,0:T(8,128)(2,1)S(1)}, u32[]{:S(2)}, u32[]{:S(2)}) %collective-permute-start.35) | collective-permute-done | bytes 524320 | tf_op jit(solution)/shard_map/ppermute | solution.py:215
  426.0 11.5 %collective-permute-done.36.refs_5_ = bf16[128,2048]{1,0:T(8,128)(2,1)S(1)} collective-permute-done((bf16[128,2048]{1,0:T(8,128)(2,1)}, bf16[128,2048]{1,0:T(8,128)(2,1)S(1)}, u32[]{:S(2)}, u32[]{:S(2)}) %collective-permute-start.36) | collective-permute-done | bytes 524320 | tf_op jit(solution)/shard_map/ppermute | solution.py:215
  438.8 13.7 %convolution_convert_fusion.1 = bf16[2048,2048]{1,0:T(8,128)(2,1)} fusion(bf16[512,2048]{1,0:T(8,128)(2,1)} %bitcast.298, bf16[512,2048]{1,0:T(8,128)(2,1)S(1)} %bitcast.293, bf16[512,2048]{1,0:T(8,128)(2,1)} %get-tuple-element.249.refs_0_, bf16[512,2048]{1,0:T(8,128)(2,1)} %get-tuple-element.248.refs_0_), kind=kOutput, calls=%fused_computation.1 | convolution fusion | flops 8610906112 | bytes 16777216 | tf_op jit(solution)/shard_map/dot_general | solution.py:36
  459.4 6.9 collective-permute-done.37.refs_3_
  485.7 16.2 %attend_back.2 = (bf16[2,256,512]{2,1,0:T(8,128)(2,1)}, bf16[2,256,256]{2,1,0:T(8,128)(2,1)}, bf16[2,256,256]{2,1,0:T(8,128)(2,1)}, bf16[2,256,256]{2,1,0:T(8,128)(2,1)}, bf16[2,256,256]{2,1,0:T(8,128)(2,1)}) custom-call(s32[5]{0:T(128)} %stack.29.place_ref, bf16[2,256,512]{2,1,0:T(8,128)(2,1)} %bitcast.316, bf16[2,256,256]{2,1,0:T(8,128)(2,1)} %bitcast.324, ...), custom_call_target="tpu_custom_call" | custom-call | flops 10737418240 | bytes 3145728 | tf_op jit(solution)/shard_map/attend_back/pallas_call | solution.py:592
  534.0 11.4 %convolution_convert_fusion = bf16[2048,2048]{1,0:T(8,128)(2,1)} fusion(bf16[512,2048]{1,0:T(8,128)(2,1)S(1)} %bitcast.299, bf16[512,2048]{1,0:T(8,128)(2,1)S(1)} %bitcast.294, bf16[512,2048]{1,0:T(8,128)(2,1)S(1)} %copy-done.84, bf16[512,2048]{1,0:T(8,128)(2,1)S(1)} %copy-done.83), kind=kOutput, calls=%fused_computation | convolution fusion | flops 8610906112 | bytes 16777216 | tf_op jit(solution)/shard_map/dot_general | solution.py:36
  555.9 8.6 %collective-permute-done.49 = f32[2048]{0:T(1024)S(1)} collective-permute-done((f32[2048]{0:T(1024)S(1)}, f32[2048]{0:T(1024)S(1)}, u32[]{:S(2)}, u32[]{:S(2)}) %collective-permute-start.49) | collective-permute-done | bytes 8224 | tf_op jit(solution)/shard_map/ppermute | solution.py:215
  573.3 8.9 %product.7 = bf16[512,2048]{1,0:T(8,128)(2,1)} custom-call(bf16[512,2048]{1,0:T(8,128)(2,1)} %get-tuple-element.273.refs_0_, bf16[2048,2048]{1,0:T(8,128)(2,1)} %turn_over.5.refs_1_), custom_call_target="tpu_custom_call" | custom-call | flops 4294967296 | bytes 10485760 | tf_op jit(solution)/shard_map/product/pallas_call | solution.py:354
  599.2 16.9 %attend_back.3 = (bf16[2,256,512]{2,1,0:T(8,128)(2,1)}, bf16[2,256,256]{2,1,0:T(8,128)(2,1)}, bf16[2,256,256]{2,1,0:T(8,128)(2,1)}, bf16[2,256,256]{2,1,0:T(8,128)(2,1)}, bf16[2,256,256]{2,1,0:T(8,128)(2,1)}) custom-call(s32[5]{0:T(128)} %stack.29.place_ref, bf16[2,256,512]{2,1,0:T(8,128)(2,1)} %bitcast.314, bf16[2,256,256]{2,1,0:T(8,128)(2,1)} %bitcast.318, ...), custom_call_target="tpu_custom_call" | custom-call | flops 10737418240 | bytes 3145728 | tf_op jit(solution)/shard_map/attend_back/pallas_call | solution.py:592
  655.7 7.8 fusion.29
  681.0 8.9 %collective-permute-done.64.refs_3_ = bf16[128,2048]{1,0:T(8,128)(2,1)S(1)} collective-permute-done((bf16[128,2048]{1,0:T(8,128)(2,1)}, bf16[128,2048]{1,0:T(8,128)(2,1)S(1)}, u32[]{:S(2)}, u32[]{:S(2)}) %collective-permute-start.64) | collective-permute-done | bytes 524320 | tf_op jit(solution)/shard_map/ppermute | solution.py:215
  699.2 7.7 collective-permute-done.66
  722.3 8.8 %collective-permute-done.70 = f32[2048]{0:T(1024)S(1)} collective-permute-done((f32[2048]{0:T(1024)S(1)}, f32[2048]{0:T(1024)S(1)}, u32[]{:S(2)}, u32[]{:S(2)}) %collective-permute-start.70) | collective-permute-done | bytes 8224 | tf_op jit(solution)/shard_map/ppermute | solution.py:215
  738.4 8.3 collective-permute-done.73
  786.8 5.8 collective-permute-done.81.refs_4_
  813.2 5.6 maximum_convert_fusion
  (500 shorter events, 470.3 us)
Async XLA Ops:
  7.2 43.5 %all-gather.5.cloned.1.call-start = ((), (), s32[]{:S(2)}) async-start(), calls=%async_computation.5 | async-start | bytes 4128768 | tf_op jit(solution)/shard_map/all_gather | solution.py:671
  10.7 168.3 %all-gather.7.cloned.1.call-start = ((), (), s32[]{:S(2)}) async-start(), calls=%async_computation.6 | async-start | bytes 9437184 | tf_op jit(solution)/shard_map/all_gather | solution.py:671
  11.5 189.3 %all-gather.9.cloned.1.call-start = ((), (), s32[]{:S(2)}) async-start(), calls=%async_computation.7 | async-start | bytes 9437184 | tf_op jit(solution)/shard_map/all_gather | solution.py:671
  12.2 221.5 %all-gather.11.cloned.1.call-start = ((), (), s32[]{:S(2)}) async-start(), calls=%async_computation.8 | async-start | bytes 9437184 | tf_op jit(solution)/shard_map/all_gather | solution.py:671
  12.8 637.0 %all-reduce.2.cloned.1.call-start = ((), (), s32[]{:S(2)}) async-start(), calls=%async_computation.9 | async-start | bytes 4194304 | tf_op jit(solution)/shard_map/psum | solution.py:802
  96.0 18.5 %collective-permute-start.8 = (bf16[128,2048]{1,0:T(8,128)(2,1)}, bf16[128,2048]{1,0:T(8,128)(2,1)S(1)}, u32[]{:S(2)}, u32[]{:S(2)}) collective-permute-start(bf16[128,2048]{1,0:T(8,128)(2,1)} %get-tuple-element.186), channel_id=1, source_target_pairs={{0,1},{4,5},{8,9},{12,13},{16,17},{20,21},{24,25},{28,29}} | collective-permute-start | bytes 1572872 | tf_op jit(solution)/shard_map/ppermute | solution.py:215
  157.5 18.0 %collective-permute-start.17 = (bf16[128,2048]{1,0:T(8,128)(2,1)}, bf16[128,2048]{1,0:T(8,128)(2,1)}, u32[]{:S(2)}, u32[]{:S(2)}) collective-permute-start(bf16[128,2048]{1,0:T(8,128)(2,1)} %multiply_convert_fusion.1.refs_0_), channel_id=1, source_target_pairs={{0,1},{1,2},{2,3},{4,5},{5,6},{6,7},{8,9},{9,10},{10,11},{12,13},{... | collective-permute-start | bytes 1572872 | tf_op jit(solution)/shard_map/ppermute | solution.py:215
  200.8 20.2 %collective-permute-start.21 = (bf16[128,2048]{1,0:T(8,128)(2,1)}, bf16[128,2048]{1,0:T(8,128)(2,1)}, u32[]{:S(2)}, u32[]{:S(2)}) collective-permute-start(bf16[128,2048]{1,0:T(8,128)(2,1)} %get-tuple-element.208), channel_id=1, source_target_pairs={{0,1},{1,2},{2,3},{4,5},{5,6},{6,7},{8,9},{9,10},{10,11},{12,13},{... | collective-permute-start | bytes 1572872 | tf_op jit(solution)/shard_map/ppermute | solution.py:215
  227.0 27.3 %collective-permute-start.23 = (bf16[128,2048]{1,0:T(8,128)(2,1)}, bf16[128,2048]{1,0:T(8,128)(2,1)}, u32[]{:S(2)}, u32[]{:S(2)}) collective-permute-start(bf16[128,2048]{1,0:T(8,128)(2,1)} %get-tuple-element.211), channel_id=1, source_target_pairs={{0,1},{1,2},{2,3},{4,5},{5,6},{6,7},{8,9},{9,10},{10,11},{12,13},{... | collective-permute-start | bytes 1572872 | tf_op jit(solution)/shard_map/ppermute | solution.py:215
  232.4 21.8 %collective-permute-start.24 = (bf16[128,2048]{1,0:T(8,128)(2,1)}, bf16[128,2048]{1,0:T(8,128)(2,1)}, u32[]{:S(2)}, u32[]{:S(2)}) collective-permute-start(bf16[128,2048]{1,0:T(8,128)(2,1)} %get-tuple-element.212), channel_id=1, source_target_pairs={{3,2},{2,1},{1,0},{7,6},{6,5},{5,4},{11,10},{10,9},{9,8},{15,14},{... | collective-permute-start | bytes 1572872 | tf_op jit(solution)/shard_map/ppermute | solution.py:215
  257.9 19.7 %collective-permute-start.25 = (bf16[128,2048]{1,0:T(8,128)(2,1)S(1)}, bf16[128,2048]{1,0:T(8,128)(2,1)S(1)}, u32[]{:S(2)}, u32[]{:S(2)}) collective-permute-start(bf16[128,2048]{1,0:T(8,128)(2,1)S(1)} %multiply_convert_fusion.refs_0_), channel_id=1, source_target_pairs={{0,1},{1,2},{2,3},{4,5},{5,6},{6,7},{8,9},{9,10},{10,11},{12,13},{... | collective-permute-start | bytes 1572872 | tf_op jit(solution)/shard_map/ppermute | solution.py:215
  324.4 25.9 %collective-permute-start.31 = (bf16[128,2048]{1,0:T(8,128)(2,1)}, bf16[128,2048]{1,0:T(8,128)(2,1)}, u32[]{:S(2)}, u32[]{:S(2)}) collective-permute-start(bf16[128,2048]{1,0:T(8,128)(2,1)} %get-tuple-element.228), channel_id=1, source_target_pairs={{0,1},{1,2},{2,3},{4,5},{5,6},{6,7},{8,9},{9,10},{10,11},{12,13},{... | collective-permute-start | bytes 1572872 | tf_op jit(solution)/shard_map/ppermute | solution.py:215
  328.4 21.9 %collective-permute-start.32 = (bf16[128,2048]{1,0:T(8,128)(2,1)}, bf16[128,2048]{1,0:T(8,128)(2,1)}, u32[]{:S(2)}, u32[]{:S(2)}) collective-permute-start(bf16[128,2048]{1,0:T(8,128)(2,1)} %get-tuple-element.229), channel_id=1, source_target_pairs={{3,2},{2,1},{1,0},{7,6},{6,5},{5,4},{11,10},{10,9},{9,8},{15,14},{... | collective-permute-start | bytes 1572872 | tf_op jit(solution)/shard_map/ppermute | solution.py:215
  329.7 403.5 %reduce-scatter.6.cloned.1.call-start = ((), (), s32[]{:S(2)}) async-start(), calls=%async_computation.10 | async-start | bytes 9437184 | tf_op jit(solution)/shard_map/reduce_scatter | solution.py:789
  355.0 25.6 %collective-permute-start.33 = (bf16[128,2048]{1,0:T(8,128)(2,1)}, bf16[128,2048]{1,0:T(8,128)(2,1)S(1)}, u32[]{:S(2)}, u32[]{:S(2)}) collective-permute-start(bf16[128,2048]{1,0:T(8,128)(2,1)} %get-tuple-element.236.refs_0_), channel_id=1, source_target_pairs={{0,1},{1,2},{2,3},{4,5},{5,6},{6,7},{8,9},{9,10},{10,11},{12,13},{... | collective-permute-start | bytes 1572872 | tf_op jit(solution)/shard_map/ppermute | solution.py:215
  359.6 25.0 %collective-permute-start.34 = (bf16[128,2048]{1,0:T(8,128)(2,1)}, bf16[128,2048]{1,0:T(8,128)(2,1)S(1)}, u32[]{:S(2)}, u32[]{:S(2)}) collective-permute-start(bf16[128,2048]{1,0:T(8,128)(2,1)} %get-tuple-element.236.refs_0_), channel_id=1, source_target_pairs={{3,2},{2,1},{1,0},{7,6},{6,5},{5,4},{11,10},{10,9},{9,8},{15,14},{... | collective-permute-start | bytes 1572872 | tf_op jit(solution)/shard_map/ppermute | solution.py:215
  400.9 362.5 %reduce-scatter.8.cloned.1.call-start = ((), (), s32[]{:S(2)}) async-start(), calls=%async_computation.11 | async-start | bytes 9437184 | tf_op jit(solution)/shard_map/reduce_scatter | solution.py:789
  400.9 25.0 %collective-permute-start.35 = (bf16[128,2048]{1,0:T(8,128)(2,1)}, bf16[128,2048]{1,0:T(8,128)(2,1)S(1)}, u32[]{:S(2)}, u32[]{:S(2)}) collective-permute-start(bf16[128,2048]{1,0:T(8,128)(2,1)} %get-tuple-element.239), channel_id=1, source_target_pairs={{0,1},{1,2},{2,3},{4,5},{5,6},{6,7},{8,9},{9,10},{10,11},{12,13},{... | collective-permute-start | bytes 1572872 | tf_op jit(solution)/shard_map/ppermute | solution.py:215
  402.9 34.6 %collective-permute-start.36 = (bf16[128,2048]{1,0:T(8,128)(2,1)}, bf16[128,2048]{1,0:T(8,128)(2,1)S(1)}, u32[]{:S(2)}, u32[]{:S(2)}) collective-permute-start(bf16[128,2048]{1,0:T(8,128)(2,1)} %get-tuple-element.240), channel_id=1, source_target_pairs={{1,0},{2,1},{3,2},{5,4},{6,5},{7,6},{9,8},{10,9},{11,10},{13,12},{... | collective-permute-start | bytes 1572872 | tf_op jit(solution)/shard_map/ppermute | solution.py:215
  452.6 325.2 %reduce-scatter.10.cloned.1.call-start = ((), (), s32[]{:S(2)}) async-start(), calls=%async_computation.12 | async-start | bytes 9437184 | tf_op jit(solution)/shard_map/reduce_scatter | solution.py:789
  477.1 24.8 %collective-permute-start.39 = (bf16[128,2048]{1,0:T(8,128)(2,1)}, bf16[128,2048]{1,0:T(8,128)(2,1)}, u32[]{:S(2)}, u32[]{:S(2)}) collective-permute-start(bf16[128,2048]{1,0:T(8,128)(2,1)} %get-tuple-element.250), channel_id=1, source_target_pairs={{0,1},{1,2},{2,3},{4,5},{5,6},{6,7},{8,9},{9,10},{10,11},{12,13},{... | collective-permute-start | bytes 1572872 | tf_op jit(solution)/shard_map/ppermute | solution.py:215
  480.7 21.2 %collective-permute-start.40 = (bf16[128,2048]{1,0:T(8,128)(2,1)}, bf16[128,2048]{1,0:T(8,128)(2,1)}, u32[]{:S(2)}, u32[]{:S(2)}) collective-permute-start(bf16[128,2048]{1,0:T(8,128)(2,1)} %get-tuple-element.251), channel_id=1, source_target_pairs={{3,2},{2,1},{1,0},{7,6},{6,5},{5,4},{11,10},{10,9},{9,8},{15,14},{... | collective-permute-start | bytes 1572872 | tf_op jit(solution)/shard_map/ppermute | solution.py:215
  545.4 254.0 %reduce-scatter.14.cloned.1.call-start = ((), (), s32[]{:S(2)}) async-start(), calls=%async_computation.14 | async-start | bytes 2359296 | tf_op jit(solution)/shard_map/reduce_scatter | solution.py:789
  545.5 19.1 %collective-permute-start.47 = (bf16[128,2048]{1,0:T(8,128)(2,1)}, bf16[128,2048]{1,0:T(8,128)(2,1)}, u32[]{:S(2)}, u32[]{:S(2)}) collective-permute-start(bf16[128,2048]{1,0:T(8,128)(2,1)} %get-tuple-element.266), channel_id=1, source_target_pairs={{0,1},{1,2},{2,3},{4,5},{5,6},{6,7},{8,9},{9,10},{10,11},{12,13},{... | collective-permute-start | bytes 1572872 | tf_op jit(solution)/shard_map/ppermute | solution.py:215
  591.0 25.1 %collective-permute-start.55 = (f32[2048]{0:T(1024)S(1)}, f32[2048]{0:T(1024)S(1)}, u32[]{:S(2)}, u32[]{:S(2)}) collective-permute-start(f32[2048]{0:T(1024)S(1)} %add.463), channel_id=1, source_target_pairs={{0,8},{8,0},{1,9},{9,1},{2,10},{10,2},{3,11},{11,3},{4,12},{12,4},... | collective-permute-start | bytes 24584 | tf_op jit(solution)/shard_map/ppermute | solution.py:215
  591.3 24.8 %collective-permute-start.53 = (bf16[128,2048]{1,0:T(8,128)(2,1)}, bf16[128,2048]{1,0:T(8,128)(2,1)}, u32[]{:S(2)}, u32[]{:S(2)}) collective-permute-start(bf16[128,2048]{1,0:T(8,128)(2,1)} %get-tuple-element.277), channel_id=1, source_target_pairs={{0,1},{1,2},{2,3},{4,5},{5,6},{6,7},{8,9},{9,10},{10,11},{12,13},{... | collective-permute-start | bytes 1572872 | tf_op jit(solution)/shard_map/ppermute | solution.py:215
  594.0 22.1 %collective-permute-start.54 = (bf16[128,2048]{1,0:T(8,128)(2,1)}, bf16[128,2048]{1,0:T(8,128)(2,1)}, u32[]{:S(2)}, u32[]{:S(2)}) collective-permute-start(bf16[128,2048]{1,0:T(8,128)(2,1)} %get-tuple-element.278), channel_id=1, source_target_pairs={{3,2},{2,1},{1,0},{7,6},{6,5},{5,4},{11,10},{10,9},{9,8},{15,14},{... | collective-permute-start | bytes 1572872 | tf_op jit(solution)/shard_map/ppermute | solution.py:215
  624.5 25.4 %collective-permute-start.58 = (f32[2048]{0:T(1024)S(1)}, f32[2048]{0:T(1024)S(1)}, u32[]{:S(2)}, u32[]{:S(2)}) collective-permute-start(f32[2048]{0:T(1024)S(1)} %add.468), channel_id=1, source_target_pairs={{0,16},{16,0},{1,17},{17,1},{2,18},{18,2},{3,19},{19,3},{4,20},{20... | collective-permute-start | bytes 24584 | tf_op jit(solution)/shard_map/ppermute | solution.py:215
  626.5 18.0 %collective-permute-start.56 = (bf16[128,2048]{1,0:T(8,128)(2,1)}, bf16[128,2048]{1,0:T(8,128)(2,1)}, u32[]{:S(2)}, u32[]{:S(2)}) collective-permute-start(bf16[128,2048]{1,0:T(8,128)(2,1)} %fusion.48.refs_0_), channel_id=1, source_target_pairs={{0,1},{1,2},{2,3},{4,5},{5,6},{6,7},{8,9},{9,10},{10,11},{12,13},{... | collective-permute-start | bytes 1572872 | tf_op jit(solution)/shard_map/ppermute | solution.py:215
  677.9 123.5 %reduce-scatter.12.cloned.1.call-start = ((), (), s32[]{:S(2)}) async-start(), calls=%async_computation.13 | async-start | bytes 3538944 | tf_op jit(solution)/shard_map/reduce_scatter | solution.py:789
  792.6 18.5 %collective-permute-start.83 = (bf16[128,2048]{1,0:T(8,128)(2,1)S(1)}, bf16[128,2048]{1,0:T(8,128)(2,1)}, u32[]{:S(2)}, u32[]{:S(2)}) collective-permute-start(bf16[128,2048]{1,0:T(8,128)(2,1)S(1)} %collective-permute-done.80.refs_1_), channel_id=1, source_target_pairs={{1,2},{2,3},{5,6},{6,7},{9,10},{10,11},{13,14},{14,15},{17,18},{18... | collective-permute-start | bytes 1572872 | tf_op jit(solution)/shard_map/ppermute | solution.py:215
  794.1 17.1 %collective-permute-start.84 = (bf16[128,2048]{1,0:T(8,128)(2,1)S(1)}, bf16[128,2048]{1,0:T(8,128)(2,1)}, u32[]{:S(2)}, u32[]{:S(2)}) collective-permute-start(bf16[128,2048]{1,0:T(8,128)(2,1)S(1)} %collective-permute-done.81.refs_4_), channel_id=1, source_target_pairs={{2,1},{1,0},{6,5},{5,4},{10,9},{9,8},{14,13},{13,12},{18,17},{17,1... | collective-permute-start | bytes 1572872 | tf_op jit(solution)/shard_map/ppermute | solution.py:215
  (150 other events, 1991.6 us)
Sparse Core Ops, SparseCore 0:
  10.8 39.7 all-gather.4
  52.6 58.2 all-gather.6
  112.8 58.4 all-gather.8
  173.0 54.2 all-gather.10
  329.9 106.3 all-reduce.1
  439.6 73.0 reduce-scatter.5
  516.7 71.5 reduce-scatter.7
  591.7 77.1 reduce-scatter.9
  678.0 39.1 reduce-scatter.13
  721.0 46.1 reduce-scatter.11

commit v4 on v3

--- a/solution.py
+++ b/solution.py
@@ -205,15 +205,18 @@
     def expect(self, value):
         self.last += (value,)
 
-    def slot(self, tasks, work=None, args=()):
+    def slot(self, tasks, work=None, args=(), launch=None, grad=None):
         sends = [task.sends() for task in tasks]
         flat = [send for group in sends for send in group]
         before = len(self.last)
+        extra = () if launch is None else (grad,)
         gated = lax.optimization_barrier(
-            tuple(self.last) + tuple(s[0] for s in flat) + tuple(args)
+            tuple(self.last) + tuple(s[0] for s in flat) + tuple(args) + extra
         )[before:]
+        if launch is not None:
+            self.launched = launch(gated[-1])
         moved = [lax.ppermute(g, s[1], s[2]) for g, s in zip(gated, flat)]
-        done = tuple(work(*gated[len(flat) :])) if work else ()
+        done = tuple(work(*gated[len(flat) : len(flat) + len(args)])) if work else ()
         self.last = tuple(moved) + done
         at = 0
         for task, group in zip(tasks, sends):
@@ -316,17 +319,18 @@
     d_gate_ref[...] = (d_hidden * up * (sig * (1.0 + gate * (1.0 - sig)))).astype(BF)
 
 
-def ffn_call(x, cot, g, u, d):
+def ffn_call(x, cot, g, u, d, chunk):
     rows, width = x.shape
     units = g.shape[1]
-    tile = min(256, units)
+    tile = min(512, units)
     whole = pl.BlockSpec((rows, width), lambda i: (0, 0))
+    rows_of = pl.BlockSpec((rows, width), lambda i: (chunk, 0))
     weight = pl.BlockSpec((width, tile), lambda i: (0, i))
     part = pl.BlockSpec((rows, tile), lambda i: (0, i))
     return pl.pallas_call(
         ffn_kernel,
         grid=(units // tile,),
-        in_specs=[whole, whole, weight, weight, weight],
+        in_specs=[whole, rows_of, weight, weight, weight],
         out_specs=[part] * 3,
         out_shape=[jax.ShapeDtypeStruct((rows, units), BF)] * 3,
         cost_estimate=pl.CostEstimate(
@@ -338,24 +342,30 @@
     )(x, cot, g, u, d)
 
 
-def product_kernel(count, *refs):
+def product_kernel(count, turned, *refs):
     total = None
     for k in range(count):
-        part = dot_plain(refs[k][...], refs[count + k][...])
+        dot = dot_plain if turned else dot_cols
+        part = dot(refs[k][...], refs[count + k][...])
         total = part if total is None else total + part
     refs[2 * count][...] = total.astype(BF)
 
 
-def product_call(lefts, rights):
+def product_call(lefts, rights, turned):
     count = len(lefts)
     rows, depth = lefts[0].shape
-    width = rights[0].shape[1]
-    tile = min(512, width)
+    width = rights[0].shape[1 if turned else 0]
+    tile = min(512 if turned else 256, width)
+    weight = (
+        pl.BlockSpec((depth, tile), lambda i: (0, i))
+        if turned
+        else pl.BlockSpec((tile, depth), lambda i: (i, 0))
+    )
     return pl.pallas_call(
-        functools.partial(product_kernel, count),
+        functools.partial(product_kernel, count, turned),
         grid=(width // tile,),
         in_specs=[pl.BlockSpec((rows, depth), lambda i: (0, 0))] * count
-        + [pl.BlockSpec((depth, tile), lambda i: (0, i))] * count,
+        + [weight] * count,
         out_specs=pl.BlockSpec((rows, tile), lambda i: (0, i)),
         out_shape=jax.ShapeDtypeStruct((rows, width), BF),
         cost_estimate=pl.CostEstimate(
@@ -662,19 +672,8 @@
     rows = per_chunk * block
     own_rows = rows // ways
 
-    pad = jnp.zeros((q_weight.shape[0], 126), BF)
-    packed = jnp.concatenate(
-        [q_weight, k_weight, v_weight, attn_gain[:, None], ffn_gain[:, None], pad], axis=1
-    )
-
-    def gathered(shard):
-        return lax.all_gather(shard, owners, axis=0, tiled=True)
-
-    packed = gathered(packed)
-    full_g = gathered(gate_weight)
-    full_u = gathered(up_weight)
-    full_d = gathered(down_weight)
-
+    clock = Clock()
+    slot = clock.slot
     where_all = positions(segments)
     where_here = lax.dynamic_slice_in_dim(where_all, here * block, block, 1)
     seg_here = lax.dynamic_slice_in_dim(segments, here * block, block, 1)
@@ -704,31 +703,54 @@
         s["cot"] = chunk_of(cotangent, c).reshape(rows, width)
         s["cos"] = lax.slice_in_dim(cosine, c * rows, (c + 1) * rows, axis=0)
         s["sin"] = lax.slice_in_dim(sine, c * rows, (c + 1) * rows, axis=0)
+        s["sin_back"] = -s["sin"]
+        s["scale_one"] = inverse_rms(tok.astype(F32))
         seg_q, seg_k = chunk_of(seg_here, c), chunk_of(segments, c)
         s["seg_fwd"] = (seg_q[:, :, None], seg_k[:, None, :])
         s["seg_back"] = (seg_q[:, None, :], seg_k[:, :, None])
         state.append(s)
     first, second = state
 
-    clock = Clock()
-    slot = clock.slot
-    gather_o = NearGather(o_weight)
-    slot([gather_o])
-    slot([gather_o])
-    slot([gather_o])
-    full_o = gather_o.result()
-    full_qkv = packed[:, :qkv_width]
-    gains = packed[:, qkv_width : qkv_width + 2].T.astype(F32)
+    pad = jnp.zeros((q_weight.shape[0], 126), BF)
+    packed = jnp.concatenate(
+        [q_weight, o_weight, k_weight, v_weight, attn_gain[:, None], ffn_gain[:, None], pad],
+        axis=1,
+    )
+
+    def gathered(shard):
+        return lax.all_gather(shard, owners, axis=0, tiled=True)
+
+    gather_near = NearGather(packed)
+    slot([gather_near])
+    for s in state:
+        for name in ("cos", "sin", "sin_back", "scale_one"):
+            clock.expect(s[name])
+        for name in ("seg_fwd", "seg_back"):
+            clock.last += s[name]
+    clock.expect(place)
+    slot([gather_near])
+    slot([gather_near], lambda *shards: shards, (gate_weight, up_weight, down_weight))
+    gate_weight, up_weight, down_weight = clock.last[-3:]
+    full_g = gathered(gate_weight)
+    full_u = gathered(up_weight)
+    full_d = gathered(down_weight)
+    packed = gather_near.result()
+    at = 0
+    columns = []
+    for wide in (q_width, q_width, kv_width, 2):
+        columns.append(packed[:, at : at + wide])
+        at += wide
+    full_q, full_o, full_kv, gains = columns
+    gains = gains.T.astype(F32)
     gain_one, gain_two = gains[0:1], gains[1:2]
 
     def project_kv(s, tok):
-        tok_f = tok.astype(F32)
-        normed = (tok_f * inverse_rms(tok_f) * gain_one).astype(BF)
-        kv = turn_call(dot_plain(normed, full_qkv[:, q_width:]), s["cos"], s["sin"], k_width)
+        normed = (tok.astype(F32) * s["scale_one"] * gain_one).astype(BF)
+        kv = turn_call(dot_plain(normed, full_kv), s["cos"], s["sin"], k_width)
         return normed, kv.reshape(per_chunk, block, kv_width)
 
     def project_q(s, normed):
-        q = turn_call(dot_plain(normed, full_qkv[:, :q_width]), s["cos"], s["sin"], q_width)
+        q = turn_call(dot_plain(normed, full_q), s["cos"], s["sin"], q_width)
         return (q.reshape(per_chunk, block, q_width),)
 
     def project(s, tok):
@@ -750,14 +772,16 @@
     def turn_over(weight):
         return (transpose_call(weight),)
 
-    def ffn_mid(normed_two, cot):
-        return ffn_call(normed_two, cot, full_g, full_u, full_d)
+    cot_rows = cotangent.reshape(seqs * block, width)
+
+    def ffn_mid(chunk, normed_two):
+        return ffn_call(normed_two, cot_rows, full_g, full_u, full_d, chunk)
 
     def ffn_back(d_gate, d_up):
-        return (product_call((d_gate, d_up), (turned["g"], turned["u"])),)
+        return (product_call((d_gate, d_up), (turned["g"], turned["u"]), True),)
 
     def ffn_out(hidden):
-        return (product_call((hidden,), (turned["d"],)),)
+        return (product_call((hidden,), (full_d,), False),)
 
     def leave_ffn(s, summed):
         d_norm, s["gain_two"] = norm_back(s["residual"], gain_two, summed)
@@ -776,9 +800,10 @@
         far = (b2.astype(F32) + from3.astype(F32)).astype(BF)
         from2 = lax.ppermute(far, "yy", FLIP)
         d_kv = b0.astype(F32) + from1.astype(F32) + from2.astype(F32)
-        d_q = turn_call(dq.reshape(rows, q_width), s["cos"], -s["sin"], q_width)
-        d_kv = turn_call(d_kv.reshape(rows, kv_width), s["cos"], -s["sin"], k_width)
+        d_q = turn_call(dq.reshape(rows, q_width), s["cos"], s["sin_back"], q_width)
+        d_kv = turn_call(d_kv.reshape(rows, kv_width), s["cos"], s["sin_back"], k_width)
         d_qkv = jnp.concatenate([d_q, d_kv], axis=1)
+        full_qkv = jnp.concatenate([full_q, full_kv], axis=1)
         return d_qkv, dot_cols(d_qkv, full_qkv).astype(BF)
 
     def leave_attention(s, summed):
@@ -795,6 +820,9 @@
 
     def of_both(*names):
         return tuple(s[name] for name in names for s in state)
+
+    def whole(rows_of):
+        return rows_of.reshape(per_chunk, block, width)
 
     def leave_layer(s, ffn):
         mine = own(ffn).astype(F32) + s["residual"]
@@ -831,17 +859,17 @@
     (turned["u"],) = slot([Both(gather_a0, sum_a1)], turn_over, (full_u,))
     first["normed_two"] = gather_a0.result().reshape(rows, width)
     first["hidden"], first["d_gate"], first["d_up"] = slot(
-        [sum_a1], ffn_mid, (first["normed_two"], first["cot"])
+        [sum_a1], functools.partial(ffn_mid, 0), (first["normed_two"],)
     )
     gather_a1 = LineGather(enter_ffn(second, sum_a1.result()))
     (back,) = slot([gather_a1], ffn_back, (first["d_gate"], first["d_up"]))
     sum_d0 = LineSum(blocks(back))
-    (turned["d"],) = slot([Both(gather_a1, sum_d0)], turn_over, (full_d,))
     (ffn,) = slot([Both(gather_a1, sum_d0)], ffn_out, (first["hidden"],))
     leave_layer(first, ffn)
+    slot([Both(gather_a1, sum_d0)])
     second["normed_two"] = gather_a1.result().reshape(rows, width)
     second["hidden"], second["d_gate"], second["d_up"] = slot(
-        [sum_d0], ffn_mid, (second["normed_two"], second["cot"])
+        [sum_d0], functools.partial(ffn_mid, 1), (second["normed_two"],)
     )
     gather_d0 = LineGather(leave_ffn(first, sum_d0.result()))
     (back,) = slot([gather_d0], ffn_back, (second["d_gate"], second["d_up"]))
@@ -849,93 +877,108 @@
     (grad,) = slot(
         [Both(gather_d0, sum_d1)],
         weight_grad,
-        (cotangent.reshape(seqs * block, width),) + of_both("hidden"),
-    )
-    down_grad = scattered(grad)
-    (grad,) = slot([Both(gather_d0, sum_d1)], weight_grad, of_both("normed_two", "d_gate"))
-    gate_grad = scattered(grad)
+        (cot_rows,) + of_both("hidden"),
+    )
+    (grad,) = slot(
+        [Both(gather_d0, sum_d1)],
+        weight_grad,
+        of_both("normed_two", "d_gate"),
+        scattered,
+        grad,
+    )
+    down_grad = clock.launched
     first["d_attn"] = gather_d0.result().reshape(rows, width)
-    pieces = slot([sum_d1], functools.partial(attend_back, first), (first["d_attn"],))
+    pieces = slot(
+        [sum_d1], functools.partial(attend_back, first), (first["d_attn"],), scattered, grad
+    )
+    gate_grad = clock.launched
     gather_d1 = LineGather(leave_ffn(second, sum_d1.result()))
-    gains_two = Butterfly(first["gain_two"] + second["gain_two"], axes)
     first["d_qkv"], back = slot(
-        [gather_d1, gains_two], functools.partial(project_back, first), pieces
+        [gather_d1], functools.partial(project_back, first), pieces
     )
     sum_n0 = LineSum(blocks(back))
     (grad,) = slot(
-        [Both(gather_d1, sum_n0), gains_two], weight_grad, of_both("normed_two", "d_up")
-    )
-    up_grad = scattered(grad)
-    (ffn,) = slot([Both(gather_d1, sum_n0), gains_two], ffn_out, (second["hidden"],))
-    sum_f1 = LineSum(blocks(ffn))
+        [Both(gather_d1, sum_n0)], weight_grad, of_both("normed_two", "d_up")
+    )
+    slot([Both(gather_d1, sum_n0)], None, (), scattered, grad)
+    up_grad = clock.launched
     second["d_attn"] = gather_d1.result().reshape(rows, width)
     pieces = slot(
-        [sum_n0, gains_two], functools.partial(attend_back, second), (second["d_attn"],)
+        [sum_n0], functools.partial(attend_back, second), (second["d_attn"],)
     )
     gather_n0 = LineGather(leave_attention(first, sum_n0.result()))
     second["d_qkv"], back = slot(
-        [gather_n0, gains_two], functools.partial(project_back, second), pieces
+        [gather_n0], functools.partial(project_back, second), pieces
     )
     sum_n1 = LineSum(blocks(back))
     clock.expect(first["output"])
     (grad,) = slot(
         [Both(gather_n0, sum_n1)], weight_grad, of_both("normed_one", "d_qkv")
     )
-    qkv_grad = scattered(grad)
+    qkv_part = grad
     for s in state:
         s["attended_rows"] = s["attended"].reshape(rows, q_width)
     (grad,) = slot(
-        [Both(gather_n0, sum_n1)], weight_grad, of_both("d_attn", "attended_rows")
-    )
-    o_grad = scattered(grad)
+        [Both(gather_n0, sum_n1)],
+        weight_grad,
+        of_both("d_attn", "attended_rows"),
+        scattered,
+        qkv_part,
+    )
+    qkv_grad = clock.launched
     first["input_grad"] = gather_n0.result()
-    slot([sum_n1])
+    (ffn,) = slot([sum_n1], ffn_out, (second["hidden"],), scattered, grad)
+    sum_f1 = LineSum(blocks(ffn))
+    o_grad = clock.launched
     gather_n1 = LineGather(leave_attention(second, sum_n1.result()))
-    gains_one = Butterfly(first["gain_one"] + second["gain_one"], axes)
+    gains_one = Butterfly(
+        jnp.stack([sum(s[name] for s in state) for name in ("gain_one", "gain_two")]), axes
+    )
     slot([gather_n1, gains_one])
-    clock.expect(down_grad)
     slot([Both(gather_n1, sum_f1), gains_one])
+    clock.expect(whole(first["input_grad"]))
     slot([Both(gather_n1, sum_f1), gains_one])
     second["input_grad"] = gather_n1.result()
+    clock.expect(down_grad)
+    slot([sum_f1, gains_one])
+    input_grad = jnp.concatenate([whole(s["input_grad"]) for s in state], axis=0).astype(F32)
+    gather_f1 = LineGather((second["residual"] + sum_f1.result()).astype(BF))
     clock.expect(gate_grad)
-    slot([sum_f1, gains_one])
-    gather_f1 = LineGather((second["residual"] + sum_f1.result()).astype(BF))
+    slot([gather_f1, gains_one])
+    clock.expect(input_grad)
+    down_grad, gate_grad = down_grad.astype(F32), gate_grad.astype(F32)
     clock.expect(up_grad)
-    slot([gather_f1, gains_one])
     slot([gather_f1])
+    clock.expect(down_grad)
+    clock.expect(gate_grad)
+    up_grad = up_grad.astype(F32)
+    clock.expect(up_grad)
     slot([gather_f1])
     second["output"] = gather_f1.result()
     while gains_one.moves:
         slot([gains_one])
-    while gains_two.moves:
-        slot([gains_two])
-
-    qkv_grad, o_grad, down_grad, gate_grad, up_grad = (
-        g.astype(F32) for g in (qkv_grad, o_grad, down_grad, gate_grad, up_grad)
-    )
+
+    qkv_grad, o_grad = qkv_grad.astype(F32), o_grad.astype(F32)
     share = attn_gain.shape[0]
     index = lax.axis_index("fsdp") * parts + here
 
     def owned(gain):
         return lax.dynamic_slice_in_dim(gain, index * share, share, 0)
 
-    def whole(name):
-        return jnp.concatenate(
-            [s[name].reshape(per_chunk, block, width) for s in state], axis=0
-        )
+    gain_one_grad, gain_two_grad = gains_one.value
 
     return (
-        whole("output"),
-        whole("input_grad").astype(F32),
+        jnp.concatenate([whole(s["output"]) for s in state], axis=0),
+        input_grad,
         qkv_grad[:, :q_width],
         qkv_grad[:, q_width : q_width + k_width],
         qkv_grad[:, q_width + k_width :],
         o_grad,
-        owned(gains_one.value),
+        owned(gain_one_grad),
         gate_grad,
         up_grad,
         down_grad,
-        owned(gains_two.value),
+        owned(gain_two_grad),
     )
 
 

time: 851 us -> 805 us (0.946)
  waiting for transfers between devices: 205 us -> 160 us
  local copies, waits for them, and re-layouts: 31.8 us -> 44 us
    ppermute x81 -> x76, waiting for transfers between devices: 186 us -> 156 us  [slot(): moved = [lax.ppermute(g, s[1], s[2]) for g, s in zip(gated, flat)]]
    all_gather x4 -> x3, waiting for transfers between devices: 12.6 us -> 0.02 us  [gathered(): return lax.all_gather(shard, owners, axis=0, tiled=True)]
    pallas_call x3 -> x2, Pallas kernels: 29.9 us -> 20 us  [transpose_call(): pl.pallas_call(transpose_kernel, grid=(rows // tile,), in_specs=[pl.Block...]
    ppermute x81 -> x76, starting transfers between devices: 167 us -> 158 us  [slot(): moved = [lax.ppermute(g, s[1], s[2]) for g, s in zip(gated, flat)]]
  transfers between devices with their start and end apart: 97 -> 91, of which waited for: 45 -> 37; matrix products, arithmetic and copies ran while one was open for 24% -> 28% of each run, Pallas kernels for 25% -> 26%
where the time goes in v4:
time: 805 us; the launch traced here: 797 us
  Pallas kernels  211 us (26%)
  starting transfers between devices  164 us (20%)
  waiting for transfers between devices  160 us (20%)
  other arithmetic  110 us (14%)
  matrix products  91.2 us (11%)
  local copies, waits for them, and re-layouts  44 us (5%)
  between operations  15.8 us (2%)
    ppermute x76, starting transfers between devices, slot(): moved = [lax.ppermute(g, s[1], s[2]) for g, s in zip(gated, flat)]  158 us
    ppermute x76, waiting for transfers between devices, slot(): moved = [lax.ppermute(g, s[1], s[2]) for g, s in zip(gated, flat)]  156 us
    dot_general x5, matrix products, dot_rows(): lax.dot_general(left_in, right_in, (((0,), (0,)), ((), ())), preferred_el...  53.4 us
    pallas_call x4, Pallas kernels, product_call(): pl.pallas_call(functools.partial(product_kernel, count, turned), grid=(wi...  49.5 us
    pallas_call x2, Pallas kernels, ffn_call(): pl.pallas_call(ffn_kernel, grid=(units // tile,), in_specs=[whole, rows_o...  40.2 us
    pallas_call x2, Pallas kernels, attend_back_call(): pl.pallas_call(functools.partial(attend_back_kernel, group), grid_spec=pl...  32.2 us
    select_n x12, other arithmetic, sends(): value = jnp.where(rank >= first, whole[0], part[0])  30.4 us
    dot_general x6, matrix products, dot_plain(): return jnp.dot(left_in, right_in, preferred_element_type=F32)  23.1 us
  transfers between devices with their start and end apart: 91, of which 37 were waited for; matrix products, arithmetic and copies ran while one was open for 28% of the time, Pallas kernels for 26%

profile of v4, /device:TPU:0, one launch (start us, length us, event | category | flops | bytes accessed | tf_op | source)
XLA Modules:
  0.0 797.0 jit_solution(3799836672856614664)
XLA Ops:
  34.7 5.1 collective-permute-done.2
  48.9 6.6 spread.1
  79.2 11.5 %attend.2 = (bf16[2,256,512]{2,1,0:T(8,128)(2,1)}, f32[2,8,256]{2,1,0:T(8,128)}) custom-call(s32[5]{0:T(128)} %stack.34.place_ref, bf16[2,256,512]{2,1,0:T(8,128)(2,1)} %bitcast.325, bf16[2,256,256]{2,1,0:T(8,128)(2,1)} %bitcast.345, bf16[2,256,256]{2,1,0:T(8,128)(2,1)} %copy-done.64, bf16[2,256,256]{2,1,0:T(8,128)(2,1)} %copy-done.63, ...), custom_call_target="tpu_custom_call" | custom-call | flops 4294967296 | bytes 1572864 | tf_op jit(solution)/shard_map/attend/pallas_call | solution.py:482
  106.9 5.0 fusion.131.x_ref
  121.8 8.1 %collective-permute-done.10 = bf16[128,2048]{1,0:T(8,128)(2,1)S(1)} collective-permute-done((bf16[128,2048]{1,0:T(8,128)(2,1)}, bf16[128,2048]{1,0:T(8,128)(2,1)S(1)}, u32[]{:S(2)}, u32[]{:S(2)}) %collective-permute-start.10) | collective-permute-done | bytes 524320 | tf_op jit(solution)/shard_map/ppermute | solution.py:218
  132.3 5.5 collective-permute-start.14
  140.1 8.1 %collective-permute-done.14 = bf16[128,2048]{1,0:T(8,128)(2,1)S(1)} collective-permute-done((bf16[128,2048]{1,0:T(8,128)(2,1)S(1)}, bf16[128,2048]{1,0:T(8,128)(2,1)S(1)}, u32[]{:S(2)}, u32[]{:S(2)}) %collective-permute-start.14) | collective-permute-done | bytes 524320 | tf_op jit(solution)/shard_map/ppermute | solution.py:218
  158.9 11.4 %attend.3 = (bf16[2,256,512]{2,1,0:T(8,128)(2,1)}, f32[2,8,256]{2,1,0:T(8,128)}) custom-call(s32[5]{0:T(128)} %stack.34.place_ref, bf16[2,256,512]{2,1,0:T(8,128)(2,1)} %bitcast.323, bf16[2,256,256]{2,1,0:T(8,128)(2,1)} %bitcast.339, bf16[2,256,256]{2,1,0:T(8,128)(2,1)} %copy-done.61, bf16[2,256,256]{2,1,0:T(8,128)(2,1)} %copy-done.60, ...), custom_call_target="tpu_custom_call" | custom-call | flops 4294967296 | bytes 1572864 | tf_op jit(solution)/shard_map/attend/pallas_call | solution.py:482
  181.7 10.0 %turn_over.2.refs_2_ = bf16[2048,2048]{1,0:T(8,128)(2,1)} custom-call(bf16[2048,2048]{1,0:T(8,128)(2,1)} %all-gather.4.cloned.1.call-done.x_ref.g_ref), custom_call_target="tpu_custom_call" | custom-call | bytes 16777216 | tf_op jit(solution)/shard_map/turn_over/pallas_call | solution.py:387
  200.7 10.0 %turn_over.3.refs_3_ = bf16[2048,2048]{1,0:T(8,128)(2,1)} custom-call(bf16[2048,2048]{1,0:T(8,128)(2,1)} %all-gather.6.cloned.1.call-done.x_ref.u_ref), custom_call_target="tpu_custom_call" | custom-call | bytes 16777216 | tf_op jit(solution)/shard_map/turn_over/pallas_call | solution.py:387
  224.0 20.1 %ffn.2 = (bf16[512,2048]{1,0:T(8,128)(2,1)}, bf16[512,2048]{1,0:T(8,128)(2,1)}, bf16[512,2048]{1,0:T(8,128)(2,1)}) custom-call(bf16[512,2048]{1,0:T(8,128)(2,1)} %bitcast.308, bf16[1024,2048]{1,0:T(8,128)(2,1)} %bitcast.303, bf16[2048,2048]{1,0:T(8,128)(2,1)} %all-gather.4.cloned.1.call-done.x_ref.g_ref, ...), custom_call_target="tpu_custom_call" | custom-call | flops 12884901888 | bytes 31457280 | tf_op jit(solution)/shard_map/ffn/pallas_call | solution.py:330
  251.2 13.8 %product.4 = bf16[512,2048]{1,0:T(8,128)(2,1)} custom-call(bf16[512,2048]{1,0:T(8,128)(2,1)} %get-tuple-element.248.refs_0_, bf16[512,2048]{1,0:T(8,128)(2,1)} %get-tuple-element.269.refs_1_, bf16[2048,2048]{1,0:T(8,128)(2,1)} %turn_over.2.refs_2_, bf16[2048,2048]{1,0:T(8,128)(2,1)} %turn_over.3.refs_3_), custom_call_target="tpu_custom_call" | custom-call | flops 8589934592 | bytes 20971520 | tf_op jit(solution)/shard_map/product/pallas_call | solution.py:364
  273.5 10.6 %product.5 = bf16[512,2048]{1,0:T(8,128)(2,1)} custom-call(bf16[512,2048]{1,0:T(8,128)(2,1)} %get-tuple-element.242.refs_0_, bf16[2048,2048]{1,0:T(8,128)(2,1)} %all-gather.8.cloned.1.call-done.d_ref.refs_1_), custom_call_target="tpu_custom_call" | custom-call | flops 4294967296 | bytes 10485760 | tf_op jit(solution)/shard_map/product/pallas_call | solution.py:364
  312.5 20.1 %ffn.3 = (bf16[512,2048]{1,0:T(8,128)(2,1)}, bf16[512,2048]{1,0:T(8,128)(2,1)}, bf16[512,2048]{1,0:T(8,128)(2,1)}) custom-call(bf16[512,2048]{1,0:T(8,128)(2,1)} %bitcast.313, bf16[1024,2048]{1,0:T(8,128)(2,1)} %bitcast.304, bf16[2048,2048]{1,0:T(8,128)(2,1)} %all-gather.4.cloned.1.call-done.x_ref.g_ref, ...), custom_call_target="tpu_custom_call" | custom-call | flops 12884901888 | bytes 31457280 | tf_op jit(solution)/shard_map/ffn/pallas_call | solution.py:330
  332.6 16.3 %collective-permute-done.32 = bf16[128,2048]{1,0:T(8,128)(2,1)S(1)} collective-permute-done((bf16[128,2048]{1,0:T(8,128)(2,1)}, bf16[128,2048]{1,0:T(8,128)(2,1)S(1)}, u32[]{:S(2)}, u32[]{:S(2)}) %collective-permute-start.32) | collective-permute-done | bytes 524320 | tf_op jit(solution)/shard_map/ppermute | solution.py:218
  358.5 14.0 %product.6 = bf16[512,2048]{1,0:T(8,128)(2,1)} custom-call(bf16[512,2048]{1,0:T(8,128)(2,1)} %get-tuple-element.249.refs_0_, bf16[512,2048]{1,0:T(8,128)(2,1)} %get-tuple-element.270.refs_1_, bf16[2048,2048]{1,0:T(8,128)(2,1)} %turn_over.2.refs_2_, bf16[2048,2048]{1,0:T(8,128)(2,1)} %turn_over.3.refs_3_), custom_call_target="tpu_custom_call" | custom-call | flops 8589934592 | bytes 20971520 | tf_op jit(solution)/shard_map/product/pallas_call | solution.py:364
  375.2 5.5 collective-permute-start.35
  382.0 13.7 %convolution_convert_fusion.2 = bf16[2048,2048]{1,0:T(8,128)(2,1)} fusion(bf16[1024,2048]{1,0:T(8,128)(2,1)} %bitcast.305, bf16[512,2048]{1,0:T(8,128)(2,1)S(1)} %copy-done.71, bf16[512,2048]{1,0:T(8,128)(2,1)} %get-tuple-element.242.refs_0_), kind=kOutput, calls=%fused_computation.2 | convolution fusion | flops 8602517504 | bytes 16777216 | tf_op jit(solution)/shard_map/dot_general | solution.py:36
  400.6 12.7 %collective-permute-done.36.refs_5_ = bf16[128,2048]{1,0:T(8,128)(2,1)} collective-permute-done((bf16[128,2048]{1,0:T(8,128)(2,1)}, bf16[128,2048]{1,0:T(8,128)(2,1)}, u32[]{:S(2)}, u32[]{:S(2)}) %collective-permute-start.36) | collective-permute-done | bytes 524320 | tf_op jit(solution)/shard_map/ppermute | solution.py:218
  421.1 14.8 %convolution_convert_fusion.1 = bf16[2048,2048]{1,0:T(8,128)(2,1)} fusion(bf16[512,2048]{1,0:T(8,128)(2,1)} %bitcast.314, bf16[512,2048]{1,0:T(8,128)(2,1)} %bitcast.309, bf16[512,2048]{1,0:T(8,128)(2,1)} %get-tuple-element.249.refs_0_, bf16[512,2048]{1,0:T(8,128)(2,1)} %get-tuple-element.248.refs_0_), kind=kOutput, calls=%fused_computation.1 | convolution fusion | flops 8610906112 | bytes 16777216 | tf_op jit(solution)/shard_map/dot_general | solution.py:36
  443.6 5.3 collective-permute-start.39
  455.2 16.0 %attend_back.2 = (bf16[2,256,512]{2,1,0:T(8,128)(2,1)}, bf16[2,256,256]{2,1,0:T(8,128)(2,1)}, bf16[2,256,256]{2,1,0:T(8,128)(2,1)}, bf16[2,256,256]{2,1,0:T(8,128)(2,1)}, bf16[2,256,256]{2,1,0:T(8,128)(2,1)}) custom-call(s32[5]{0:T(128)} %stack.34.place_ref, bf16[2,256,512]{2,1,0:T(8,128)(2,1)} %bitcast.326, bf16[2,256,256]{2,1,0:T(8,128)(2,1)} %bitcast.346, ...), custom_call_target="tpu_custom_call" | custom-call | flops 10737418240 | bytes 3145728 | tf_op jit(solution)/shard_map/attend_back/pallas_call | solution.py:602
  513.0 11.5 %convolution_convert_fusion = bf16[2048,2048]{1,0:T(8,128)(2,1)} fusion(bf16[512,2048]{1,0:T(8,128)(2,1)S(1)} %bitcast.315, bf16[512,2048]{1,0:T(8,128)(2,1)S(1)} %bitcast.310, bf16[512,2048]{1,0:T(8,128)(2,1)S(1)} %copy-done.73, bf16[512,2048]{1,0:T(8,128)(2,1)S(1)} %copy-done.72), kind=kOutput, calls=%fused_computation | convolution fusion | flops 8610906112 | bytes 16777216 | tf_op jit(solution)/shard_map/dot_general | solution.py:36
  535.6 7.1 collective-permute-done.48.refs_3_
  560.7 16.2 %attend_back.3 = (bf16[2,256,512]{2,1,0:T(8,128)(2,1)}, bf16[2,256,256]{2,1,0:T(8,128)(2,1)}, bf16[2,256,256]{2,1,0:T(8,128)(2,1)}, bf16[2,256,256]{2,1,0:T(8,128)(2,1)}, bf16[2,256,256]{2,1,0:T(8,128)(2,1)}) custom-call(s32[5]{0:T(128)} %stack.34.place_ref, bf16[2,256,512]{2,1,0:T(8,128)(2,1)} %bitcast.324, bf16[2,256,256]{2,1,0:T(8,128)(2,1)} %bitcast.340, ...), custom_call_target="tpu_custom_call" | custom-call | flops 10737418240 | bytes 3145728 | tf_op jit(solution)/shard_map/attend_back/pallas_call | solution.py:602
  612.3 8.1 %fusion.23 = bf16[2048,768]{1,0:T(8,128)(2,1)} fusion(bf16[512,2048]{1,0:T(8,128)(2,1)} %copy-done.38, bf16[512,2048]{1,0:T(8,128)(2,1)} %copy-done.37, bf16[512,768]{1,0:T(8,128)(2,1)} %pad_maximum_fusion.5, bf16[512,768]{1,0:T(8,128)(2,1)} %pad_maximum_fusion.4), kind=kOutput, calls=%fused_computation.32 | convolution fusion | flops 3234332672 | bytes 8912896 | tf_op jit(solution)/shard_map/dot_general | solution.py:36
  632.9 5.3 fusion.26
  652.6 11.0 %product.7 = bf16[512,2048]{1,0:T(8,128)(2,1)} custom-call(bf16[512,2048]{1,0:T(8,128)(2,1)} %get-tuple-element.300.refs_0_, bf16[2048,2048]{1,0:T(8,128)(2,1)} %all-gather.8.cloned.1.call-done.d_ref.refs_1_), custom_call_target="tpu_custom_call" | custom-call | flops 4294967296 | bytes 10485760 | tf_op jit(solution)/shard_map/product/pallas_call | solution.py:364
  678.0 9.2 %collective-permute-done.65 = f32[2,2048]{1,0:T(2,128)S(1)} collective-permute-done((f32[2,2048]{1,0:T(2,128)S(1)}, f32[2,2048]{1,0:T(2,128)S(1)}, u32[]{:S(2)}, u32[]{:S(2)}) %collective-permute-start.65) | collective-permute-done | bytes 16416 | tf_op jit(solution)/shard_map/ppermute | solution.py:218
  697.5 5.9 collective-permute-done.68
  747.2 5.5 maximum_convert_fusion
  773.3 8.8 %collective-permute-done.81.refs_6_ = bf16[128,2048]{1,0:T(8,128)(2,1)S(1)} collective-permute-done((bf16[128,2048]{1,0:T(8,128)(2,1)}, bf16[128,2048]{1,0:T(8,128)(2,1)S(1)}, u32[]{:S(2)}, u32[]{:S(2)}) %collective-permute-start.81) | collective-permute-done | bytes 524320 | tf_op jit(solution)/shard_map/ppermute | solution.py:218
  (466 shorter events, 448.4 us)
Async XLA Ops:
  7.2 168.6 %all-gather.4.cloned.1.call-start = ((), (), s32[]{:S(2)}) async-start(), calls=%async_computation.5 | async-start | bytes 9437184 | tf_op jit(solution)/shard_map/all_gather | solution.py:721
  10.1 20.7 %collective-permute-start = (bf16[256,1408]{1,0:T(8,128)(2,1)S(1)}, bf16[256,1408]{1,0:T(8,128)(2,1)S(1)}, u32[]{:S(2)}, u32[]{:S(2)}) collective-permute-start(bf16[256,1408]{1,0:T(8,128)(2,1)S(1)} %concatenate.52), channel_id=1, source_target_pairs={{0,16},{16,0},{1,17},{17,1},{2,18},{18,2},{3,19},{19,3},{4,20},{20... | collective-permute-start | bytes 2162696 | tf_op jit(solution)/shard_map/ppermute | solution.py:218
  13.1 17.6 %collective-permute-start.1 = (bf16[256,1408]{1,0:T(8,128)(2,1)S(1)}, bf16[256,1408]{1,0:T(8,128)(2,1)S(1)}, u32[]{:S(2)}, u32[]{:S(2)}) collective-permute-start(bf16[256,1408]{1,0:T(8,128)(2,1)S(1)} %concatenate.52), channel_id=1, source_target_pairs={{0,8},{8,0},{1,9},{9,1},{2,10},{10,2},{3,11},{11,3},{4,12},{12,4},... | collective-permute-start | bytes 2162696 | tf_op jit(solution)/shard_map/ppermute | solution.py:218
  41.4 155.3 %all-gather.6.cloned.1.call-start = ((), (), s32[]{:S(2)}) async-start(), calls=%async_computation.6 | async-start | bytes 9437184 | tf_op jit(solution)/shard_map/all_gather | solution.py:721
  42.2 181.8 %all-gather.8.cloned.1.call-start = ((), (), s32[]{:S(2)}) async-start(), calls=%async_computation.7 | async-start | bytes 9437184 | tf_op jit(solution)/shard_map/all_gather | solution.py:721
  42.9 564.9 %all-reduce.2.cloned.1.call-start = ((), (), s32[]{:S(2)}) async-start(), calls=%async_computation.8 | async-start | bytes 4194304 | tf_op jit(solution)/shard_map/psum | solution.py:830
  95.0 19.6 %collective-permute-start.8 = (bf16[128,2048]{1,0:T(8,128)(2,1)}, bf16[128,2048]{1,0:T(8,128)(2,1)S(1)}, u32[]{:S(2)}, u32[]{:S(2)}) collective-permute-start(bf16[128,2048]{1,0:T(8,128)(2,1)} %get-tuple-element.189), channel_id=1, source_target_pairs={{0,1},{4,5},{8,9},{12,13},{16,17},{20,21},{24,25},{28,29}} | collective-permute-start | bytes 1572872 | tf_op jit(solution)/shard_map/ppermute | solution.py:218
  98.4 16.2 %collective-permute-start.9 = (bf16[128,2048]{1,0:T(8,128)(2,1)S(1)}, bf16[128,2048]{1,0:T(8,128)(2,1)}, u32[]{:S(2)}, u32[]{:S(2)}) collective-permute-start(bf16[128,2048]{1,0:T(8,128)(2,1)S(1)} %get-tuple-element.190), channel_id=1, source_target_pairs={{3,2},{7,6},{11,10},{15,14},{19,18},{23,22},{27,26},{31,30}} | collective-permute-start | bytes 1572872 | tf_op jit(solution)/shard_map/ppermute | solution.py:218
  155.4 18.0 %collective-permute-start.17 = (bf16[128,2048]{1,0:T(8,128)(2,1)S(1)}, bf16[128,2048]{1,0:T(8,128)(2,1)S(1)}, u32[]{:S(2)}, u32[]{:S(2)}) collective-permute-start(bf16[128,2048]{1,0:T(8,128)(2,1)S(1)} %multiply_convert_fusion.3.refs_0_), channel_id=1, source_target_pairs={{0,1},{1,2},{2,3},{4,5},{5,6},{6,7},{8,9},{9,10},{10,11},{12,13},{... | collective-permute-start | bytes 1572872 | tf_op jit(solution)/shard_map/ppermute | solution.py:218
  218.0 26.0 %collective-permute-start.24 = (bf16[128,2048]{1,0:T(8,128)(2,1)S(1)}, bf16[128,2048]{1,0:T(8,128)(2,1)S(1)}, u32[]{:S(2)}, u32[]{:S(2)}) collective-permute-start(bf16[128,2048]{1,0:T(8,128)(2,1)S(1)} %get-tuple-element.215), channel_id=1, source_target_pairs={{3,2},{2,1},{1,0},{7,6},{6,5},{5,4},{11,10},{10,9},{9,8},{15,14},{... | collective-permute-start | bytes 1572872 | tf_op jit(solution)/shard_map/ppermute | solution.py:218
  219.3 24.7 %collective-permute-start.23 = (bf16[128,2048]{1,0:T(8,128)(2,1)S(1)}, bf16[128,2048]{1,0:T(8,128)(2,1)S(1)}, u32[]{:S(2)}, u32[]{:S(2)}) collective-permute-start(bf16[128,2048]{1,0:T(8,128)(2,1)S(1)} %get-tuple-element.214), channel_id=1, source_target_pairs={{0,1},{1,2},{2,3},{4,5},{5,6},{6,7},{8,9},{9,10},{10,11},{12,13},{... | collective-permute-start | bytes 1572872 | tf_op jit(solution)/shard_map/ppermute | solution.py:218
  246.5 18.5 %collective-permute-start.25 = (bf16[128,2048]{1,0:T(8,128)(2,1)S(1)}, bf16[128,2048]{1,0:T(8,128)(2,1)S(1)}, u32[]{:S(2)}, u32[]{:S(2)}) collective-permute-start(bf16[128,2048]{1,0:T(8,128)(2,1)S(1)} %multiply_convert_fusion.2.refs_0_), channel_id=1, source_target_pairs={{0,1},{1,2},{2,3},{4,5},{5,6},{6,7},{8,9},{9,10},{10,11},{12,13},{... | collective-permute-start | bytes 1572872 | tf_op jit(solution)/shard_map/ppermute | solution.py:218
  267.6 16.5 %collective-permute-start.27 = (bf16[128,2048]{1,0:T(8,128)(2,1)}, bf16[128,2048]{1,0:T(8,128)(2,1)S(1)}, u32[]{:S(2)}, u32[]{:S(2)}) collective-permute-start(bf16[128,2048]{1,0:T(8,128)(2,1)} %get-tuple-element.225), channel_id=1, source_target_pairs={{0,1},{1,2},{2,3},{4,5},{5,6},{6,7},{8,9},{9,10},{10,11},{12,13},{... | collective-permute-start | bytes 1572872 | tf_op jit(solution)/shard_map/ppermute | solution.py:218
  300.0 421.2 %reduce-scatter.6.cloned.1.call-start = ((), (), s32[]{:S(2)}) async-start(), calls=%async_computation.9 | async-start | bytes 9437184 | tf_op jit(solution)/shard_map/reduce_scatter | solution.py:814
  309.5 23.1 %collective-permute-start.31 = (bf16[128,2048]{1,0:T(8,128)(2,1)}, bf16[128,2048]{1,0:T(8,128)(2,1)S(1)}, u32[]{:S(2)}, u32[]{:S(2)}) collective-permute-start(bf16[128,2048]{1,0:T(8,128)(2,1)} %get-tuple-element.229), channel_id=1, source_target_pairs={{0,1},{1,2},{2,3},{4,5},{5,6},{6,7},{8,9},{9,10},{10,11},{12,13},{... | collective-permute-start | bytes 1572872 | tf_op jit(solution)/shard_map/ppermute | solution.py:218
  311.2 37.7 %collective-permute-start.32 = (bf16[128,2048]{1,0:T(8,128)(2,1)}, bf16[128,2048]{1,0:T(8,128)(2,1)S(1)}, u32[]{:S(2)}, u32[]{:S(2)}) collective-permute-start(bf16[128,2048]{1,0:T(8,128)(2,1)} %get-tuple-element.230), channel_id=1, source_target_pairs={{3,2},{2,1},{1,0},{7,6},{6,5},{5,4},{11,10},{10,9},{9,8},{15,14},{... | collective-permute-start | bytes 1572872 | tf_op jit(solution)/shard_map/ppermute | solution.py:218
  353.5 19.0 %collective-permute-start.33 = (bf16[128,2048]{1,0:T(8,128)(2,1)S(1)}, bf16[128,2048]{1,0:T(8,128)(2,1)S(1)}, u32[]{:S(2)}, u32[]{:S(2)}) collective-permute-start(bf16[128,2048]{1,0:T(8,128)(2,1)S(1)} %get-tuple-element.236.refs_0_), channel_id=1, source_target_pairs={{0,1},{1,2},{2,3},{4,5},{5,6},{6,7},{8,9},{9,10},{10,11},{12,13},{... | collective-permute-start | bytes 1572872 | tf_op jit(solution)/shard_map/ppermute | solution.py:218
  375.2 25.3 %collective-permute-start.35 = (bf16[128,2048]{1,0:T(8,128)(2,1)}, bf16[128,2048]{1,0:T(8,128)(2,1)}, u32[]{:S(2)}, u32[]{:S(2)}) collective-permute-start(bf16[128,2048]{1,0:T(8,128)(2,1)} %get-tuple-element.239), channel_id=1, source_target_pairs={{0,1},{1,2},{2,3},{4,5},{5,6},{6,7},{8,9},{9,10},{10,11},{12,13},{... | collective-permute-start | bytes 1572872 | tf_op jit(solution)/shard_map/ppermute | solution.py:218
  380.7 32.6 %collective-permute-start.36 = (bf16[128,2048]{1,0:T(8,128)(2,1)}, bf16[128,2048]{1,0:T(8,128)(2,1)}, u32[]{:S(2)}, u32[]{:S(2)}) collective-permute-start(bf16[128,2048]{1,0:T(8,128)(2,1)} %get-tuple-element.240), channel_id=1, source_target_pairs={{1,0},{2,1},{3,2},{5,4},{6,5},{7,6},{9,8},{10,9},{11,10},{13,12},{... | collective-permute-start | bytes 1572872 | tf_op jit(solution)/shard_map/ppermute | solution.py:218
  416.4 320.4 %reduce-scatter.8.cloned.1.call-start = ((), (), s32[]{:S(2)}) async-start(), calls=%async_computation.10 | async-start | bytes 9437184 | tf_op jit(solution)/shard_map/reduce_scatter | solution.py:814
  416.4 19.5 %collective-permute-start.37 = (bf16[128,2048]{1,0:T(8,128)(2,1)}, bf16[128,2048]{1,0:T(8,128)(2,1)}, u32[]{:S(2)}, u32[]{:S(2)}) collective-permute-start(bf16[128,2048]{1,0:T(8,128)(2,1)} %get-tuple-element.244), channel_id=1, source_target_pairs={{0,1},{1,2},{2,3},{4,5},{5,6},{6,7},{8,9},{9,10},{10,11},{12,13},{... | collective-permute-start | bytes 1572872 | tf_op jit(solution)/shard_map/ppermute | solution.py:218
  441.7 311.2 %reduce-scatter.10.cloned.1.call-start = ((), (), s32[]{:S(2)}) async-start(), calls=%async_computation.11 | async-start | bytes 9437184 | tf_op jit(solution)/shard_map/reduce_scatter | solution.py:814
  443.6 27.6 %collective-permute-start.39 = (bf16[128,2048]{1,0:T(8,128)(2,1)}, bf16[128,2048]{1,0:T(8,128)(2,1)}, u32[]{:S(2)}, u32[]{:S(2)}) collective-permute-start(bf16[128,2048]{1,0:T(8,128)(2,1)} %get-tuple-element.250), channel_id=1, source_target_pairs={{0,1},{1,2},{2,3},{4,5},{5,6},{6,7},{8,9},{9,10},{10,11},{12,13},{... | collective-permute-start | bytes 1572872 | tf_op jit(solution)/shard_map/ppermute | solution.py:218
  448.9 22.3 %collective-permute-start.40 = (bf16[128,2048]{1,0:T(8,128)(2,1)}, bf16[128,2048]{1,0:T(8,128)(2,1)}, u32[]{:S(2)}, u32[]{:S(2)}) collective-permute-start(bf16[128,2048]{1,0:T(8,128)(2,1)} %get-tuple-element.251), channel_id=1, source_target_pairs={{3,2},{2,1},{1,0},{7,6},{6,5},{5,4},{11,10},{10,9},{9,8},{15,14},{... | collective-permute-start | bytes 1572872 | tf_op jit(solution)/shard_map/ppermute | solution.py:218
  476.4 17.7 %collective-permute-start.43 = (bf16[2,256,256]{2,1,0:T(8,128)(2,1)}, bf16[2,256,256]{2,1,0:T(8,128)(2,1)S(1)}, u32[]{:S(2)}, u32[]{:S(2)}) collective-permute-start(bf16[2,256,256]{2,1,0:T(8,128)(2,1)} %get-tuple-element.262), channel_id=1, source_target_pairs={{0,4},{4,0},{1,5},{5,1},{2,6},{6,2},{3,7},{7,3},{8,12},{12,8},{9,1... | collective-permute-start | bytes 786440 | tf_op jit(solution)/shard_map/ppermute | solution.py:799
  486.0 17.1 %collective-permute-start.41 = (bf16[128,2048]{1,0:T(8,128)(2,1)}, bf16[128,2048]{1,0:T(8,128)(2,1)}, u32[]{:S(2)}, u32[]{:S(2)}) collective-permute-start(bf16[128,2048]{1,0:T(8,128)(2,1)} %get-tuple-element.259.refs_0_), channel_id=1, source_target_pairs={{0,1},{1,2},{2,3},{4,5},{5,6},{6,7},{8,9},{9,10},{10,11},{12,13},{... | collective-permute-start | bytes 1572872 | tf_op jit(solution)/shard_map/ppermute | solution.py:218
  529.8 226.0 %reduce-scatter.14.cloned.1.call-start = ((), (), s32[]{:S(2)}) async-start(), calls=%async_computation.13 | async-start | bytes 2359296 | tf_op jit(solution)/shard_map/reduce_scatter | solution.py:814
  553.4 23.5 %collective-permute-start.50 = (bf16[128,2048]{1,0:T(8,128)(2,1)}, bf16[128,2048]{1,0:T(8,128)(2,1)}, u32[]{:S(2)}, u32[]{:S(2)}) collective-permute-start(bf16[128,2048]{1,0:T(8,128)(2,1)} %get-tuple-element.273), channel_id=1, source_target_pairs={{0,1},{1,2},{2,3},{4,5},{5,6},{6,7},{8,9},{9,10},{10,11},{12,13},{... | collective-permute-start | bytes 1572872 | tf_op jit(solution)/shard_map/ppermute | solution.py:218
  555.7 21.1 %collective-permute-start.51 = (bf16[128,2048]{1,0:T(8,128)(2,1)}, bf16[128,2048]{1,0:T(8,128)(2,1)}, u32[]{:S(2)}, u32[]{:S(2)}) collective-permute-start(bf16[128,2048]{1,0:T(8,128)(2,1)} %get-tuple-element.274), channel_id=1, source_target_pairs={{3,2},{2,1},{1,0},{7,6},{6,5},{5,4},{11,10},{10,9},{9,8},{15,14},{... | collective-permute-start | bytes 1572872 | tf_op jit(solution)/shard_map/ppermute | solution.py:218
  585.0 17.7 %collective-permute-start.52 = (bf16[128,2048]{1,0:T(8,128)(2,1)}, bf16[128,2048]{1,0:T(8,128)(2,1)}, u32[]{:S(2)}, u32[]{:S(2)}) collective-permute-start(bf16[128,2048]{1,0:T(8,128)(2,1)} %fusion.48.refs_0_), channel_id=1, source_target_pairs={{0,1},{1,2},{2,3},{4,5},{5,6},{6,7},{8,9},{9,10},{10,11},{12,13},{... | collective-permute-start | bytes 1572872 | tf_op jit(solution)/shard_map/ppermute | solution.py:218
  648.9 108.7 %reduce-scatter.12.cloned.1.call-start = ((), (), s32[]{:S(2)}) async-start(), calls=%async_computation.12 | async-start | bytes 3538944 | tf_op jit(solution)/shard_map/reduce_scatter | solution.py:814
  669.7 17.5 %collective-permute-start.63 = (bf16[128,2048]{1,0:T(8,128)(2,1)}, bf16[128,2048]{1,0:T(8,128)(2,1)}, u32[]{:S(2)}, u32[]{:S(2)}) collective-permute-start(bf16[128,2048]{1,0:T(8,128)(2,1)} %fusion.56.refs_0_), channel_id=1, source_target_pairs={{0,1},{1,2},{2,3},{4,5},{5,6},{6,7},{8,9},{9,10},{10,11},{12,13},{... | collective-permute-start | bytes 1572872 | tf_op jit(solution)/shard_map/ppermute | solution.py:218
  (133 other events, 1487.6 us)
Sparse Core Ops, SparseCore 0:
  41.5 56.9 all-gather.3
  100.4 57.8 all-gather.5
  160.2 54.2 all-gather.7
  300.1 112.3 all-reduce.1
  416.5 77.8 reduce-scatter.5
  498.3 71.4 reduce-scatter.7
  573.3 71.4 reduce-scatter.9
  649.0 40.8 reduce-scatter.13
  693.8 46.3 reduce-scatter.11

commit v5 on v4

--- a/solution.py
+++ b/solution.py
@@ -235,6 +235,44 @@
         lax.rem(lane, 64) < 32, pltpu.roll(values, 96, 1), pltpu.roll(values, 32, 1)
     )
     return values * cosine + swapped * sine
+
+
+def turn_back_kernel(k_width, dq_ref, b0_ref, b1_ref, b2_ref, cos_ref, sin_ref, out_ref):
+    cosine, sine = cos_ref[...], sin_ref[...]
+    q_width = dq_ref.shape[1]
+    for begin in range(0, q_width, 128):
+        piece = dq_ref[:, begin : begin + 128].astype(F32)
+        out_ref[:, begin : begin + 128] = turn(piece, cosine, sine).astype(BF)
+    for begin in range(0, b0_ref.shape[1], 128):
+        piece = sum(
+            ref[:, begin : begin + 128].astype(F32) for ref in (b0_ref, b1_ref, b2_ref)
+        )
+        if begin < k_width:
+            piece = turn(piece, cosine, sine)
+        out_ref[:, q_width + begin : q_width + begin + 128] = piece.astype(BF)
+
+
+def turn_back_call(dq, parts, cosine, sine, k_width):
+    rows, q_width = dq.shape
+    kv_width = parts[0].shape[1]
+    tile = min(256, rows)
+
+    def tall(wide):
+        return pl.BlockSpec((tile, wide), lambda i: (i, 0))
+
+    return pl.pallas_call(
+        functools.partial(turn_back_kernel, k_width),
+        grid=(rows // tile,),
+        in_specs=[tall(q_width)] + [tall(kv_width)] * 3 + [tall(128)] * 2,
+        out_specs=tall(q_width + kv_width),
+        out_shape=jax.ShapeDtypeStruct((rows, q_width + kv_width), BF),
+        cost_estimate=pl.CostEstimate(
+            flops=4 * rows * (q_width + kv_width),
+            bytes_accessed=4 * rows * (q_width + 2 * kv_width),
+            transcendentals=0,
+        ),
+        name="turn_back",
+    )(dq, *parts, cosine, sine)
 
 
 def place_kernel(count, me_ref, *refs):
@@ -692,6 +730,10 @@
     def own(x):
         return lax.dynamic_slice_in_dim(x, me * own_rows, own_rows, 0)
 
+    def own_of(x, chunk):
+        flat = x.reshape(seqs * block, width)
+        return lax.dynamic_slice_in_dim(flat, chunk * rows + me * own_rows, own_rows, 0)
+
     def blocks(x):
         return x.reshape(ways, own_rows, width)
 
@@ -700,7 +742,7 @@
         s = {}
         tok = chunk_of(tokens, c).reshape(rows, width)
         s["tok"] = tok
-        s["cot"] = chunk_of(cotangent, c).reshape(rows, width)
+        s["own_tok"], s["own_cot"] = own_of(tokens, c), own_of(cotangent, c)
         s["cos"] = lax.slice_in_dim(cosine, c * rows, (c + 1) * rows, axis=0)
         s["sin"] = lax.slice_in_dim(sine, c * rows, (c + 1) * rows, axis=0)
         s["sin_back"] = -s["sin"]
@@ -764,7 +806,7 @@
         return attended, lse, attn
 
     def enter_ffn(s, summed):
-        s["residual"] = own(s["tok"]).astype(F32) + summed
+        s["residual"] = s["own_tok"].astype(F32) + summed
         return (s["residual"] * inverse_rms(s["residual"]) * gain_two).astype(BF)
 
     turned = {}
@@ -785,7 +827,7 @@
 
     def leave_ffn(s, summed):
         d_norm, s["gain_two"] = norm_back(s["residual"], gain_two, summed)
-        s["d_resid"] = own(s["cot"]).astype(F32) + d_norm
+        s["d_resid"] = s["own_cot"].astype(F32) + d_norm
         return s["d_resid"].astype(BF)
 
     def attend_back(s, d_attn):
@@ -799,15 +841,15 @@
         from1 = lax.ppermute(b1, "core", FLIP)
         far = (b2.astype(F32) + from3.astype(F32)).astype(BF)
         from2 = lax.ppermute(far, "yy", FLIP)
-        d_kv = b0.astype(F32) + from1.astype(F32) + from2.astype(F32)
-        d_q = turn_call(dq.reshape(rows, q_width), s["cos"], s["sin_back"], q_width)
-        d_kv = turn_call(d_kv.reshape(rows, kv_width), s["cos"], s["sin_back"], k_width)
-        d_qkv = jnp.concatenate([d_q, d_kv], axis=1)
+        kv_parts = [x.reshape(rows, kv_width) for x in (b0, from1, from2)]
+        d_qkv = turn_back_call(
+            dq.reshape(rows, q_width), kv_parts, s["cos"], s["sin_back"], k_width
+        )
         full_qkv = jnp.concatenate([full_q, full_kv], axis=1)
         return d_qkv, dot_cols(d_qkv, full_qkv).astype(BF)
 
     def leave_attention(s, summed):
-        d_norm, s["gain_one"] = norm_back(own(s["tok"]).astype(F32), gain_one, summed)
+        d_norm, s["gain_one"] = norm_back(s["own_tok"].astype(F32), gain_one, summed)
         return (s["d_resid"] + d_norm).astype(BF)
 
     def scattered(grad):
@@ -823,11 +865,6 @@
 
     def whole(rows_of):
         return rows_of.reshape(per_chunk, block, width)
-
-    def leave_layer(s, ffn):
-        mine = own(ffn).astype(F32) + s["residual"]
-        ffn = lax.dynamic_update_slice_in_dim(ffn, mine.astype(BF), me * own_rows, 0)
-        s["output"] = lax.psum(ffn, "tensor")
 
     axes = ("tensor", "core", "yy", "fsdp")
     first["normed_one"], kv = slot(
@@ -865,7 +902,7 @@
     (back,) = slot([gather_a1], ffn_back, (first["d_gate"], first["d_up"]))
     sum_d0 = LineSum(blocks(back))
     (ffn,) = slot([Both(gather_a1, sum_d0)], ffn_out, (first["hidden"],))
-    leave_layer(first, ffn)
+    sum_f0 = LineSum(blocks(ffn))
     slot([Both(gather_a1, sum_d0)])
     second["normed_two"] = gather_a1.result().reshape(rows, width)
     second["hidden"], second["d_gate"], second["d_up"] = slot(
@@ -880,7 +917,7 @@
         (cot_rows,) + of_both("hidden"),
     )
     (grad,) = slot(
-        [Both(gather_d0, sum_d1)],
+        [Both(gather_d0, sum_d1), sum_f0],
         weight_grad,
         of_both("normed_two", "d_gate"),
         scattered,
@@ -889,29 +926,30 @@
     down_grad = clock.launched
     first["d_attn"] = gather_d0.result().reshape(rows, width)
     pieces = slot(
-        [sum_d1], functools.partial(attend_back, first), (first["d_attn"],), scattered, grad
+        [sum_d1, sum_f0], functools.partial(attend_back, first), (first["d_attn"],), scattered, grad
     )
     gate_grad = clock.launched
     gather_d1 = LineGather(leave_ffn(second, sum_d1.result()))
     first["d_qkv"], back = slot(
-        [gather_d1], functools.partial(project_back, first), pieces
+        [gather_d1, sum_f0], functools.partial(project_back, first), pieces
     )
     sum_n0 = LineSum(blocks(back))
+    gather_f0 = LineGather((first["residual"] + sum_f0.result()).astype(BF))
     (grad,) = slot(
-        [Both(gather_d1, sum_n0)], weight_grad, of_both("normed_two", "d_up")
-    )
-    slot([Both(gather_d1, sum_n0)], None, (), scattered, grad)
+        [Both(gather_d1, sum_n0), gather_f0], weight_grad, of_both("normed_two", "d_up")
+    )
+    slot([Both(gather_d1, sum_n0), gather_f0], None, (), scattered, grad)
     up_grad = clock.launched
     second["d_attn"] = gather_d1.result().reshape(rows, width)
     pieces = slot(
-        [sum_n0], functools.partial(attend_back, second), (second["d_attn"],)
+        [sum_n0, gather_f0], functools.partial(attend_back, second), (second["d_attn"],)
     )
     gather_n0 = LineGather(leave_attention(first, sum_n0.result()))
     second["d_qkv"], back = slot(
         [gather_n0], functools.partial(project_back, second), pieces
     )
     sum_n1 = LineSum(blocks(back))
-    clock.expect(first["output"])
+    first["output"] = gather_f0.result()
     (grad,) = slot(
         [Both(gather_n0, sum_n1)], weight_grad, of_both("normed_one", "d_qkv")
     )
@@ -937,6 +975,7 @@
     slot([gather_n1, gains_one])
     slot([Both(gather_n1, sum_f1), gains_one])
     clock.expect(whole(first["input_grad"]))
+    clock.expect(first["output"])
     slot([Both(gather_n1, sum_f1), gains_one])
     second["input_grad"] = gather_n1.result()
     clock.expect(down_grad)

time: 805 us -> 794 us (0.986)
  waiting for transfers between devices: 160 us -> 127 us
  starting transfers between devices: 164 us -> 194 us
    ppermute x76 -> x88, waiting for transfers between devices: 156 us -> 121 us  [slot(): moved = [lax.ppermute(g, s[1], s[2]) for g, s in zip(gated, flat)]]
    ppermute x76 -> x88, starting transfers between devices: 158 us -> 190 us  [slot(): moved = [lax.ppermute(g, s[1], s[2]) for g, s in zip(gated, flat)]]
    pallas_call x8 -> x4, Pallas kernels: 17.8 us -> 9.18 us  [turn_call(): pl.pallas_call(functools.partial(turn_kernel, turned), grid=(rows // tile...]
    convert_element_type x8 -> x10, other arithmetic: 17.7 us -> 24.3 us  [sends(): to_left = (to_left.astype(F32) + self.from_right.astype(F32)).astype(BF)]
    pallas_call x7 -> x8, Pallas kernels: 22.1 us -> 25.5 us  [place_call(): pl.pallas_call(functools.partial(place_kernel, count), grid_spec=pltpu.Pr...]
  transfers between devices with their start and end apart: 91 -> 102, of which waited for: 37 -> 35; matrix products, arithmetic and copies ran while one was open for 28% -> 26% of each run, Pallas kernels for 26% -> 26%
where the time goes in v5:
time: 794 us; the launch traced here: 786 us
  Pallas kernels  210 us (26%)
  starting transfers between devices  194 us (24%)
  waiting for transfers between devices  127 us (16%)
  other arithmetic  109 us (14%)
  matrix products  88.5 us (11%)
  local copies, waits for them, and re-layouts  41.7 us (5%)
  between operations  16.3 us (2%)
    ppermute x88, starting transfers between devices, slot(): moved = [lax.ppermute(g, s[1], s[2]) for g, s in zip(gated, flat)]  190 us
    ppermute x88, waiting for transfers between devices, slot(): moved = [lax.ppermute(g, s[1], s[2]) for g, s in zip(gated, flat)]  121 us
    dot_general x5, matrix products, dot_rows(): lax.dot_general(left_in, right_in, (((0,), (0,)), ((), ())), preferred_el...  50.6 us
    pallas_call x4, Pallas kernels, product_call(): pl.pallas_call(functools.partial(product_kernel, count, turned), grid=(wi...  48.9 us
    pallas_call x2, Pallas kernels, ffn_call(): pl.pallas_call(ffn_kernel, grid=(units // tile,), in_specs=[whole, rows_o...  40.1 us
    pallas_call x2, Pallas kernels, attend_back_call(): pl.pallas_call(functools.partial(attend_back_kernel, group), grid_spec=pl...  32.2 us
    select_n x12, other arithmetic, sends(): value = jnp.where(rank >= first, whole[0], part[0])  29 us
    pallas_call x8, Pallas kernels, place_call(): pl.pallas_call(functools.partial(place_kernel, count), grid_spec=pltpu.Pr...  25.5 us
  transfers between devices with their start and end apart: 102, of which 35 were waited for; matrix products, arithmetic and copies ran while one was open for 26% of the time, Pallas kernels for 26%

profile of v5, /device:TPU:0, one launch (start us, length us, event | category | flops | bytes accessed | tf_op | source)
XLA Modules:
  0.0 786.4 jit_solution(2166233923417456663)
XLA Ops:
  49.4 6.4 spread.1
  79.9 11.5 %attend.2 = (bf16[2,256,512]{2,1,0:T(8,128)(2,1)}, f32[2,8,256]{2,1,0:T(8,128)}) custom-call(s32[5]{0:T(128)} %stack.34.place_ref, bf16[2,256,512]{2,1,0:T(8,128)(2,1)} %bitcast.347, bf16[2,256,256]{2,1,0:T(8,128)(2,1)} %bitcast.372, bf16[2,256,256]{2,1,0:T(8,128)(2,1)} %copy-done.79, bf16[2,256,256]{2,1,0:T(8,128)(2,1)} %copy-done.78, ...), custom_call_target="tpu_custom_call" | custom-call | flops 4294967296 | bytes 1572864 | tf_op jit(solution)/shard_map/attend/pallas_call | solution.py:520
  120.9 9.4 %collective-permute-done.10 = bf16[128,2048]{1,0:T(8,128)(2,1)S(1)} collective-permute-done((bf16[128,2048]{1,0:T(8,128)(2,1)}, bf16[128,2048]{1,0:T(8,128)(2,1)S(1)}, u32[]{:S(2)}, u32[]{:S(2)}) %collective-permute-start.10) | collective-permute-done | bytes 524320 | tf_op jit(solution)/shard_map/ppermute | solution.py:218
  133.0 5.2 collective-permute-start.14
  140.4 7.9 collective-permute-done.14
  159.2 11.4 %attend.3 = (bf16[2,256,512]{2,1,0:T(8,128)(2,1)}, f32[2,8,256]{2,1,0:T(8,128)}) custom-call(s32[5]{0:T(128)} %stack.34.place_ref, bf16[2,256,512]{2,1,0:T(8,128)(2,1)} %bitcast.345, bf16[2,256,256]{2,1,0:T(8,128)(2,1)} %bitcast.366, bf16[2,256,256]{2,1,0:T(8,128)(2,1)} %copy-done.76, bf16[2,256,256]{2,1,0:T(8,128)(2,1)} %copy-done.75, ...), custom_call_target="tpu_custom_call" | custom-call | flops 4294967296 | bytes 1572864 | tf_op jit(solution)/shard_map/attend/pallas_call | solution.py:520
  182.0 9.9 %turn_over.2.refs_2_ = bf16[2048,2048]{1,0:T(8,128)(2,1)} custom-call(bf16[2048,2048]{1,0:T(8,128)(2,1)} %all-gather.4.cloned.1.call-done.x_ref.g_ref), custom_call_target="tpu_custom_call" | custom-call | bytes 16777216 | tf_op jit(solution)/shard_map/turn_over/pallas_call | solution.py:425
  201.4 10.0 %turn_over.3.refs_3_ = bf16[2048,2048]{1,0:T(8,128)(2,1)} custom-call(bf16[2048,2048]{1,0:T(8,128)(2,1)} %all-gather.6.cloned.1.call-done.x_ref.u_ref), custom_call_target="tpu_custom_call" | custom-call | bytes 16777216 | tf_op jit(solution)/shard_map/turn_over/pallas_call | solution.py:425
  223.3 20.1 %ffn.2 = (bf16[512,2048]{1,0:T(8,128)(2,1)}, bf16[512,2048]{1,0:T(8,128)(2,1)}, bf16[512,2048]{1,0:T(8,128)(2,1)}) custom-call(bf16[512,2048]{1,0:T(8,128)(2,1)} %bitcast.333, bf16[1024,2048]{1,0:T(8,128)(2,1)} %bitcast.361, bf16[2048,2048]{1,0:T(8,128)(2,1)} %all-gather.4.cloned.1.call-done.x_ref.g_ref, ...), custom_call_target="tpu_custom_call" | custom-call | flops 12884901888 | bytes 31457280 | tf_op jit(solution)/shard_map/ffn/pallas_call | solution.py:368
  251.3 13.8 %product.4 = bf16[512,2048]{1,0:T(8,128)(2,1)} custom-call(bf16[512,2048]{1,0:T(8,128)(2,1)} %get-tuple-element.262.refs_0_, bf16[512,2048]{1,0:T(8,128)(2,1)} %get-tuple-element.289.refs_1_, bf16[2048,2048]{1,0:T(8,128)(2,1)} %turn_over.2.refs_2_, bf16[2048,2048]{1,0:T(8,128)(2,1)} %turn_over.3.refs_3_), custom_call_target="tpu_custom_call" | custom-call | flops 8589934592 | bytes 20971520 | tf_op jit(solution)/shard_map/product/pallas_call | solution.py:402
  273.6 10.6 %product.5 = bf16[512,2048]{1,0:T(8,128)(2,1)} custom-call(bf16[512,2048]{1,0:T(8,128)(2,1)} %get-tuple-element.254.refs_0_, bf16[2048,2048]{1,0:T(8,128)(2,1)} %all-gather.8.cloned.1.call-done.d_ref.refs_1_), custom_call_target="tpu_custom_call" | custom-call | flops 4294967296 | bytes 10485760 | tf_op jit(solution)/shard_map/product/pallas_call | solution.py:402
  311.9 20.1 %ffn.3 = (bf16[512,2048]{1,0:T(8,128)(2,1)}, bf16[512,2048]{1,0:T(8,128)(2,1)}, bf16[512,2048]{1,0:T(8,128)(2,1)}) custom-call(bf16[512,2048]{1,0:T(8,128)(2,1)} %bitcast.338, bf16[1024,2048]{1,0:T(8,128)(2,1)} %bitcast.362, bf16[2048,2048]{1,0:T(8,128)(2,1)} %all-gather.4.cloned.1.call-done.x_ref.g_ref, ...), custom_call_target="tpu_custom_call" | custom-call | flops 12884901888 | bytes 31457280 | tf_op jit(solution)/shard_map/ffn/pallas_call | solution.py:368
  336.7 5.3 collective-permute-start.33
  343.5 13.8 %product.6 = bf16[512,2048]{1,0:T(8,128)(2,1)} custom-call(bf16[512,2048]{1,0:T(8,128)(2,1)} %get-tuple-element.263.refs_0_, bf16[512,2048]{1,0:T(8,128)(2,1)} %get-tuple-element.290.refs_1_, bf16[2048,2048]{1,0:T(8,128)(2,1)} %turn_over.2.refs_2_, bf16[2048,2048]{1,0:T(8,128)(2,1)} %turn_over.3.refs_3_), custom_call_target="tpu_custom_call" | custom-call | flops 8589934592 | bytes 20971520 | tf_op jit(solution)/shard_map/product/pallas_call | solution.py:402
  359.9 5.5 collective-permute-start.35
  366.7 13.7 %convolution_convert_fusion.2 = bf16[2048,2048]{1,0:T(8,128)(2,1)} fusion(bf16[1024,2048]{1,0:T(8,128)(2,1)} %bitcast.364, bf16[512,2048]{1,0:T(8,128)(2,1)S(1)} %copy-done.87, bf16[512,2048]{1,0:T(8,128)(2,1)} %get-tuple-element.254.refs_0_), kind=kOutput, calls=%fused_computation.2 | convolution fusion | flops 8602517504 | bytes 16777216 | tf_op jit(solution)/shard_map/dot_general | solution.py:36
  384.0 5.4 collective-permute-start.37
  390.7 5.3 collective-permute-start.39
  397.5 14.5 %convolution_convert_fusion.1 = bf16[2048,2048]{1,0:T(8,128)(2,1)} fusion(bf16[512,2048]{1,0:T(8,128)(2,1)} %bitcast.339, bf16[512,2048]{1,0:T(8,128)(2,1)} %bitcast.334, bf16[512,2048]{1,0:T(8,128)(2,1)} %get-tuple-element.263.refs_0_, bf16[512,2048]{1,0:T(8,128)(2,1)} %get-tuple-element.262.refs_0_), kind=kOutput, calls=%fused_computation.1 | convolution fusion | flops 8610906112 | bytes 16777216 | tf_op jit(solution)/shard_map/dot_general | solution.py:36
  434.9 16.0 %attend_back.2 = (bf16[2,256,512]{2,1,0:T(8,128)(2,1)}, bf16[2,256,256]{2,1,0:T(8,128)(2,1)}, bf16[2,256,256]{2,1,0:T(8,128)(2,1)}, bf16[2,256,256]{2,1,0:T(8,128)(2,1)}, bf16[2,256,256]{2,1,0:T(8,128)(2,1)}) custom-call(s32[5]{0:T(128)} %stack.34.place_ref, bf16[2,256,512]{2,1,0:T(8,128)(2,1)} %bitcast.348, bf16[2,256,256]{2,1,0:T(8,128)(2,1)} %bitcast.373, ...), custom_call_target="tpu_custom_call" | custom-call | flops 10737418240 | bytes 3145728 | tf_op jit(solution)/shard_map/attend_back/pallas_call | solution.py:640
  461.3 5.5 collective-permute-start.47
  474.0 5.3 collective-permute-start.45
  500.5 5.3 collective-permute-start.52
  507.2 11.4 %convolution_convert_fusion = bf16[2048,2048]{1,0:T(8,128)(2,1)} fusion(bf16[512,2048]{1,0:T(8,128)(2,1)S(1)} %bitcast.340, bf16[512,2048]{1,0:T(8,128)(2,1)S(1)} %bitcast.335, bf16[512,2048]{1,0:T(8,128)(2,1)S(1)} %copy-done.89, bf16[512,2048]{1,0:T(8,128)(2,1)S(1)} %copy-done.88), kind=kOutput, calls=%fused_computation | convolution fusion | flops 8610906112 | bytes 16777216 | tf_op jit(solution)/shard_map/dot_general | solution.py:36
  536.2 8.3 %collective-permute-done.58.refs_6_ = bf16[128,2048]{1,0:T(8,128)(2,1)S(1)} collective-permute-done((bf16[128,2048]{1,0:T(8,128)(2,1)}, bf16[128,2048]{1,0:T(8,128)(2,1)S(1)}, u32[]{:S(2)}, u32[]{:S(2)}) %collective-permute-start.58) | collective-permute-done | bytes 524320 | tf_op jit(solution)/shard_map/ppermute | solution.py:218
  562.8 16.2 %attend_back.3 = (bf16[2,256,512]{2,1,0:T(8,128)(2,1)}, bf16[2,256,256]{2,1,0:T(8,128)(2,1)}, bf16[2,256,256]{2,1,0:T(8,128)(2,1)}, bf16[2,256,256]{2,1,0:T(8,128)(2,1)}, bf16[2,256,256]{2,1,0:T(8,128)(2,1)}) custom-call(s32[5]{0:T(128)} %stack.34.place_ref, bf16[2,256,512]{2,1,0:T(8,128)(2,1)} %bitcast.346, bf16[2,256,256]{2,1,0:T(8,128)(2,1)} %bitcast.367, ...), custom_call_target="tpu_custom_call" | custom-call | flops 10737418240 | bytes 3145728 | tf_op jit(solution)/shard_map/attend_back/pallas_call | solution.py:640
  586.4 5.3 collective-permute-start.64
  632.2 6.0 fusion.26
  649.7 10.8 %product.7 = bf16[512,2048]{1,0:T(8,128)(2,1)} custom-call(bf16[512,2048]{1,0:T(8,128)(2,1)} %get-tuple-element.324.refs_0_, bf16[2048,2048]{1,0:T(8,128)(2,1)} %all-gather.8.cloned.1.call-done.d_ref.refs_1_), custom_call_target="tpu_custom_call" | custom-call | flops 4294967296 | bytes 10485760 | tf_op jit(solution)/shard_map/product/pallas_call | solution.py:402
  673.2 7.2 collective-permute-done.77
  738.2 5.5 maximum_convert_fusion
  763.2 8.9 %collective-permute-done.93.refs_6_ = bf16[128,2048]{1,0:T(8,128)(2,1)} collective-permute-done((bf16[128,2048]{1,0:T(8,128)(2,1)}, bf16[128,2048]{1,0:T(8,128)(2,1)}, u32[]{:S(2)}, u32[]{:S(2)}) %collective-permute-start.93) | collective-permute-done | bytes 524320 | tf_op jit(solution)/shard_map/ppermute | solution.py:218
  (516 shorter events, 458.7 us)
Async XLA Ops:
  7.2 168.9 %all-gather.4.cloned.1.call-start = ((), (), s32[]{:S(2)}) async-start(), calls=%async_computation.5 | async-start | bytes 9437184 | tf_op jit(solution)/shard_map/all_gather | solution.py:763
  41.8 155.2 %all-gather.6.cloned.1.call-start = ((), (), s32[]{:S(2)}) async-start(), calls=%async_computation.6 | async-start | bytes 9437184 | tf_op jit(solution)/shard_map/all_gather | solution.py:763
  42.6 180.7 %all-gather.8.cloned.1.call-start = ((), (), s32[]{:S(2)}) async-start(), calls=%async_computation.7 | async-start | bytes 9437184 | tf_op jit(solution)/shard_map/all_gather | solution.py:763
  43.3 669.8 %reduce-scatter.6.cloned.1.call-start = ((), (), s32[]{:S(2)}) async-start(), calls=%async_computation.8 | async-start | bytes 9437184 | tf_op jit(solution)/shard_map/reduce_scatter | solution.py:856
  218.6 24.8 %collective-permute-start.23 = (bf16[128,2048]{1,0:T(8,128)(2,1)S(1)}, bf16[128,2048]{1,0:T(8,128)(2,1)S(1)}, u32[]{:S(2)}, u32[]{:S(2)}) collective-permute-start(bf16[128,2048]{1,0:T(8,128)(2,1)S(1)} %get-tuple-element.226), channel_id=1, source_target_pairs={{0,1},{1,2},{2,3},{4,5},{5,6},{6,7},{8,9},{9,10},{10,11},{12,13},{... | collective-permute-start | bytes 1572872 | tf_op jit(solution)/shard_map/ppermute | solution.py:218
  221.9 21.4 %collective-permute-start.24 = (bf16[128,2048]{1,0:T(8,128)(2,1)S(1)}, bf16[128,2048]{1,0:T(8,128)(2,1)S(1)}, u32[]{:S(2)}, u32[]{:S(2)}) collective-permute-start(bf16[128,2048]{1,0:T(8,128)(2,1)S(1)} %get-tuple-element.227), channel_id=1, source_target_pairs={{3,2},{2,1},{1,0},{7,6},{6,5},{5,4},{11,10},{10,9},{9,8},{15,14},{... | collective-permute-start | bytes 1572872 | tf_op jit(solution)/shard_map/ppermute | solution.py:218
  308.2 23.8 %collective-permute-start.31 = (bf16[128,2048]{1,0:T(8,128)(2,1)}, bf16[128,2048]{1,0:T(8,128)(2,1)S(1)}, u32[]{:S(2)}, u32[]{:S(2)}) collective-permute-start(bf16[128,2048]{1,0:T(8,128)(2,1)} %get-tuple-element.241), channel_id=1, source_target_pairs={{0,1},{1,2},{2,3},{4,5},{5,6},{6,7},{8,9},{9,10},{10,11},{12,13},{... | collective-permute-start | bytes 1572872 | tf_op jit(solution)/shard_map/ppermute | solution.py:218
  310.6 21.4 %collective-permute-start.32 = (bf16[128,2048]{1,0:T(8,128)(2,1)}, bf16[128,2048]{1,0:T(8,128)(2,1)S(1)}, u32[]{:S(2)}, u32[]{:S(2)}) collective-permute-start(bf16[128,2048]{1,0:T(8,128)(2,1)} %get-tuple-element.242), channel_id=1, source_target_pairs={{3,2},{2,1},{1,0},{7,6},{6,5},{5,4},{11,10},{10,9},{9,8},{15,14},{... | collective-permute-start | bytes 1572872 | tf_op jit(solution)/shard_map/ppermute | solution.py:218
  336.7 20.6 %collective-permute-start.33 = (bf16[128,2048]{1,0:T(8,128)(2,1)}, bf16[128,2048]{1,0:T(8,128)(2,1)}, u32[]{:S(2)}, u32[]{:S(2)}) collective-permute-start(bf16[128,2048]{1,0:T(8,128)(2,1)} %get-tuple-element.248.refs_0_), channel_id=1, source_target_pairs={{0,1},{1,2},{2,3},{4,5},{5,6},{6,7},{8,9},{9,10},{10,11},{12,13},{... | collective-permute-start | bytes 1572872 | tf_op jit(solution)/shard_map/ppermute | solution.py:218
  359.9 20.5 %collective-permute-start.35 = (bf16[128,2048]{1,0:T(8,128)(2,1)}, bf16[128,2048]{1,0:T(8,128)(2,1)}, u32[]{:S(2)}, u32[]{:S(2)}) collective-permute-start(bf16[128,2048]{1,0:T(8,128)(2,1)} %get-tuple-element.251), channel_id=1, source_target_pairs={{0,1},{1,2},{2,3},{4,5},{5,6},{6,7},{8,9},{9,10},{10,11},{12,13},{... | collective-permute-start | bytes 1572872 | tf_op jit(solution)/shard_map/ppermute | solution.py:218
  384.0 343.7 %reduce-scatter.8.cloned.1.call-start = ((), (), s32[]{:S(2)}) async-start(), calls=%async_computation.9 | async-start | bytes 9437184 | tf_op jit(solution)/shard_map/reduce_scatter | solution.py:856
  384.0 28.0 %collective-permute-start.37 = (bf16[128,2048]{1,0:T(8,128)(2,1)}, bf16[128,2048]{1,0:T(8,128)(2,1)}, u32[]{:S(2)}, u32[]{:S(2)}) collective-permute-start(bf16[128,2048]{1,0:T(8,128)(2,1)} %get-tuple-element.256), channel_id=1, source_target_pairs={{0,1},{1,2},{2,3},{4,5},{5,6},{6,7},{8,9},{9,10},{10,11},{12,13},{... | collective-permute-start | bytes 1572872 | tf_op jit(solution)/shard_map/ppermute | solution.py:218
  389.4 22.6 %collective-permute-start.38 = (bf16[128,2048]{1,0:T(8,128)(2,1)}, bf16[128,2048]{1,0:T(8,128)(2,1)}, u32[]{:S(2)}, u32[]{:S(2)}) collective-permute-start(bf16[128,2048]{1,0:T(8,128)(2,1)} %get-tuple-element.257), channel_id=1, source_target_pairs={{1,0},{2,1},{3,2},{5,4},{6,5},{7,6},{9,8},{10,9},{11,10},{13,12},{... | collective-permute-start | bytes 1572872 | tf_op jit(solution)/shard_map/ppermute | solution.py:218
  390.7 27.4 %collective-permute-start.39 = (bf16[128,2048]{1,0:T(8,128)(2,1)}, bf16[128,2048]{1,0:T(8,128)(2,1)}, u32[]{:S(2)}, u32[]{:S(2)}) collective-permute-start(bf16[128,2048]{1,0:T(8,128)(2,1)} %get-tuple-element.258), channel_id=1, source_target_pairs={{0,1},{4,5},{8,9},{12,13},{16,17},{20,21},{24,25},{28,29}} | collective-permute-start | bytes 1572872 | tf_op jit(solution)/shard_map/ppermute | solution.py:218
  396.1 22.1 %collective-permute-start.40 = (bf16[128,2048]{1,0:T(8,128)(2,1)}, bf16[128,2048]{1,0:T(8,128)(2,1)}, u32[]{:S(2)}, u32[]{:S(2)}) collective-permute-start(bf16[128,2048]{1,0:T(8,128)(2,1)} %get-tuple-element.259), channel_id=1, source_target_pairs={{3,2},{7,6},{11,10},{15,14},{19,18},{23,22},{27,26},{31,30}} | collective-permute-start | bytes 1572872 | tf_op jit(solution)/shard_map/ppermute | solution.py:218
  420.8 323.0 %reduce-scatter.10.cloned.1.call-start = ((), (), s32[]{:S(2)}) async-start(), calls=%async_computation.10 | async-start | bytes 9437184 | tf_op jit(solution)/shard_map/reduce_scatter | solution.py:856
  423.4 29.7 %collective-permute-start.43 = (bf16[128,2048]{1,0:T(8,128)(2,1)}, bf16[128,2048]{1,0:T(8,128)(2,1)}, u32[]{:S(2)}, u32[]{:S(2)}) collective-permute-start(bf16[128,2048]{1,0:T(8,128)(2,1)} %get-tuple-element.266), channel_id=1, source_target_pairs={{0,1},{1,2},{4,5},{5,6},{8,9},{9,10},{12,13},{13,14},{16,17},{17,1... | collective-permute-start | bytes 1572872 | tf_op jit(solution)/shard_map/ppermute | solution.py:218
  425.5 27.5 %collective-permute-start.44 = (bf16[128,2048]{1,0:T(8,128)(2,1)}, bf16[128,2048]{1,0:T(8,128)(2,1)}, u32[]{:S(2)}, u32[]{:S(2)}) collective-permute-start(bf16[128,2048]{1,0:T(8,128)(2,1)} %get-tuple-element.267), channel_id=1, source_target_pairs={{3,2},{2,1},{7,6},{6,5},{11,10},{10,9},{15,14},{14,13},{19,18},{18... | collective-permute-start | bytes 1572872 | tf_op jit(solution)/shard_map/ppermute | solution.py:218
  427.0 24.0 %collective-permute-start.41 = (bf16[128,2048]{1,0:T(8,128)(2,1)}, bf16[128,2048]{1,0:T(8,128)(2,1)}, u32[]{:S(2)}, u32[]{:S(2)}) collective-permute-start(bf16[128,2048]{1,0:T(8,128)(2,1)} %get-tuple-element.264), channel_id=1, source_target_pairs={{0,1},{1,2},{2,3},{4,5},{5,6},{6,7},{8,9},{9,10},{10,11},{12,13},{... | collective-permute-start | bytes 1572872 | tf_op jit(solution)/shard_map/ppermute | solution.py:218
  429.1 21.9 %collective-permute-start.42 = (bf16[128,2048]{1,0:T(8,128)(2,1)}, bf16[128,2048]{1,0:T(8,128)(2,1)}, u32[]{:S(2)}, u32[]{:S(2)}) collective-permute-start(bf16[128,2048]{1,0:T(8,128)(2,1)} %get-tuple-element.265), channel_id=1, source_target_pairs={{3,2},{2,1},{1,0},{7,6},{6,5},{5,4},{11,10},{10,9},{9,8},{15,14},{... | collective-permute-start | bytes 1572872 | tf_op jit(solution)/shard_map/ppermute | solution.py:218
  461.3 26.5 %collective-permute-start.47 = (bf16[128,2048]{1,0:T(8,128)(2,1)}, bf16[128,2048]{1,0:T(8,128)(2,1)}, u32[]{:S(2)}, u32[]{:S(2)}) collective-permute-start(bf16[128,2048]{1,0:T(8,128)(2,1)} %get-tuple-element.277.refs_0_), channel_id=1, source_target_pairs={{0,1},{1,2},{2,3},{4,5},{5,6},{6,7},{8,9},{9,10},{10,11},{12,13},{... | collective-permute-start | bytes 1572872 | tf_op jit(solution)/shard_map/ppermute | solution.py:218
  466.8 21.0 %collective-permute-start.48 = (bf16[128,2048]{1,0:T(8,128)(2,1)}, bf16[128,2048]{1,0:T(8,128)(2,1)}, u32[]{:S(2)}, u32[]{:S(2)}) collective-permute-start(bf16[128,2048]{1,0:T(8,128)(2,1)} %get-tuple-element.277.refs_0_), channel_id=1, source_target_pairs={{3,2},{2,1},{1,0},{7,6},{6,5},{5,4},{11,10},{10,9},{9,8},{15,14},{... | collective-permute-start | bytes 1572872 | tf_op jit(solution)/shard_map/ppermute | solution.py:218
  496.9 21.7 %collective-permute-start.53 = (bf16[128,2048]{1,0:T(8,128)(2,1)}, bf16[128,2048]{1,0:T(8,128)(2,1)S(1)}, u32[]{:S(2)}, u32[]{:S(2)}) collective-permute-start(bf16[128,2048]{1,0:T(8,128)(2,1)} %get-tuple-element.284), channel_id=1, source_target_pairs={{0,1},{1,2},{2,3},{4,5},{5,6},{6,7},{8,9},{9,10},{10,11},{12,13},{... | collective-permute-start | bytes 1572872 | tf_op jit(solution)/shard_map/ppermute | solution.py:218
  500.5 21.1 %collective-permute-start.52 = (bf16[128,2048]{1,0:T(8,128)(2,1)}, bf16[128,2048]{1,0:T(8,128)(2,1)}, u32[]{:S(2)}, u32[]{:S(2)}) collective-permute-start(bf16[128,2048]{1,0:T(8,128)(2,1)} %fusion.96.refs_0_), channel_id=1, source_target_pairs={{0,1},{1,2},{2,3},{4,5},{5,6},{6,7},{8,9},{9,10},{10,11},{12,13},{... | collective-permute-start | bytes 1572872 | tf_op jit(solution)/shard_map/ppermute | solution.py:218
  524.7 221.3 %reduce-scatter.14.cloned.1.call-start = ((), (), s32[]{:S(2)}) async-start(), calls=%async_computation.12 | async-start | bytes 2359296 | tf_op jit(solution)/shard_map/reduce_scatter | solution.py:856
  530.3 21.9 %collective-permute-start.56 = (bf16[128,2048]{1,0:T(8,128)(2,1)}, bf16[128,2048]{1,0:T(8,128)(2,1)}, u32[]{:S(2)}, u32[]{:S(2)}) collective-permute-start(bf16[128,2048]{1,0:T(8,128)(2,1)} %collective-permute-done.52.refs_1_), channel_id=1, source_target_pairs={{1,2},{2,3},{5,6},{6,7},{9,10},{10,11},{13,14},{14,15},{17,18},{18... | collective-permute-start | bytes 1572872 | tf_op jit(solution)/shard_map/ppermute | solution.py:218
  531.7 20.4 %collective-permute-start.59 = (bf16[128,2048]{1,0:T(8,128)(2,1)}, bf16[128,2048]{1,0:T(8,128)(2,1)}, u32[]{:S(2)}, u32[]{:S(2)}) collective-permute-start(bf16[128,2048]{1,0:T(8,128)(2,1)} %collective-permute-done.55.refs_4_), channel_id=1, source_target_pairs={{2,1},{1,0},{6,5},{5,4},{10,9},{9,8},{14,13},{13,12},{18,17},{17,1... | collective-permute-start | bytes 1572872 | tf_op jit(solution)/shard_map/ppermute | solution.py:218
  552.2 26.8 %collective-permute-start.62 = (bf16[128,2048]{1,0:T(8,128)(2,1)}, bf16[128,2048]{1,0:T(8,128)(2,1)S(1)}, u32[]{:S(2)}, u32[]{:S(2)}) collective-permute-start(bf16[128,2048]{1,0:T(8,128)(2,1)} %get-tuple-element.297), channel_id=1, source_target_pairs={{0,1},{1,2},{2,3},{4,5},{5,6},{6,7},{8,9},{9,10},{10,11},{12,13},{... | collective-permute-start | bytes 1572872 | tf_op jit(solution)/shard_map/ppermute | solution.py:218
  554.9 24.1 %collective-permute-start.63 = (bf16[128,2048]{1,0:T(8,128)(2,1)}, bf16[128,2048]{1,0:T(8,128)(2,1)S(1)}, u32[]{:S(2)}, u32[]{:S(2)}) collective-permute-start(bf16[128,2048]{1,0:T(8,128)(2,1)} %get-tuple-element.298), channel_id=1, source_target_pairs={{3,2},{2,1},{1,0},{7,6},{6,5},{5,4},{11,10},{10,9},{9,8},{15,14},{... | collective-permute-start | bytes 1572872 | tf_op jit(solution)/shard_map/ppermute | solution.py:218
  556.2 27.0 %collective-permute-start.60 = (bf16[128,2048]{1,0:T(8,128)(2,1)}, bf16[128,2048]{1,0:T(8,128)(2,1)}, u32[]{:S(2)}, u32[]{:S(2)}) collective-permute-start(bf16[128,2048]{1,0:T(8,128)(2,1)} %collective-permute-done.56.refs_2_), channel_id=1, source_target_pairs={{2,3},{6,7},{10,11},{14,15},{18,19},{22,23},{26,27},{30,31}} | collective-permute-start | bytes 1572872 | tf_op jit(solution)/shard_map/ppermute | solution.py:218
  557.6 25.5 %collective-permute-start.61 = (bf16[128,2048]{1,0:T(8,128)(2,1)}, bf16[128,2048]{1,0:T(8,128)(2,1)}, u32[]{:S(2)}, u32[]{:S(2)}) collective-permute-start(bf16[128,2048]{1,0:T(8,128)(2,1)} %collective-permute-done.59.refs_5_), channel_id=1, source_target_pairs={{1,0},{5,4},{9,8},{13,12},{17,16},{21,20},{25,24},{29,28}} | collective-permute-start | bytes 1572872 | tf_op jit(solution)/shard_map/ppermute | solution.py:218
  646.1 101.7 %reduce-scatter.12.cloned.1.call-start = ((), (), s32[]{:S(2)}) async-start(), calls=%async_computation.11 | async-start | bytes 3538944 | tf_op jit(solution)/shard_map/reduce_scatter | solution.py:856
  (160 other events, 1757.3 us)
Sparse Core Ops, SparseCore 0:
  42.0 56.8 all-gather.3
  100.8 56.3 all-gather.5
  159.0 54.2 all-gather.7
  384.1 70.3 reduce-scatter.5
  458.4 71.5 reduce-scatter.7
  533.3 72.7 reduce-scatter.9
  646.3 39.4 reduce-scatter.13
  689.7 46.5 reduce-scatter.11

commit v6 on v5

--- a/solution.py
+++ b/solution.py
@@ -975,7 +975,11 @@
     slot([gather_n1, gains_one])
     slot([Both(gather_n1, sum_f1), gains_one])
     clock.expect(whole(first["input_grad"]))
-    clock.expect(first["output"])
+    output = whole(first["output"])
+    output = lax.optimization_barrier(
+        jnp.concatenate([output, jnp.zeros_like(output)], axis=0)
+    )
+    clock.expect(output)
     slot([Both(gather_n1, sum_f1), gains_one])
     second["input_grad"] = gather_n1.result()
     clock.expect(down_grad)
@@ -1007,7 +1011,7 @@
     gain_one_grad, gain_two_grad = gains_one.value
 
     return (
-        jnp.concatenate([whole(s["output"]) for s in state], axis=0),
+        lax.dynamic_update_slice_in_dim(output, whole(second["output"]), per_chunk, 0),
         input_grad,
         qkv_grad[:, :q_width],
         qkv_grad[:, q_width : q_width + k_width],

time: 794 us -> 808 us (1.018)
  local copies, waits for them, and re-layouts: 41.7 us -> 50.3 us
  transfers between devices with their start and end apart: 102 -> 102, of which waited for: 35 -> 36; matrix products, arithmetic and copies ran while one was open for 26% -> 26% of each run, Pallas kernels for 26% -> 26%
where the time goes in v6:
time: 808 us; the launch traced here: 797 us
  Pallas kernels  211 us (26%)
  starting transfers between devices  199 us (25%)
  waiting for transfers between devices  127 us (16%)
  other arithmetic  106 us (13%)
  matrix products  88.2 us (11%)
  local copies, waits for them, and re-layouts  50.3 us (6%)
  between operations  16.1 us (2%)
    ppermute x88, starting transfers between devices, slot(): moved = [lax.ppermute(g, s[1], s[2]) for g, s in zip(gated, flat)]  194 us
    ppermute x88, waiting for transfers between devices, slot(): moved = [lax.ppermute(g, s[1], s[2]) for g, s in zip(gated, flat)]  120 us
    dot_general x5, matrix products, dot_rows(): lax.dot_general(left_in, right_in, (((0,), (0,)), ((), ())), preferred_el...  50.6 us
    pallas_call x4, Pallas kernels, product_call(): pl.pallas_call(functools.partial(product_kernel, count, turned), grid=(wi...  49.2 us
    pallas_call x2, Pallas kernels, ffn_call(): pl.pallas_call(ffn_kernel, grid=(units // tile,), in_specs=[whole, rows_o...  40.2 us
    pallas_call x2, Pallas kernels, attend_back_call(): pl.pallas_call(functools.partial(attend_back_kernel, group), grid_spec=pl...  32.4 us
    select_n x12, other arithmetic, sends(): value = jnp.where(rank >= first, whole[0], part[0])  29.9 us
    pallas_call x8, Pallas kernels, place_call(): pl.pallas_call(functools.partial(place_kernel, count), grid_spec=pltpu.Pr...  25.6 us
  transfers between devices with their start and end apart: 102, of which 36 were waited for; matrix products, arithmetic and copies ran while one was open for 26% of the time, Pallas kernels for 26%

profile of v6, /device:TPU:0, one launch (start us, length us, event | category | flops | bytes accessed | tf_op | source)
XLA Modules:
  0.0 797.0 jit_solution(14623899386952361009)
XLA Ops:
  34.6 5.2 collective-permute-done.2
  49.6 6.5 spread.1
  80.6 11.4 %attend.2 = (bf16[2,256,512]{2,1,0:T(8,128)(2,1)}, f32[2,8,256]{2,1,0:T(8,128)}) custom-call(s32[5]{0:T(128)} %stack.34.place_ref, bf16[2,256,512]{2,1,0:T(8,128)(2,1)} %bitcast.349, bf16[2,256,256]{2,1,0:T(8,128)(2,1)} %bitcast.374, bf16[2,256,256]{2,1,0:T(8,128)(2,1)} %copy-done.68, bf16[2,256,256]{2,1,0:T(8,128)(2,1)} %copy-done.67, ...), custom_call_target="tpu_custom_call" | custom-call | flops 4294967296 | bytes 1572864 | tf_op jit(solution)/shard_map/attend/pallas_call | solution.py:520
  121.2 9.5 %collective-permute-done.10 = bf16[128,2048]{1,0:T(8,128)(2,1)S(1)} collective-permute-done((bf16[128,2048]{1,0:T(8,128)(2,1)}, bf16[128,2048]{1,0:T(8,128)(2,1)S(1)}, u32[]{:S(2)}, u32[]{:S(2)}) %collective-permute-start.10) | collective-permute-done | bytes 524320 | tf_op jit(solution)/shard_map/ppermute | solution.py:218
  133.1 5.6 collective-permute-start.14
  141.0 7.6 collective-permute-done.14
  159.6 11.4 %attend.3 = (bf16[2,256,512]{2,1,0:T(8,128)(2,1)}, f32[2,8,256]{2,1,0:T(8,128)}) custom-call(s32[5]{0:T(128)} %stack.34.place_ref, bf16[2,256,512]{2,1,0:T(8,128)(2,1)} %bitcast.347, bf16[2,256,256]{2,1,0:T(8,128)(2,1)} %bitcast.368, bf16[2,256,256]{2,1,0:T(8,128)(2,1)} %copy-done.65, bf16[2,256,256]{2,1,0:T(8,128)(2,1)} %copy-done.64, ...), custom_call_target="tpu_custom_call" | custom-call | flops 4294967296 | bytes 1572864 | tf_op jit(solution)/shard_map/attend/pallas_call | solution.py:520
  182.3 10.0 %turn_over.2.refs_2_ = bf16[2048,2048]{1,0:T(8,128)(2,1)} custom-call(bf16[2048,2048]{1,0:T(8,128)(2,1)} %all-gather.4.cloned.1.call-done.x_ref.g_ref), custom_call_target="tpu_custom_call" | custom-call | bytes 16777216 | tf_op jit(solution)/shard_map/turn_over/pallas_call | solution.py:425
  201.3 10.1 %turn_over.3.refs_3_ = bf16[2048,2048]{1,0:T(8,128)(2,1)} custom-call(bf16[2048,2048]{1,0:T(8,128)(2,1)} %all-gather.6.cloned.1.call-done.x_ref.u_ref), custom_call_target="tpu_custom_call" | custom-call | bytes 16777216 | tf_op jit(solution)/shard_map/turn_over/pallas_call | solution.py:425
  223.3 20.1 %ffn.2 = (bf16[512,2048]{1,0:T(8,128)(2,1)}, bf16[512,2048]{1,0:T(8,128)(2,1)}, bf16[512,2048]{1,0:T(8,128)(2,1)}) custom-call(bf16[512,2048]{1,0:T(8,128)(2,1)} %bitcast.335, bf16[1024,2048]{1,0:T(8,128)(2,1)} %bitcast.363, bf16[2048,2048]{1,0:T(8,128)(2,1)} %all-gather.4.cloned.1.call-done.x_ref.g_ref, ...), custom_call_target="tpu_custom_call" | custom-call | flops 12884901888 | bytes 31457280 | tf_op jit(solution)/shard_map/ffn/pallas_call | solution.py:368
  251.3 13.8 %product.4 = bf16[512,2048]{1,0:T(8,128)(2,1)} custom-call(bf16[512,2048]{1,0:T(8,128)(2,1)} %get-tuple-element.262.refs_0_, bf16[512,2048]{1,0:T(8,128)(2,1)} %get-tuple-element.289.refs_1_, bf16[2048,2048]{1,0:T(8,128)(2,1)} %turn_over.2.refs_2_, bf16[2048,2048]{1,0:T(8,128)(2,1)} %turn_over.3.refs_3_), custom_call_target="tpu_custom_call" | custom-call | flops 8589934592 | bytes 20971520 | tf_op jit(solution)/shard_map/product/pallas_call | solution.py:402
  273.7 10.6 %product.5 = bf16[512,2048]{1,0:T(8,128)(2,1)} custom-call(bf16[512,2048]{1,0:T(8,128)(2,1)} %get-tuple-element.254.refs_0_, bf16[2048,2048]{1,0:T(8,128)(2,1)} %all-gather.8.cloned.1.call-done.d_ref.refs_1_), custom_call_target="tpu_custom_call" | custom-call | flops 4294967296 | bytes 10485760 | tf_op jit(solution)/shard_map/product/pallas_call | solution.py:402
  311.9 20.1 %ffn.3 = (bf16[512,2048]{1,0:T(8,128)(2,1)}, bf16[512,2048]{1,0:T(8,128)(2,1)}, bf16[512,2048]{1,0:T(8,128)(2,1)}) custom-call(bf16[512,2048]{1,0:T(8,128)(2,1)} %bitcast.340, bf16[1024,2048]{1,0:T(8,128)(2,1)} %bitcast.364, bf16[2048,2048]{1,0:T(8,128)(2,1)} %all-gather.4.cloned.1.call-done.x_ref.g_ref, ...), custom_call_target="tpu_custom_call" | custom-call | flops 12884901888 | bytes 31457280 | tf_op jit(solution)/shard_map/ffn/pallas_call | solution.py:368
  342.9 13.9 %product.6 = bf16[512,2048]{1,0:T(8,128)(2,1)} custom-call(bf16[512,2048]{1,0:T(8,128)(2,1)} %get-tuple-element.263.refs_0_, bf16[512,2048]{1,0:T(8,128)(2,1)} %get-tuple-element.290.refs_1_, bf16[2048,2048]{1,0:T(8,128)(2,1)} %turn_over.2.refs_2_, bf16[2048,2048]{1,0:T(8,128)(2,1)} %turn_over.3.refs_3_), custom_call_target="tpu_custom_call" | custom-call | flops 8589934592 | bytes 20971520 | tf_op jit(solution)/shard_map/product/pallas_call | solution.py:402
  365.4 13.7 %convolution_convert_fusion.2 = bf16[2048,2048]{1,0:T(8,128)(2,1)} fusion(bf16[1024,2048]{1,0:T(8,128)(2,1)} %bitcast.366, bf16[512,2048]{1,0:T(8,128)(2,1)S(1)} %copy-done.76, bf16[512,2048]{1,0:T(8,128)(2,1)} %get-tuple-element.254.refs_0_), kind=kOutput, calls=%fused_computation.2 | convolution fusion | flops 8602517504 | bytes 16777216 | tf_op jit(solution)/shard_map/dot_general | solution.py:36
  388.2 5.4 collective-permute-start.39
  395.0 15.1 %convolution_convert_fusion.1 = bf16[2048,2048]{1,0:T(8,128)(2,1)} fusion(bf16[512,2048]{1,0:T(8,128)(2,1)} %bitcast.341, bf16[512,2048]{1,0:T(8,128)(2,1)} %bitcast.336, bf16[512,2048]{1,0:T(8,128)(2,1)} %get-tuple-element.263.refs_0_, bf16[512,2048]{1,0:T(8,128)(2,1)} %get-tuple-element.262.refs_0_), kind=kOutput, calls=%fused_computation.1 | convolution fusion | flops 8610906112 | bytes 16777216 | tf_op jit(solution)/shard_map/dot_general | solution.py:36
  433.6 16.0 %attend_back.2 = (bf16[2,256,512]{2,1,0:T(8,128)(2,1)}, bf16[2,256,256]{2,1,0:T(8,128)(2,1)}, bf16[2,256,256]{2,1,0:T(8,128)(2,1)}, bf16[2,256,256]{2,1,0:T(8,128)(2,1)}, bf16[2,256,256]{2,1,0:T(8,128)(2,1)}) custom-call(s32[5]{0:T(128)} %stack.34.place_ref, bf16[2,256,512]{2,1,0:T(8,128)(2,1)} %bitcast.350, bf16[2,256,256]{2,1,0:T(8,128)(2,1)} %bitcast.375, ...), custom_call_target="tpu_custom_call" | custom-call | flops 10737418240 | bytes 3145728 | tf_op jit(solution)/shard_map/attend_back/pallas_call | solution.py:640
  459.7 5.2 collective-permute-start.47
  472.3 5.3 collective-permute-start.45
  501.0 5.3 collective-permute-start.52
  507.6 11.5 %convolution_convert_fusion = bf16[2048,2048]{1,0:T(8,128)(2,1)} fusion(bf16[512,2048]{1,0:T(8,128)(2,1)S(1)} %bitcast.342, bf16[512,2048]{1,0:T(8,128)(2,1)S(1)} %bitcast.337, bf16[512,2048]{1,0:T(8,128)(2,1)S(1)} %copy-done.78, bf16[512,2048]{1,0:T(8,128)(2,1)S(1)} %copy-done.77), kind=kOutput, calls=%fused_computation | convolution fusion | flops 8610906112 | bytes 16777216 | tf_op jit(solution)/shard_map/dot_general | solution.py:36
  536.4 9.0 %collective-permute-done.58.refs_6_ = bf16[128,2048]{1,0:T(8,128)(2,1)} collective-permute-done((bf16[128,2048]{1,0:T(8,128)(2,1)}, bf16[128,2048]{1,0:T(8,128)(2,1)}, u32[]{:S(2)}, u32[]{:S(2)}) %collective-permute-start.58) | collective-permute-done | bytes 524320 | tf_op jit(solution)/shard_map/ppermute | solution.py:218
  563.5 16.4 %attend_back.3 = (bf16[2,256,512]{2,1,0:T(8,128)(2,1)}, bf16[2,256,256]{2,1,0:T(8,128)(2,1)}, bf16[2,256,256]{2,1,0:T(8,128)(2,1)}, bf16[2,256,256]{2,1,0:T(8,128)(2,1)}, bf16[2,256,256]{2,1,0:T(8,128)(2,1)}) custom-call(s32[5]{0:T(128)} %stack.34.place_ref, bf16[2,256,512]{2,1,0:T(8,128)(2,1)} %bitcast.348, bf16[2,256,256]{2,1,0:T(8,128)(2,1)} %bitcast.369, ...), custom_call_target="tpu_custom_call" | custom-call | flops 10737418240 | bytes 3145728 | tf_op jit(solution)/shard_map/attend_back/pallas_call | solution.py:640
  587.9 6.0 collective-permute-start.64
  618.1 5.1 fusion.23
  637.3 5.3 fusion.26
  655.4 10.9 %product.7 = bf16[512,2048]{1,0:T(8,128)(2,1)} custom-call(bf16[512,2048]{1,0:T(8,128)(2,1)} %get-tuple-element.324.refs_0_, bf16[2048,2048]{1,0:T(8,128)(2,1)} %all-gather.8.cloned.1.call-done.d_ref.refs_1_), custom_call_target="tpu_custom_call" | custom-call | flops 4294967296 | bytes 10485760 | tf_op jit(solution)/shard_map/product/pallas_call | solution.py:402
  671.2 5.4 collective-permute-start.75
  680.6 8.0 collective-permute-done.77
  749.7 5.5 maximum_convert_fusion
  774.0 8.8 %collective-permute-done.93.refs_6_ = bf16[128,2048]{1,0:T(8,128)(2,1)S(1)} collective-permute-done((bf16[128,2048]{1,0:T(8,128)(2,1)}, bf16[128,2048]{1,0:T(8,128)(2,1)S(1)}, u32[]{:S(2)}, u32[]{:S(2)}) %collective-permute-start.93) | collective-permute-done | bytes 524320 | tf_op jit(solution)/shard_map/ppermute | solution.py:218
  (495 shorter events, 467.4 us)
Async XLA Ops:
  7.2 169.3 %all-gather.4.cloned.1.call-start = ((), (), s32[]{:S(2)}) async-start(), calls=%async_computation.5 | async-start | bytes 9437184 | tf_op jit(solution)/shard_map/all_gather | solution.py:763
  41.8 155.4 %all-gather.6.cloned.1.call-start = ((), (), s32[]{:S(2)}) async-start(), calls=%async_computation.6 | async-start | bytes 9437184 | tf_op jit(solution)/shard_map/all_gather | solution.py:763
  42.6 180.7 %all-gather.8.cloned.1.call-start = ((), (), s32[]{:S(2)}) async-start(), calls=%async_computation.7 | async-start | bytes 9437184 | tf_op jit(solution)/shard_map/all_gather | solution.py:763
  43.3 682.1 %reduce-scatter.6.cloned.1.call-start = ((), (), s32[]{:S(2)}) async-start(), calls=%async_computation.8 | async-start | bytes 9437184 | tf_op jit(solution)/shard_map/reduce_scatter | solution.py:856
  218.8 24.6 %collective-permute-start.23 = (bf16[128,2048]{1,0:T(8,128)(2,1)S(1)}, bf16[128,2048]{1,0:T(8,128)(2,1)S(1)}, u32[]{:S(2)}, u32[]{:S(2)}) collective-permute-start(bf16[128,2048]{1,0:T(8,128)(2,1)S(1)} %get-tuple-element.226), channel_id=1, source_target_pairs={{0,1},{1,2},{2,3},{4,5},{5,6},{6,7},{8,9},{9,10},{10,11},{12,13},{... | collective-permute-start | bytes 1572872 | tf_op jit(solution)/shard_map/ppermute | solution.py:218
  222.0 21.4 %collective-permute-start.24 = (bf16[128,2048]{1,0:T(8,128)(2,1)S(1)}, bf16[128,2048]{1,0:T(8,128)(2,1)S(1)}, u32[]{:S(2)}, u32[]{:S(2)}) collective-permute-start(bf16[128,2048]{1,0:T(8,128)(2,1)S(1)} %get-tuple-element.227), channel_id=1, source_target_pairs={{3,2},{2,1},{1,0},{7,6},{6,5},{5,4},{11,10},{10,9},{9,8},{15,14},{... | collective-permute-start | bytes 1572872 | tf_op jit(solution)/shard_map/ppermute | solution.py:218
  308.3 23.8 %collective-permute-start.31 = (bf16[128,2048]{1,0:T(8,128)(2,1)}, bf16[128,2048]{1,0:T(8,128)(2,1)S(1)}, u32[]{:S(2)}, u32[]{:S(2)}) collective-permute-start(bf16[128,2048]{1,0:T(8,128)(2,1)} %get-tuple-element.241), channel_id=1, source_target_pairs={{0,1},{1,2},{2,3},{4,5},{5,6},{6,7},{8,9},{9,10},{10,11},{12,13},{... | collective-permute-start | bytes 1572872 | tf_op jit(solution)/shard_map/ppermute | solution.py:218
  310.6 21.4 %collective-permute-start.32 = (bf16[128,2048]{1,0:T(8,128)(2,1)}, bf16[128,2048]{1,0:T(8,128)(2,1)S(1)}, u32[]{:S(2)}, u32[]{:S(2)}) collective-permute-start(bf16[128,2048]{1,0:T(8,128)(2,1)} %get-tuple-element.242), channel_id=1, source_target_pairs={{3,2},{2,1},{1,0},{7,6},{6,5},{5,4},{11,10},{10,9},{9,8},{15,14},{... | collective-permute-start | bytes 1572872 | tf_op jit(solution)/shard_map/ppermute | solution.py:218
  336.6 20.2 %collective-permute-start.33 = (bf16[128,2048]{1,0:T(8,128)(2,1)S(1)}, bf16[128,2048]{1,0:T(8,128)(2,1)S(1)}, u32[]{:S(2)}, u32[]{:S(2)}) collective-permute-start(bf16[128,2048]{1,0:T(8,128)(2,1)S(1)} %get-tuple-element.248.refs_0_), channel_id=1, source_target_pairs={{0,1},{1,2},{2,3},{4,5},{5,6},{6,7},{8,9},{9,10},{10,11},{12,13},{... | collective-permute-start | bytes 1572872 | tf_op jit(solution)/shard_map/ppermute | solution.py:218
  382.3 358.7 %reduce-scatter.8.cloned.1.call-start = ((), (), s32[]{:S(2)}) async-start(), calls=%async_computation.9 | async-start | bytes 9437184 | tf_op jit(solution)/shard_map/reduce_scatter | solution.py:856
  382.4 27.8 %collective-permute-start.37 = (bf16[128,2048]{1,0:T(8,128)(2,1)}, bf16[128,2048]{1,0:T(8,128)(2,1)S(1)}, u32[]{:S(2)}, u32[]{:S(2)}) collective-permute-start(bf16[128,2048]{1,0:T(8,128)(2,1)} %get-tuple-element.256), channel_id=1, source_target_pairs={{0,1},{1,2},{2,3},{4,5},{5,6},{6,7},{8,9},{9,10},{10,11},{12,13},{... | collective-permute-start | bytes 1572872 | tf_op jit(solution)/shard_map/ppermute | solution.py:218
  386.9 23.2 %collective-permute-start.38 = (bf16[128,2048]{1,0:T(8,128)(2,1)}, bf16[128,2048]{1,0:T(8,128)(2,1)S(1)}, u32[]{:S(2)}, u32[]{:S(2)}) collective-permute-start(bf16[128,2048]{1,0:T(8,128)(2,1)} %get-tuple-element.257), channel_id=1, source_target_pairs={{1,0},{2,1},{3,2},{5,4},{6,5},{7,6},{9,8},{10,9},{11,10},{13,12},{... | collective-permute-start | bytes 1572872 | tf_op jit(solution)/shard_map/ppermute | solution.py:218
  388.2 29.7 %collective-permute-start.39 = (bf16[128,2048]{1,0:T(8,128)(2,1)}, bf16[128,2048]{1,0:T(8,128)(2,1)}, u32[]{:S(2)}, u32[]{:S(2)}) collective-permute-start(bf16[128,2048]{1,0:T(8,128)(2,1)} %get-tuple-element.258), channel_id=1, source_target_pairs={{0,1},{4,5},{8,9},{12,13},{16,17},{20,21},{24,25},{28,29}} | collective-permute-start | bytes 1572872 | tf_op jit(solution)/shard_map/ppermute | solution.py:218
  393.6 24.3 %collective-permute-start.40 = (bf16[128,2048]{1,0:T(8,128)(2,1)}, bf16[128,2048]{1,0:T(8,128)(2,1)}, u32[]{:S(2)}, u32[]{:S(2)}) collective-permute-start(bf16[128,2048]{1,0:T(8,128)(2,1)} %get-tuple-element.259), channel_id=1, source_target_pairs={{3,2},{7,6},{11,10},{15,14},{19,18},{23,22},{27,26},{31,30}} | collective-permute-start | bytes 1572872 | tf_op jit(solution)/shard_map/ppermute | solution.py:218
  420.6 335.8 %reduce-scatter.10.cloned.1.call-start = ((), (), s32[]{:S(2)}) async-start(), calls=%async_computation.10 | async-start | bytes 9437184 | tf_op jit(solution)/shard_map/reduce_scatter | solution.py:856
  422.5 28.9 %collective-permute-start.43 = (bf16[128,2048]{1,0:T(8,128)(2,1)}, bf16[128,2048]{1,0:T(8,128)(2,1)}, u32[]{:S(2)}, u32[]{:S(2)}) collective-permute-start(bf16[128,2048]{1,0:T(8,128)(2,1)} %get-tuple-element.266), channel_id=1, source_target_pairs={{0,1},{1,2},{4,5},{5,6},{8,9},{9,10},{12,13},{13,14},{16,17},{17,1... | collective-permute-start | bytes 1572872 | tf_op jit(solution)/shard_map/ppermute | solution.py:218
  424.6 26.8 %collective-permute-start.44 = (bf16[128,2048]{1,0:T(8,128)(2,1)}, bf16[128,2048]{1,0:T(8,128)(2,1)}, u32[]{:S(2)}, u32[]{:S(2)}) collective-permute-start(bf16[128,2048]{1,0:T(8,128)(2,1)} %get-tuple-element.267), channel_id=1, source_target_pairs={{3,2},{2,1},{7,6},{6,5},{11,10},{10,9},{15,14},{14,13},{19,18},{18... | collective-permute-start | bytes 1572872 | tf_op jit(solution)/shard_map/ppermute | solution.py:218
  426.1 23.6 %collective-permute-start.41 = (bf16[128,2048]{1,0:T(8,128)(2,1)}, bf16[128,2048]{1,0:T(8,128)(2,1)S(1)}, u32[]{:S(2)}, u32[]{:S(2)}) collective-permute-start(bf16[128,2048]{1,0:T(8,128)(2,1)} %get-tuple-element.264), channel_id=1, source_target_pairs={{0,1},{1,2},{2,3},{4,5},{5,6},{6,7},{8,9},{9,10},{10,11},{12,13},{... | collective-permute-start | bytes 1572872 | tf_op jit(solution)/shard_map/ppermute | solution.py:218
  427.9 21.8 %collective-permute-start.42 = (bf16[128,2048]{1,0:T(8,128)(2,1)}, bf16[128,2048]{1,0:T(8,128)(2,1)S(1)}, u32[]{:S(2)}, u32[]{:S(2)}) collective-permute-start(bf16[128,2048]{1,0:T(8,128)(2,1)} %get-tuple-element.265), channel_id=1, source_target_pairs={{3,2},{2,1},{1,0},{7,6},{6,5},{5,4},{11,10},{10,9},{9,8},{15,14},{... | collective-permute-start | bytes 1572872 | tf_op jit(solution)/shard_map/ppermute | solution.py:218
  457.1 20.5 %collective-permute-start.49 = (bf16[2,256,256]{2,1,0:T(8,128)(2,1)S(1)}, bf16[2,256,256]{2,1,0:T(8,128)(2,1)S(1)}, u32[]{:S(2)}, u32[]{:S(2)}) collective-permute-start(bf16[2,256,256]{2,1,0:T(8,128)(2,1)S(1)} %copy-done.70), channel_id=1, source_target_pairs={{0,4},{4,0},{1,5},{5,1},{2,6},{6,2},{3,7},{7,3},{8,12},{12,8},{9,1... | collective-permute-start | bytes 786440 | tf_op jit(solution)/shard_map/ppermute | solution.py:841
  458.7 20.2 %collective-permute-start.51 = (bf16[2,256,256]{2,1,0:T(8,128)(2,1)S(1)}, bf16[2,256,256]{2,1,0:T(8,128)(2,1)}, u32[]{:S(2)}, u32[]{:S(2)}) collective-permute-start(bf16[2,256,256]{2,1,0:T(8,128)(2,1)S(1)} %add_convert_fusion.1), channel_id=1, source_target_pairs={{0,8},{8,0},{1,9},{9,1},{2,10},{10,2},{3,11},{11,3},{4,12},{12,4},... | collective-permute-start | bytes 786440 | tf_op jit(solution)/shard_map/ppermute | solution.py:843
  459.7 26.2 %collective-permute-start.47 = (bf16[128,2048]{1,0:T(8,128)(2,1)S(1)}, bf16[128,2048]{1,0:T(8,128)(2,1)S(1)}, u32[]{:S(2)}, u32[]{:S(2)}) collective-permute-start(bf16[128,2048]{1,0:T(8,128)(2,1)S(1)} %get-tuple-element.277.refs_0_), channel_id=1, source_target_pairs={{0,1},{1,2},{2,3},{4,5},{5,6},{6,7},{8,9},{9,10},{10,11},{12,13},{... | collective-permute-start | bytes 1572872 | tf_op jit(solution)/shard_map/ppermute | solution.py:218
  464.9 21.0 %collective-permute-start.48 = (bf16[128,2048]{1,0:T(8,128)(2,1)S(1)}, bf16[128,2048]{1,0:T(8,128)(2,1)}, u32[]{:S(2)}, u32[]{:S(2)}) collective-permute-start(bf16[128,2048]{1,0:T(8,128)(2,1)S(1)} %get-tuple-element.277.refs_0_), channel_id=1, source_target_pairs={{3,2},{2,1},{1,0},{7,6},{6,5},{5,4},{11,10},{10,9},{9,8},{15,14},{... | collective-permute-start | bytes 1572872 | tf_op jit(solution)/shard_map/ppermute | solution.py:218
  495.4 23.7 %collective-permute-start.53 = (bf16[128,2048]{1,0:T(8,128)(2,1)}, bf16[128,2048]{1,0:T(8,128)(2,1)}, u32[]{:S(2)}, u32[]{:S(2)}) collective-permute-start(bf16[128,2048]{1,0:T(8,128)(2,1)} %get-tuple-element.284), channel_id=1, source_target_pairs={{0,1},{1,2},{2,3},{4,5},{5,6},{6,7},{8,9},{9,10},{10,11},{12,13},{... | collective-permute-start | bytes 1572872 | tf_op jit(solution)/shard_map/ppermute | solution.py:218
  501.0 21.3 %collective-permute-start.52 = (bf16[128,2048]{1,0:T(8,128)(2,1)}, bf16[128,2048]{1,0:T(8,128)(2,1)}, u32[]{:S(2)}, u32[]{:S(2)}) collective-permute-start(bf16[128,2048]{1,0:T(8,128)(2,1)} %fusion.96.refs_0_), channel_id=1, source_target_pairs={{0,1},{1,2},{2,3},{4,5},{5,6},{6,7},{8,9},{9,10},{10,11},{12,13},{... | collective-permute-start | bytes 1572872 | tf_op jit(solution)/shard_map/ppermute | solution.py:218
  524.5 234.7 %reduce-scatter.14.cloned.1.call-start = ((), (), s32[]{:S(2)}) async-start(), calls=%async_computation.12 | async-start | bytes 2359296 | tf_op jit(solution)/shard_map/reduce_scatter | solution.py:856
  531.1 20.8 %collective-permute-start.56 = (bf16[128,2048]{1,0:T(8,128)(2,1)}, bf16[128,2048]{1,0:T(8,128)(2,1)}, u32[]{:S(2)}, u32[]{:S(2)}) collective-permute-start(bf16[128,2048]{1,0:T(8,128)(2,1)} %collective-permute-done.52.refs_1_), channel_id=1, source_target_pairs={{1,2},{2,3},{5,6},{6,7},{9,10},{10,11},{13,14},{14,15},{17,18},{18... | collective-permute-start | bytes 1572872 | tf_op jit(solution)/shard_map/ppermute | solution.py:218
  552.6 27.3 %collective-permute-start.62 = (bf16[128,2048]{1,0:T(8,128)(2,1)}, bf16[128,2048]{1,0:T(8,128)(2,1)}, u32[]{:S(2)}, u32[]{:S(2)}) collective-permute-start(bf16[128,2048]{1,0:T(8,128)(2,1)} %get-tuple-element.297), channel_id=1, source_target_pairs={{0,1},{1,2},{2,3},{4,5},{5,6},{6,7},{8,9},{9,10},{10,11},{12,13},{... | collective-permute-start | bytes 1572872 | tf_op jit(solution)/shard_map/ppermute | solution.py:218
  555.3 24.5 %collective-permute-start.63 = (bf16[128,2048]{1,0:T(8,128)(2,1)}, bf16[128,2048]{1,0:T(8,128)(2,1)}, u32[]{:S(2)}, u32[]{:S(2)}) collective-permute-start(bf16[128,2048]{1,0:T(8,128)(2,1)} %get-tuple-element.298), channel_id=1, source_target_pairs={{3,2},{2,1},{1,0},{7,6},{6,5},{5,4},{11,10},{10,9},{9,8},{15,14},{... | collective-permute-start | bytes 1572872 | tf_op jit(solution)/shard_map/ppermute | solution.py:218
  556.6 28.2 %collective-permute-start.60 = (bf16[128,2048]{1,0:T(8,128)(2,1)}, bf16[128,2048]{1,0:T(8,128)(2,1)}, u32[]{:S(2)}, u32[]{:S(2)}) collective-permute-start(bf16[128,2048]{1,0:T(8,128)(2,1)} %collective-permute-done.56.refs_2_), channel_id=1, source_target_pairs={{2,3},{6,7},{10,11},{14,15},{18,19},{22,23},{26,27},{30,31}} | collective-permute-start | bytes 1572872 | tf_op jit(solution)/shard_map/ppermute | solution.py:218
  558.1 26.7 %collective-permute-start.61 = (bf16[128,2048]{1,0:T(8,128)(2,1)}, bf16[128,2048]{1,0:T(8,128)(2,1)}, u32[]{:S(2)}, u32[]{:S(2)}) collective-permute-start(bf16[128,2048]{1,0:T(8,128)(2,1)} %collective-permute-done.59.refs_5_), channel_id=1, source_target_pairs={{1,0},{5,4},{9,8},{13,12},{17,16},{21,20},{25,24},{29,28}} | collective-permute-start | bytes 1572872 | tf_op jit(solution)/shard_map/ppermute | solution.py:218
  651.8 109.2 %reduce-scatter.12.cloned.1.call-start = ((), (), s32[]{:S(2)}) async-start(), calls=%async_computation.11 | async-start | bytes 3538944 | tf_op jit(solution)/shard_map/reduce_scatter | solution.py:856
  (149 other events, 1655.7 us)
Sparse Core Ops, SparseCore 0:
  42.0 57.2 all-gather.3
  101.1 56.0 all-gather.5
  159.1 54.2 all-gather.7
  382.4 71.6 reduce-scatter.5
  458.0 71.4 reduce-scatter.7
  532.9 74.7 reduce-scatter.9
  651.9 40.4 reduce-scatter.13
  695.9 46.2 reduce-scatter.11
